TPU v7x, 32 devices: a whole 2x2x4 slice. The times are simulated.
32 devices in a mesh: dp: 16 (over z, y, core), seq: 2 (over x).
Axes of the slice: x: 2, y: 2, z: 4, core: 2. Of those that a mesh axis runs over, the one named last changes fastest.
Arguments:
- tokens: bfloat16 [32, 320, 1024], P('dp', 'seq'), may hold values from -6 to 6
- keep: int32 [32, 320], P('dp', 'seq'), may hold values from 0 to 1, as said below
- norm_gain: bfloat16 [2, 2, 1024], P(None, None, ('dp', 'seq')), may hold values from 0.5 to 1.5
- norm_bias: bfloat16 [2, 2, 1024], P(None, None, ('dp', 'seq')), may hold values from -2 to 2
- qkv_weight: bfloat16 [2, 1024, 3072], P(None, ('dp', 'seq')), may hold values from -0.1875 to 0.1875
- qv_bias: bfloat16 [2, 2, 1024], P(None, None, ('dp', 'seq')), may hold values from -2 to 2
- out_weight: bfloat16 [2, 1024, 1024], P(None, ('dp', 'seq')), may hold values from -0.75 to 0.75
- out_bias: bfloat16 [2, 1024], P(None, ('dp', 'seq')), may hold values from -2 to 2
- up_weight: bfloat16 [2, 1024, 4096], P(None, ('dp', 'seq')), may hold values from -0.1875 to 0.1875
- up_bias: bfloat16 [2, 4096], P(None, ('dp', 'seq')), may hold values from -2 to 2
- down_weight: bfloat16 [2, 4096, 1024], P(None, ('dp', 'seq')), may hold values from -0.09375 to 0.09375
- down_bias: bfloat16 [2, 1024], P(None, ('dp', 'seq')), may hold values from -2 to 2
- cotangent: bfloat16 [32, 320, 1024], P('dp', 'seq'), may hold values from -6 to 6
Outputs:
- output: bfloat16 [32, 320, 1024], P('dp', 'seq')
- input_grad: float32 [32, 320, 1024], P('dp', 'seq')
- grad_norm_gain: float32 [2, 2, 1024], P(None, None, ('dp', 'seq'))
- grad_norm_bias: float32 [2, 2, 1024], P(None, None, ('dp', 'seq'))
- grad_qkv_weight: float32 [2, 1024, 3072], P(None, ('dp', 'seq'))
- grad_qv_bias: float32 [2, 2, 1024], P(None, None, ('dp', 'seq'))
- grad_out_weight: float32 [2, 1024, 1024], P(None, ('dp', 'seq'))
- grad_out_bias: float32 [2, 1024], P(None, ('dp', 'seq'))
- grad_up_weight: float32 [2, 1024, 4096], P(None, ('dp', 'seq'))
- grad_up_bias: float32 [2, 4096], P(None, ('dp', 'seq'))
- grad_down_weight: float32 [2, 4096, 1024], P(None, ('dp', 'seq'))
- grad_down_bias: float32 [2, 1024], P(None, ('dp', 'seq'))
Inputs may be any that keep to these rules, and one draw needn't show every extreme that they name: `keep`: 1 marks a kept token; the first 64 tokens of every image take part whatever their entry; each image has its own rate of kept patches.
All inputs are finite; a program needn't handle non-finite values.
Results may differ from a plain program's by a relative error of at most 0.014.
Values may be sent and summed in bfloat16 or wider, within the bound.
No kernel may reach another device: no remote copies, remote signals or barrier semaphores. Data moves between devices by JAX's collectives and lax.ppermute only.
A program may use at most 384 MiB of HBM per device.

v0:
```python
import jax
import jax.numpy as jnp
from jax import lax
from jax.sharding import PartitionSpec as P

HEAD = 64
BUFFER = 64
LAYERS = 2
MICRO = 2


masked_score = -1e30


def norm_rows(x, gain_vec, shift_vec):
    row_mean = jnp.mean(x, axis=-1, keepdims=True)
    centered = x - row_mean
    variance = jnp.mean(centered * centered, axis=-1, keepdims=True)
    return centered * lax.rsqrt(variance + 1e-06) * gain_vec + shift_vec


def gelu_exact(v):
    return jax.nn.gelu(v, approximate=False)


def layer_pieces(shards, layer_number):
    return (
        shards[0][layer_number].T,
        shards[1][layer_number].T,
        shards[2][layer_number],
        shards[3][layer_number].T,
        shards[4][layer_number],
        shards[5][layer_number],
        shards[6][layer_number],
        shards[7][layer_number],
        shards[8][layer_number],
        shards[9][layer_number],
    )


def restore_pairs(pieces):
    return (
        pieces[0].T,
        pieces[1].T,
        pieces[2],
        pieces[3].T,
        pieces[4],
        pieces[5],
        pieces[6],
        pieces[7],
        pieces[8],
        pieces[9],
    )


def gather_forward(shards, layer_number):
    pieces = layer_pieces(shards, layer_number)
    return restore_pairs(
        (
            lax.all_gather(pieces[0], ("dp", "seq"), axis=0, tiled=True),
            lax.all_gather(pieces[1], ("dp", "seq"), axis=0, tiled=True),
            lax.all_gather(pieces[2], ("dp", "seq"), axis=0, tiled=True),
            lax.all_gather(pieces[3], ("dp", "seq"), axis=0, tiled=True),
            lax.all_gather(pieces[4], ("dp", "seq"), axis=0, tiled=True),
            lax.all_gather(pieces[5], ("dp", "seq"), axis=0, tiled=True),
            lax.all_gather(pieces[6], ("dp", "seq"), axis=0, tiled=True),
            lax.all_gather(pieces[7], ("dp", "seq"), axis=0, tiled=True),
            lax.all_gather(pieces[8], ("dp", "seq"), axis=0, tiled=True),
            lax.all_gather(pieces[9], ("dp", "seq"), axis=0, tiled=True),
        )
    )


def gather_backward(shards, layer_number):
    pieces = layer_pieces(shards, layer_number)
    return restore_pairs(
        (
            lax.all_gather(pieces[0], ("dp", "seq"), axis=0, tiled=True),
            lax.all_gather(pieces[1], ("dp", "seq"), axis=0, tiled=True),
            lax.all_gather(pieces[2], ("dp", "seq"), axis=0, tiled=True),
            lax.all_gather(pieces[3], ("dp", "seq"), axis=0, tiled=True),
            lax.all_gather(pieces[4], ("dp", "seq"), axis=0, tiled=True),
            lax.all_gather(pieces[5], ("dp", "seq"), axis=0, tiled=True),
            lax.all_gather(pieces[6], ("dp", "seq"), axis=0, tiled=True),
            lax.all_gather(pieces[7], ("dp", "seq"), axis=0, tiled=True),
            lax.all_gather(pieces[8], ("dp", "seq"), axis=0, tiled=True),
            lax.all_gather(pieces[9], ("dp", "seq"), axis=0, tiled=True),
        )
    )


def reduce_all(sums):
    turned = (
        jnp.swapaxes(sums[0], 1, 2),
        jnp.swapaxes(sums[1], 1, 2),
        sums[2],
        jnp.swapaxes(sums[3], 1, 2),
        sums[4],
        sums[5],
        sums[6],
        sums[7],
        sums[8],
        sums[9],
    )
    result = (
        lax.psum_scatter(turned[0], ("dp", "seq"), scatter_dimension=1, tiled=True),
        lax.psum_scatter(turned[1], ("dp", "seq"), scatter_dimension=1, tiled=True),
        lax.psum_scatter(turned[2], ("dp", "seq"), scatter_dimension=1, tiled=True),
        lax.psum_scatter(turned[3], ("dp", "seq"), scatter_dimension=1, tiled=True),
        lax.psum_scatter(turned[4], ("dp", "seq"), scatter_dimension=1, tiled=True),
        lax.psum_scatter(turned[5], ("dp", "seq"), scatter_dimension=1, tiled=True),
        lax.psum_scatter(turned[6], ("dp", "seq"), scatter_dimension=1, tiled=True),
        lax.psum_scatter(turned[7], ("dp", "seq"), scatter_dimension=1, tiled=True),
        lax.psum_scatter(turned[8], ("dp", "seq"), scatter_dimension=1, tiled=True),
        lax.psum_scatter(turned[9], ("dp", "seq"), scatter_dimension=1, tiled=True),
    )
    return (
        jnp.swapaxes(result[0], 1, 2),
        jnp.swapaxes(result[1], 1, 2),
        result[2],
        jnp.swapaxes(result[3], 1, 2),
        result[4],
        result[5],
        result[6],
        result[7],
        result[8],
        result[9],
    )


def attention_scores(query_h, key_h, key_flags, attention_score_scale):
    scores = (
        jnp.einsum("nqhd,nkhd->nhqk", query_h, key_h, preferred_element_type=jnp.float32)
        * attention_score_scale
    )
    return jnp.where(key_flags[:, None, None, :] > 0, scores, masked_score)


def layer_forward(x, flag_send, layer_weight_list, attention_score_scale):
    gain_pair, shift_pair, w_qkv, qv_shift, w_out, out_shift, w_up, up_shift, w_down, down_shift = (
        layer_weight_list
    )
    n_images, local_len, model_dim = x.shape
    n_heads = model_dim // HEAD
    x_rows = x.reshape(n_images * local_len, model_dim)
    gains = gain_pair.astype(jnp.float32)
    shifts = shift_pair.astype(jnp.float32)
    normed = norm_rows(x_rows, gains[0], shifts[0]).astype(jnp.bfloat16)
    qkv_all = jnp.dot(normed, w_qkv, preferred_element_type=jnp.float32)
    query_bf = (qkv_all[:, :model_dim] + qv_shift[0].astype(jnp.float32)).astype(jnp.bfloat16)
    key_bf = qkv_all[:, model_dim : 2 * model_dim].astype(jnp.bfloat16)
    value_bf = (qkv_all[:, 2 * model_dim :] + qv_shift[1].astype(jnp.float32)).astype(jnp.bfloat16)
    device_local_shape = (n_images, local_len, model_dim)
    key_all, value_all, key_flags = (
        lax.all_gather(key_bf.reshape(device_local_shape), "seq", axis=1, tiled=True),
        lax.all_gather(value_bf.reshape(device_local_shape), "seq", axis=1, tiled=True),
        lax.all_gather(flag_send, "seq", axis=1, tiled=True),
    )
    query_h = query_bf.reshape(n_images, local_len, n_heads, HEAD)
    key_h = key_all.reshape(n_images, -1, n_heads, HEAD)
    value_h = value_all.reshape(n_images, -1, n_heads, HEAD)
    scores = attention_scores(query_h, key_h, key_flags, attention_score_scale)
    row_max = jnp.max(scores, axis=-1, keepdims=True)
    row_sum = jnp.sum(jnp.exp(scores - row_max), axis=-1, keepdims=True)
    log_total = row_max + jnp.log(row_sum)
    attn_probs = jnp.exp(scores - log_total).astype(jnp.bfloat16)
    attended = jnp.einsum(
        "nhqk,nkhd->nqhd", attn_probs, value_h, preferred_element_type=jnp.float32
    )
    attended = attended.reshape(n_images * local_len, model_dim).astype(jnp.bfloat16)
    resid_mid = (
        x_rows
        + jnp.dot(attended, w_out, preferred_element_type=jnp.float32)
        + out_shift.astype(jnp.float32)
    )
    normed_two = norm_rows(resid_mid, gains[1], shifts[1]).astype(jnp.bfloat16)
    up_pre = jnp.dot(normed_two, w_up, preferred_element_type=jnp.float32) + up_shift.astype(
        jnp.float32
    )
    hidden = gelu_exact(up_pre).astype(jnp.bfloat16)
    result = (
        resid_mid
        + jnp.dot(hidden, w_down, preferred_element_type=jnp.float32)
        + down_shift.astype(jnp.float32)
    )
    saved_activation = (
        x_rows,
        normed,
        query_h,
        key_h,
        value_h,
        key_flags,
        log_total,
        attended,
        resid_mid,
        normed_two,
        up_pre,
        hidden,
    )
    return (result.reshape(device_local_shape), saved_activation)


def layer_backward(gradient_token_rows, saved_activation, layer_weight_list, attention_score_scale):
    (
        x_rows,
        normed,
        query_h,
        key_h,
        value_h,
        key_flags,
        log_total,
        attended,
        resid_mid,
        normed_two,
        up_pre,
        hidden,
    ) = saved_activation
    gain_pair, shift_pair, w_qkv, qv_shift, w_out, out_shift, w_up, up_shift, w_down, down_shift = (
        layer_weight_list
    )
    gains = gain_pair.astype(jnp.float32)
    shifts = shift_pair.astype(jnp.float32)
    n_images, local_len, n_heads, head_dim = query_h.shape
    model_dim = x_rows.shape[1]
    grad_bf = gradient_token_rows.astype(jnp.bfloat16)
    g_down = jnp.einsum("rf,rd->fd", hidden, grad_bf, preferred_element_type=jnp.float32)
    g_down_shift = jnp.sum(gradient_token_rows, axis=0)
    d_hidden = jnp.einsum("rd,fd->rf", grad_bf, w_down, preferred_element_type=jnp.float32)
    d_up = jax.vjp(gelu_exact, up_pre)[1](d_hidden)[0]
    d_up_bf = d_up.astype(jnp.bfloat16)
    g_up = jnp.einsum("rd,rf->df", normed_two, d_up_bf, preferred_element_type=jnp.float32)
    g_up_shift = jnp.sum(d_up, axis=0)
    d_normed_two = jnp.einsum("rf,df->rd", d_up_bf, w_up, preferred_element_type=jnp.float32)
    norm_back_two = jax.vjp(norm_rows, resid_mid, gains[1], shifts[1])[1]
    d_mid, gradient_second_gain, g_shift_two = norm_back_two(d_normed_two)
    d_mid = gradient_token_rows + d_mid
    d_mid_bf = d_mid.astype(jnp.bfloat16)
    g_out = jnp.einsum("rc,rd->cd", attended, d_mid_bf, preferred_element_type=jnp.float32)
    g_out_shift = jnp.sum(d_mid, axis=0)
    d_attended = jnp.einsum("rd,cd->rc", d_mid_bf, w_out, preferred_element_type=jnp.float32)
    d_attended = d_attended.astype(jnp.bfloat16).reshape(n_images, local_len, n_heads, head_dim)
    scores = attention_scores(query_h, key_h, key_flags, attention_score_scale)
    attn_probs = jnp.exp(scores - log_total)
    probs_bf = attn_probs.astype(jnp.bfloat16)
    d_value_part = jnp.einsum(
        "nhqk,nqhd->nkhd", probs_bf, d_attended, preferred_element_type=jnp.float32
    )
    d_probs = jnp.einsum("nqhd,nkhd->nhqk", d_attended, value_h, preferred_element_type=jnp.float32)
    inner = jnp.sum(attn_probs * d_probs, axis=-1, keepdims=True)
    d_scores = (attn_probs * (d_probs - inner)).astype(jnp.bfloat16)
    d_query = (
        jnp.einsum("nhqk,nkhd->nqhd", d_scores, key_h, preferred_element_type=jnp.float32)
        * attention_score_scale
    )
    d_key_part = (
        jnp.einsum("nhqk,nqhd->nkhd", d_scores, query_h, preferred_element_type=jnp.float32)
        * attention_score_scale
    )
    full_shape = (n_images, key_h.shape[1], model_dim)
    d_key, d_value = (
        lax.psum_scatter(
            d_key_part.reshape(full_shape).astype(jnp.bfloat16),
            "seq",
            scatter_dimension=1,
            tiled=True,
        ).astype(jnp.float32),
        lax.psum_scatter(
            d_value_part.reshape(full_shape).astype(jnp.bfloat16),
            "seq",
            scatter_dimension=1,
            tiled=True,
        ).astype(jnp.float32),
    )
    row_count = n_images * local_len
    d_query_bf = d_query.reshape(row_count, model_dim).astype(jnp.bfloat16)
    d_key_bf = d_key.reshape(row_count, model_dim).astype(jnp.bfloat16)
    d_value_bf = d_value.reshape(row_count, model_dim).astype(jnp.bfloat16)
    d_qkv = jnp.concatenate([d_query_bf, d_key_bf, d_value_bf], axis=1)
    g_qkv = jnp.einsum("rd,re->de", normed, d_qkv, preferred_element_type=jnp.float32)
    g_qv_shift = jnp.stack(
        [
            jnp.sum(d_query_bf.astype(jnp.float32), axis=0),
            jnp.sum(d_value_bf.astype(jnp.float32), axis=0),
        ]
    )
    d_normed = jnp.einsum("re,de->rd", d_qkv, w_qkv, preferred_element_type=jnp.float32)
    norm_back_one = jax.vjp(norm_rows, x_rows, gains[0], shifts[0])[1]
    d_rows, g_gain_one, g_shift_one = norm_back_one(d_normed)
    d_rows = d_mid + d_rows
    layer_grads = (
        jnp.stack([g_gain_one, gradient_second_gain]),
        jnp.stack([g_shift_one, g_shift_two]),
        g_qkv,
        g_qv_shift,
        g_out,
        g_out_shift,
        g_up,
        g_up_shift,
        g_down,
        g_down_shift,
    )
    return (d_rows, layer_grads)


def per_device(
    tokens,
    keep,
    norm_gain,
    norm_bias,
    qkv_weight,
    qv_bias,
    out_weight,
    out_bias,
    up_weight,
    up_bias,
    down_weight,
    down_bias,
    cotangent,
):
    shards = (
        norm_gain,
        norm_bias,
        qkv_weight,
        qv_bias,
        out_weight,
        out_bias,
        up_weight,
        up_bias,
        down_weight,
        down_bias,
    )
    n_images, local_len, model_dim = tokens.shape
    micro_len = n_images // MICRO
    attention_score_scale = HEAD ** (-0.5)
    positions = lax.axis_index("seq") * local_len + lax.iota(jnp.int32, local_len)
    key_keep = (keep == 1) | (positions < BUFFER)[None, :]
    layer_sums = [None] * LAYERS
    outputs = []
    input_grads = []
    for micro_idx in range(MICRO):
        first_image = micro_idx * micro_len
        x = tokens[first_image : first_image + micro_len].astype(jnp.float32)
        keep_part = key_keep[first_image : first_image + micro_len]
        flag_send = keep_part.astype(jnp.bfloat16)
        saved_activations = []
        for layer_number in range(LAYERS):
            layer_weight_list = gather_forward(shards, layer_number)
            x, saved_activation = layer_forward(
                x, flag_send, layer_weight_list, attention_score_scale
            )
            saved_activations.append(saved_activation)
        mask_rows = keep_part.astype(jnp.float32)[..., None]
        outputs.append((x * mask_rows).astype(jnp.bfloat16))
        gradient_token_rows = (
            cotangent[first_image : first_image + micro_len].astype(jnp.float32) * mask_rows
        ).reshape(-1, model_dim)
        for layer_number in reversed(range(LAYERS)):
            layer_weight_list = gather_backward(shards, layer_number)
            gradient_token_rows, layer_grads = layer_backward(
                gradient_token_rows,
                saved_activations[layer_number],
                layer_weight_list,
                attention_score_scale,
            )
            if micro_idx == 0:
                layer_sums[layer_number] = layer_grads
            else:
                layer_sums[layer_number] = tuple(
                    (s + g for s, g in zip(layer_sums[layer_number], layer_grads))
                )
        input_grads.append(gradient_token_rows.reshape(micro_len, local_len, model_dim))
    stacked = tuple(
        (
            jnp.stack([layer_sums[layer_number][member] for layer_number in range(LAYERS)])
            for member in range(10)
        )
    )
    reduced = reduce_all(stacked)
    return (
        jnp.concatenate(outputs, axis=0),
        jnp.concatenate(input_grads, axis=0),
        reduced[0],
        reduced[1],
        reduced[2],
        reduced[3],
        reduced[4],
        reduced[5],
        reduced[6],
        reduced[7],
        reduced[8],
        reduced[9],
    )


def solution(mesh):
    placed = (
        P("dp", "seq", None),
        P("dp", "seq"),
        P(None, None, ("dp", "seq")),
        P(None, None, ("dp", "seq")),
        P(None, ("dp", "seq"), None),
        P(None, None, ("dp", "seq")),
        P(None, ("dp", "seq"), None),
        P(None, ("dp", "seq")),
        P(None, ("dp", "seq"), None),
        P(None, ("dp", "seq")),
        P(None, ("dp", "seq"), None),
        P(None, ("dp", "seq")),
        P("dp", "seq", None),
    )
    return jax.shard_map(
        per_device,
        mesh=mesh,
        in_specs=placed,
        out_specs=(
            P("dp", "seq", None),
            P("dp", "seq", None),
            P(None, None, ("dp", "seq")),
            P(None, None, ("dp", "seq")),
            P(None, ("dp", "seq"), None),
            P(None, None, ("dp", "seq")),
            P(None, ("dp", "seq"), None),
            P(None, ("dp", "seq")),
            P(None, ("dp", "seq"), None),
            P(None, ("dp", "seq")),
            P(None, ("dp", "seq"), None),
            P(None, ("dp", "seq")),
        ),
        check_vma=False,
    )
```

profile of v0, /device:TPU:0, one launch (start us, length us, event | category | flops | bytes accessed | tf_op | source)
XLA Modules:
  0.0 3677.4 jit_solution(14347329898653400945)
XLA Ops:
  25.7 41.6 %all-reduce.6 = (bf16[1024]{0:T(1024)(128)(2,1)S(1)}, bf16[1024]{0:T(1024)(128)(2,1)S(1)}, bf16[1024]{0:T(1024)(128)(2,1)S(1)}, bf16[1024]{0:T(1024)(128)(2,1)}) all-reduce(bf16[1024]{0:T(1024)(128)(2,1)S(1)} %dynamic-update-slice.1, bf16[1024]{0:T(1024)(128)(2,1)S(1)} %dynamic-update-slice.2, ...), channel_id=6, replica_groups=mesh['dp'=16,'seq'=2] {'dp','seq'}, use_global_device_ids=true, to_apply=%add.1 | all-reduce | flops 4096 | bytes 16384
  68.5 65.6 %all-gather.15 = bf16[1,4096]{1,0:T(2,128)(2,1)S(1)} all-gather(bf16[1,128]{1,0:T(2,128)(2,1)S(1)} %get-tuple-element.137), channel_id=17, replica_groups=mesh['dp'=16,'seq'=2] {'dp','seq'}, dimensions={1}, use_global_device_ids=true | all-gather | bytes 8448 | tf_op jit(solution)/shard_map/all_gather | solution.py:67
  134.1 63.0 %all-gather.27 = bf16[32,32,2]{1,2,0:T(2,128)(2,1)S(1)} all-gather(bf16[1,32,2]{1,2,0:T(2,128)(2,1)S(1)} %get-tuple-element.131), channel_id=1, replica_groups=mesh['dp'=16,'seq'=2] {'dp','seq'}, dimensions={0}, use_global_device_ids=true | all-gather | bytes 4224 | tf_op jit(solution)/shard_map/all_gather | solution.py:63
  197.2 65.3 %all-gather.26 = bf16[32,32,2]{1,2,0:T(2,128)(2,1)S(1)} all-gather(bf16[1,32,2]{1,2,0:T(2,128)(2,1)S(1)} %get-tuple-element.135), channel_id=1, replica_groups=mesh['dp'=16,'seq'=2] {'dp','seq'}, dimensions={0}, use_global_device_ids=true | all-gather | bytes 4224 | tf_op jit(solution)/shard_map/all_gather | solution.py:61
  262.6 63.5 %all-gather.25 = bf16[32,32,2]{1,2,0:T(2,128)(2,1)S(1)} all-gather(bf16[1,32,2]{1,2,0:T(2,128)(2,1)S(1)} %get-tuple-element.133), channel_id=1, replica_groups=mesh['dp'=16,'seq'=2] {'dp','seq'}, dimensions={0}, use_global_device_ids=true | all-gather | bytes 4224 | tf_op jit(solution)/shard_map/all_gather | solution.py:60
  326.3 65.2 %all-gather.6 = bf16[1,4096]{1,0:T(2,128)(2,1)S(1)} all-gather(bf16[1,128]{1,0:T(2,128)(2,1)S(1)} %get-tuple-element.138), channel_id=8, replica_groups=mesh['dp'=16,'seq'=2] {'dp','seq'}, dimensions={1}, use_global_device_ids=true | all-gather | bytes 8448 | tf_op jit(solution)/shard_map/all_gather | solution.py:67
  391.5 63.3 %all-gather.24 = bf16[32,32,2]{1,2,0:T(2,128)(2,1)S(1)} all-gather(bf16[1,32,2]{1,2,0:T(2,128)(2,1)S(1)} %get-tuple-element.132), channel_id=1, replica_groups=mesh['dp'=16,'seq'=2] {'dp','seq'}, dimensions={0}, use_global_device_ids=true | all-gather | bytes 4224 | tf_op jit(solution)/shard_map/all_gather | solution.py:63
  454.9 65.3 %all-gather.23 = bf16[32,32,2]{1,2,0:T(2,128)(2,1)S(1)} all-gather(bf16[1,32,2]{1,2,0:T(2,128)(2,1)S(1)} %get-tuple-element.136), channel_id=1, replica_groups=mesh['dp'=16,'seq'=2] {'dp','seq'}, dimensions={0}, use_global_device_ids=true | all-gather | bytes 4224 | tf_op jit(solution)/shard_map/all_gather | solution.py:61
  520.3 63.7 %all-gather.22 = bf16[32,32,2]{1,2,0:T(2,128)(2,1)S(1)} all-gather(bf16[1,32,2]{1,2,0:T(2,128)(2,1)S(1)} %get-tuple-element.134), channel_id=1, replica_groups=mesh['dp'=16,'seq'=2] {'dp','seq'}, dimensions={0}, use_global_device_ids=true | all-gather | bytes 4224 | tf_op jit(solution)/shard_map/all_gather | solution.py:60
  711.7 13.4 all-gather.20
  1061.4 17.9 pad_maximum_fusion.2
  1105.0 23.0 pad_maximum_fusion
  1131.9 12.9 add_bitcast_fusion
  1147.3 12.4 add_bitcast_fusion.1
  1159.7 23.7 pad_maximum_fusion.1
  1201.9 80.6 %reduce-scatter.77.cloned.1.call-done = f32[32,2]{1,0:T(8,128)} async-done(((f32[1024,2]{1,0:T(8,128)}), f32[32,2]{1,0:T(8,128)}) %reduce-scatter.77.cloned.1.call-update) | async-done | bytes 272
  1283.9 134.5 %reduce-scatter.79.cloned.1.call-done = f32[128,2]{1,0:T(8,128)} async-done(((f32[4096,2]{1,0:T(8,128)}), f32[128,2]{1,0:T(8,128)}) %reduce-scatter.79.cloned.1.call-update) | async-done | bytes 1040
  1421.6 129.0 %reduce-scatter.71.cloned.1.call-done = f32[32,4]{1,0:T(8,128)} async-done(((f32[1024,4]{1,0:T(8,128)}), f32[32,4]{1,0:T(8,128)}) %reduce-scatter.71.cloned.1.call-update) | async-done | bytes 528
  1552.1 130.7 %reduce-scatter.73.cloned.1.call-done = f32[32,4]{1,0:T(8,128)} async-done(((f32[1024,4]{1,0:T(8,128)}), f32[32,4]{1,0:T(8,128)}) %reduce-scatter.73.cloned.1.call-update) | async-done | bytes 528
  1684.3 130.8 %reduce-scatter.75.cloned.1.call-done = f32[32,4]{1,0:T(8,128)} async-done(((f32[1024,4]{1,0:T(8,128)}), f32[32,4]{1,0:T(8,128)}) %reduce-scatter.75.cloned.1.call-update) | async-done | bytes 528
  1816.5 180.4 %reduce-scatter.49.cloned.1.call-done = f32[2,32,1024]{2,1,0:T(8,128)} async-done(((f32[2,1024,1024]{2,1,0:T(8,128)}), f32[2,32,1024]{2,1,0:T(8,128)}) %reduce-scatter.49.cloned.1.call-update) | async-done | bytes 262160 | tf_op jit(solution)/shard_map/reduce_scatter | solution.py:110
  1997.0 253.3 %reduce-scatter.47.cloned.1.call-done = f32[2,32,3072]{2,1,0:T(8,128)} async-done(((f32[2,1024,3072]{2,1,0:T(8,128)}), f32[2,32,3072]{2,1,0:T(8,128)}) %reduce-scatter.47.cloned.1.call-update) | async-done | bytes 786448 | tf_op jit(solution)/shard_map/reduce_scatter | solution.py:108
  2250.3 708.5 %reduce-scatter.51.cloned.1.call-done = f32[2,32,4096]{2,1,0:T(8,128)} async-done(((f32[2,1024,4096]{2,1,0:T(8,128)}), f32[2,32,4096]{2,1,0:T(8,128)}) %reduce-scatter.51.cloned.1.call-update) | async-done | bytes 1048592 | tf_op jit(solution)/shard_map/reduce_scatter | solution.py:112
  2958.8 711.6 %reduce-scatter.53.cloned.1.call-done = f32[2,128,1024]{2,1,0:T(8,128)} async-done(((f32[2,4096,1024]{2,1,0:T(8,128)}), f32[2,128,1024]{2,1,0:T(8,128)}) %reduce-scatter.53.cloned.1.call-update) | async-done | bytes 1048592 | tf_op jit(solution)/shard_map/reduce_scatter | solution.py:114
  (822 shorter events, 539.2 us)
Async XLA Ops:
  7.3 576.9 %all-gather.37.cloned.1.call-start = ((), (), s32[]{:S(2)}) async-start(), calls=%async_computation.22 | async-start | bytes 6488064 | tf_op jit(solution)/shard_map/all_gather | solution.py:62
  9.4 632.1 %all-gather.39.cloned.1.call-start = ((), (), s32[]{:S(2)}) async-start(), calls=%async_computation.23 | async-start | bytes 2162688 | tf_op jit(solution)/shard_map/all_gather | solution.py:64
  11.0 638.3 %all-gather.41.cloned.1.call-start = ((), (), s32[]{:S(2)}) async-start(), calls=%async_computation.24 | async-start | bytes 8650752 | tf_op jit(solution)/shard_map/all_gather | solution.py:66
  12.9 647.7 %all-gather.43.cloned.1.call-start = ((), (), s32[]{:S(2)}) async-start(), calls=%async_computation.25 | async-start | bytes 8650752 | tf_op jit(solution)/shard_map/all_gather | solution.py:68
  13.8 652.6 %all-gather.45.cloned.1.call-start = ((), (), s32[]{:S(2)}) async-start(), calls=%async_computation.26 | async-start | bytes 6488064 | tf_op jit(solution)/shard_map/all_gather | solution.py:62
  14.4 728.2 %all-gather.47.cloned.1.call-start = ((), (), s32[]{:S(2)}) async-start(), calls=%async_computation.27 | async-start | bytes 2162688 | tf_op jit(solution)/shard_map/all_gather | solution.py:64
  15.0 735.5 %all-gather.49.cloned.1.call-start = ((), (), s32[]{:S(2)}) async-start(), calls=%async_computation.28 | async-start | bytes 8650752 | tf_op jit(solution)/shard_map/all_gather | solution.py:66
  15.7 751.5 %all-gather.51.cloned.1.call-start = ((), (), s32[]{:S(2)}) async-start(), calls=%async_computation.29 | async-start | bytes 8650752 | tf_op jit(solution)/shard_map/all_gather | solution.py:68
  16.5 843.1 %reduce-scatter.65.cloned.1.call-start = ((), (), s32[]{:S(2)}) async-start(), calls=%async_computation.35 | async-start | bytes 983040
  810.2 52.1 %reduce-scatter.57.cloned.1.call-start = ((), (), s32[]{:S(2)}) async-start(), calls=%async_computation.31 | async-start | bytes 983040
  835.5 47.5 %reduce-scatter.63.cloned.1.call-start = ((), (), s32[]{:S(2)}) async-start(), calls=%async_computation.34 | async-start | bytes 983040
  849.8 154.1 %reduce-scatter.69.cloned.1.call-start = ((), (), s32[]{:S(2)}) async-start(), calls=%async_computation.37 | async-start | bytes 983040
  941.7 64.5 %reduce-scatter.61.cloned.1.call-start = ((), (), s32[]{:S(2)}) async-start(), calls=%async_computation.33 | async-start | bytes 983040
  958.3 51.8 %reduce-scatter.59.cloned.1.call-start = ((), (), s32[]{:S(2)}) async-start(), calls=%async_computation.32 | async-start | bytes 983040
  994.6 206.0 %reduce-scatter.81.cloned.1.call-start = ((), (), s32[]{:S(2)}) async-start(), calls=%async_computation.43 | async-start | bytes 540672
  1000.1 282.5 %reduce-scatter.77.cloned.1.call-start = ((), (), s32[]{:S(2)}) async-start(), calls=%async_computation.41 | async-start | bytes 540672
  1001.2 417.2 %reduce-scatter.79.cloned.1.call-start = ((), (), s32[]{:S(2)}) async-start(), calls=%async_computation.42 | async-start | bytes 2162688
  1003.7 547.0 %reduce-scatter.71.cloned.1.call-start = ((), (), s32[]{:S(2)}) async-start(), calls=%async_computation.38 | async-start | bytes 540672
  1028.7 654.1 %reduce-scatter.73.cloned.1.call-start = ((), (), s32[]{:S(2)}) async-start(), calls=%async_computation.39 | async-start | bytes 540672
  1030.8 784.3 %reduce-scatter.75.cloned.1.call-start = ((), (), s32[]{:S(2)}) async-start(), calls=%async_computation.40 | async-start | bytes 540672
  1032.9 964.0 %reduce-scatter.49.cloned.1.call-start = ((), (), s32[]{:S(2)}) async-start(), calls=%async_computation.19 | async-start | bytes 8650752 | tf_op jit(solution)/shard_map/reduce_scatter | solution.py:110
  1041.5 1208.8 %reduce-scatter.47.cloned.1.call-start = ((), (), s32[]{:S(2)}) async-start(), calls=%async_computation.18 | async-start | bytes 25952256 | tf_op jit(solution)/shard_map/reduce_scatter | solution.py:108
  1079.5 1879.3 %reduce-scatter.51.cloned.1.call-start = ((), (), s32[]{:S(2)}) async-start(), calls=%async_computation.20 | async-start | bytes 34603008 | tf_op jit(solution)/shard_map/reduce_scatter | solution.py:112
  1128.0 2542.4 %reduce-scatter.53.cloned.1.call-start = ((), (), s32[]{:S(2)}) async-start(), calls=%async_computation.21 | async-start | bytes 34603008 | tf_op jit(solution)/shard_map/reduce_scatter | solution.py:114
  (230 other events, 9309.1 us)
Sparse Core Ops, SparseCore 0:
  11.6 72.9 all-gather.36
  87.5 55.0 all-gather.38
  146.2 76.3 all-gather.40
  226.0 76.0 all-gather.42
  304.9 68.1 all-gather.44
  375.9 55.0 all-gather.46
  434.0 76.2 all-gather.48
  513.9 80.0 all-gather.50
  810.4 17.2 reduce-scatter.64
  848.1 16.0 reduce-scatter.54
  866.9 16.0 reduce-scatter.62
  941.8 15.9 reduce-scatter.68
  960.6 16.0 reduce-scatter.60
  979.4 15.9 reduce-scatter.58
  1016.2 134.1 reduce-scatter.80
  1152.6 129.9 reduce-scatter.76
  1284.8 133.5 reduce-scatter.78
  1420.6 130.0 reduce-scatter.70
  1552.9 129.8 reduce-scatter.72
  1685.1 129.9 reduce-scatter.74
  1817.9 178.9 reduce-scatter.48
  2003.8 246.3 reduce-scatter.46
  2253.2 705.5 reduce-scatter.50
  2961.6 708.7 reduce-scatter.52
  (2 shorter events, 31.8 us)
where the time goes:
time: 3690 us; the launch traced here: 3680 us
  waiting for transfers between devices  2470 us (67%)
  blocking collectives  635 us (17%)
  matrix products  303 us (8%)
  local copies, waits for them, and re-layouts  139 us (4%)
  other arithmetic  105 us (3%)
    reduce_scatter x1, waiting for transfers between devices, reduce_all(): lax.psum_scatter(turned[8], ('dp', 'seq'), scatter_dimension=1, tiled=True)  712 us
    reduce_scatter x1, waiting for transfers between devices, reduce_all(): lax.psum_scatter(turned[6], ('dp', 'seq'), scatter_dimension=1, tiled=True)  709 us
    unnamed x40, waiting for transfers between devices  621 us
    reduce_scatter x1, waiting for transfers between devices, reduce_all(): lax.psum_scatter(turned[2], ('dp', 'seq'), scatter_dimension=1, tiled=True)  253 us
    reduce_scatter x1, waiting for transfers between devices, reduce_all(): lax.psum_scatter(turned[4], ('dp', 'seq'), scatter_dimension=1, tiled=True)  180 us
    all_gather x2, blocking collectives, gather_forward(): lax.all_gather(pieces[7], ('dp', 'seq'), axis=0, tiled=True)  131 us
    all_gather x2, blocking collectives, gather_forward(): lax.all_gather(pieces[1], ('dp', 'seq'), axis=0, tiled=True)  131 us
    all_gather x2, blocking collectives, gather_forward(): lax.all_gather(pieces[0], ('dp', 'seq'), axis=0, tiled=True)  127 us
  transfers between devices with their start and end apart: 26, of which 10 were waited for; matrix products, arithmetic and copies ran while one was open for 12% of the time, Pallas kernels for 0%

commit v1 on v0

v1 whole, which is shorter than its diff:
```python
import jax
import jax.numpy as jnp
from jax import lax
from jax.experimental import pallas as pl
from jax.experimental.pallas import tpu as pltpu
from jax.sharding import PartitionSpec as P

HEAD = 64
BUFFER = 64
LAYERS = 2
AXES = ("dp", "seq")

masked_score = -1e30
f32 = jnp.float32
bf16 = jnp.bfloat16


def norm_rows(x, gain_vec, shift_vec):
    row_mean = jnp.mean(x, axis=-1, keepdims=True)
    centered = x - row_mean
    variance = jnp.mean(centered * centered, axis=-1, keepdims=True)
    return centered * lax.rsqrt(variance + 1e-06) * gain_vec + shift_vec


def gelu_exact(v):
    return jax.nn.gelu(v, approximate=False)


def exchange(value, mask, n):
    return lax.ppermute(value, AXES, [(i, i ^ mask) for i in range(n)])


def mask_orders(n):
    bits = n.bit_length() - 1
    across, partner = 1, 2
    near = [4] if bits > 2 else []
    far = [(1 << k) | (1 << (k - 1)) if k > 3 else 1 << k for k in range(bits - 1, 2, -1)]
    return {
        "up": far + [across] + near + [partner],
        "down": far + near + [across] + [partner],
        "qkv": [across] + near + far + [partner],
    }


def span_table(masks):
    table = [0]
    for m in masks:
        table = table + [t ^ m for t in table]
    return table


def positions_of(masks, me):
    n = 1 << len(masks)
    table = span_table(masks)
    inverse = [0] * n
    for p, t in enumerate(table):
        inverse[t] = p
    inverse = jnp.asarray(inverse, jnp.int32)
    return inverse[me ^ jnp.arange(n, dtype=jnp.int32)]


def owners_of(masks, me):
    return me ^ jnp.asarray(span_table(masks), jnp.int32)


def reorder_body(order, src, dst):
    dst[...] = src[...]


def reorder(blocks, order):
    n, rows, cols = blocks.shape
    spec_in = pl.BlockSpec((1, rows, cols), lambda j, o: (o[j], 0, 0))
    spec_out = pl.BlockSpec((1, rows, cols), lambda j, o: (j, 0, 0))
    size = blocks.size * blocks.dtype.itemsize
    return pl.pallas_call(
        reorder_body,
        grid_spec=pltpu.PrefetchScalarGridSpec(
            num_scalar_prefetch=1, grid=(n,), in_specs=[spec_in], out_specs=spec_out
        ),
        out_shape=jax.ShapeDtypeStruct(blocks.shape, blocks.dtype),
        cost_estimate=pl.CostEstimate(flops=0, bytes_accessed=2 * size, transcendentals=0),
        name="reorder",
    )(order, blocks)


def gather(own, masks, me, n):
    held = own[None]
    for m in masks:
        held = jnp.concatenate([held, exchange(held, m, n)], axis=0)
    whole = reorder(held, positions_of(masks, me))
    return whole.reshape(n * own.shape[0], own.shape[1])


def scatter_sum(whole, masks, me, n):
    rows, cols = whole.shape
    held = reorder(whole.reshape(n, rows // n, cols), owners_of(masks, me))
    for m in reversed(masks):
        half = held.shape[0] // 2
        got = exchange(held[half:], m, n)
        total = held[:half].astype(f32) + got.astype(f32)
        held = total if half == 1 else total.astype(bf16)
    return held[0]


def attention_scores(query_h, key_h, key_flags, attention_score_scale):
    scores = (
        jnp.einsum("qhd,khd->hqk", query_h, key_h, preferred_element_type=f32)
        * attention_score_scale
    )
    return jnp.where(key_flags[None, None, :] > 0, scores, masked_score)


def layer_forward(x_rows, key_flags, vectors, w_qkv, w_up_out, w_down, scale):
    length, model_dim = x_rows.shape
    n_heads = model_dim // HEAD
    hidden_dim = w_down.shape[0]
    gains, shifts, qv_shift, out_shift, up_shift, down_shift = vectors
    normed = norm_rows(x_rows, gains[0], shifts[0]).astype(bf16)
    qkv_all = jnp.dot(normed, w_qkv, preferred_element_type=f32)
    query_bf = (qkv_all[:, :model_dim] + qv_shift[0]).astype(bf16)
    key_bf = qkv_all[:, model_dim : 2 * model_dim].astype(bf16)
    value_bf = (qkv_all[:, 2 * model_dim : 3 * model_dim] + qv_shift[1]).astype(bf16)
    query_h = query_bf.reshape(length, n_heads, HEAD)
    key_h = key_bf.reshape(length, n_heads, HEAD)
    value_h = value_bf.reshape(length, n_heads, HEAD)
    scores = attention_scores(query_h, key_h, key_flags, scale)
    row_max = jnp.max(scores, axis=-1, keepdims=True)
    row_sum = jnp.sum(jnp.exp(scores - row_max), axis=-1, keepdims=True)
    log_total = row_max + jnp.log(row_sum)
    attn_probs = jnp.exp(scores - log_total).astype(bf16)
    attended = jnp.einsum("hqk,khd->qhd", attn_probs, value_h, preferred_element_type=f32)
    attended = attended.reshape(length, model_dim).astype(bf16)
    w_out = w_up_out[:, hidden_dim:]
    resid_mid = x_rows + jnp.dot(attended, w_out, preferred_element_type=f32) + out_shift
    normed_two = norm_rows(resid_mid, gains[1], shifts[1]).astype(bf16)
    w_up = w_up_out[:, :hidden_dim]
    up_pre = jnp.dot(normed_two, w_up, preferred_element_type=f32) + up_shift
    hidden = gelu_exact(up_pre).astype(bf16)
    result = resid_mid + jnp.dot(hidden, w_down, preferred_element_type=f32) + down_shift
    saved = (
        x_rows,
        normed,
        query_h,
        key_h,
        value_h,
        key_flags,
        log_total,
        attended,
        resid_mid,
        normed_two,
        up_pre,
        hidden,
    )
    return result, saved


def layer_backward(grad_rows, saved, vectors, w_qkv, w_up_out, w_down, scale):
    (
        x_rows,
        normed,
        query_h,
        key_h,
        value_h,
        key_flags,
        log_total,
        attended,
        resid_mid,
        normed_two,
        up_pre,
        hidden,
    ) = saved
    gains, shifts, qv_shift, out_shift, up_shift, down_shift = vectors
    length, model_dim = x_rows.shape
    hidden_dim = w_down.shape[0]
    grad_bf = grad_rows.astype(bf16)
    g_down = jnp.einsum("rf,rd->fd", hidden, grad_bf, preferred_element_type=f32).astype(bf16)
    g_down_shift = jnp.sum(grad_rows, axis=0)
    d_hidden = jnp.einsum("rd,fd->rf", grad_bf, w_down, preferred_element_type=f32)
    d_up = jax.vjp(gelu_exact, up_pre)[1](d_hidden)[0]
    d_up_bf = d_up.astype(bf16)
    g_up = jnp.einsum("rd,rf->df", normed_two, d_up_bf, preferred_element_type=f32).astype(bf16)
    g_up_shift = jnp.sum(d_up, axis=0)
    w_up = w_up_out[:, :hidden_dim]
    d_normed_two = jnp.einsum("rf,df->rd", d_up_bf, w_up, preferred_element_type=f32)
    norm_back_two = jax.vjp(norm_rows, resid_mid, gains[1], shifts[1])[1]
    d_mid, g_gain_two, g_shift_two = norm_back_two(d_normed_two)
    d_mid = grad_rows + d_mid
    d_mid_bf = d_mid.astype(bf16)
    g_out = jnp.einsum("rc,rd->cd", attended, d_mid_bf, preferred_element_type=f32).astype(bf16)
    g_out_shift = jnp.sum(d_mid, axis=0)
    w_out = w_up_out[:, hidden_dim:]
    d_attended = jnp.einsum("rd,cd->rc", d_mid_bf, w_out, preferred_element_type=f32)
    d_attended = d_attended.astype(bf16).reshape(query_h.shape)
    scores = attention_scores(query_h, key_h, key_flags, scale)
    attn_probs = jnp.exp(scores - log_total)
    probs_bf = attn_probs.astype(bf16)
    d_value = jnp.einsum("hqk,qhd->khd", probs_bf, d_attended, preferred_element_type=f32)
    d_probs = jnp.einsum("qhd,khd->hqk", d_attended, value_h, preferred_element_type=f32)
    inner = jnp.sum(attn_probs * d_probs, axis=-1, keepdims=True)
    d_scores = (attn_probs * (d_probs - inner)).astype(bf16)
    d_query = jnp.einsum("hqk,khd->qhd", d_scores, key_h, preferred_element_type=f32) * scale
    d_key = jnp.einsum("hqk,qhd->khd", d_scores, query_h, preferred_element_type=f32) * scale
    d_query_bf = d_query.reshape(length, model_dim).astype(bf16)
    d_key_bf = d_key.reshape(length, model_dim).astype(bf16)
    d_value_bf = d_value.reshape(length, model_dim).astype(bf16)
    d_qkv = jnp.concatenate([d_query_bf, d_key_bf, d_value_bf], axis=1)
    g_qkv = jnp.einsum("rd,re->de", normed, d_qkv, preferred_element_type=f32).astype(bf16)
    g_query_shift = jnp.sum(d_query_bf.astype(f32), axis=0)
    g_value_shift = jnp.sum(d_value_bf.astype(f32), axis=0)
    d_normed = jnp.einsum("re,de->rd", d_qkv, w_qkv, preferred_element_type=f32)
    norm_back_one = jax.vjp(norm_rows, x_rows, gains[0], shifts[0])[1]
    d_rows, g_gain_one, g_shift_one = norm_back_one(d_normed)
    d_rows = d_mid + d_rows
    vector_grads = [
        g_gain_one,
        g_gain_two,
        g_shift_one,
        g_shift_two,
        g_query_shift,
        g_value_shift,
        g_out_shift,
        g_down_shift,
        g_up_shift,
    ]
    return d_rows, vector_grads, g_qkv, jnp.concatenate([g_up, g_out], axis=1), g_down


def per_device(
    n_devices,
    tokens,
    keep,
    norm_gain,
    norm_bias,
    qkv_weight,
    qv_bias,
    out_weight,
    out_bias,
    up_weight,
    up_bias,
    down_weight,
    down_bias,
    cotangent,
):
    n = n_devices
    seq_at = lax.axis_index("seq")
    me = lax.axis_index("dp") * 2 + seq_at
    n_images, local_len, model_dim = tokens.shape
    half_images = n_images // 2
    scale = HEAD ** (-0.5)
    orders = mask_orders(n)
    width = norm_gain.shape[2]
    ratio = up_bias.shape[1] // width

    positions = seq_at * local_len + lax.iota(jnp.int32, local_len)
    key_keep = ((keep == 1) | (positions < BUFFER)[None, :]).astype(bf16)

    def halves(value):
        low, high = value[:half_images], value[half_images:]
        mine = jnp.where(seq_at == 0, low, high)
        other = jnp.where(seq_at == 0, high, low)
        return mine, other

    def joined(mine, other):
        return jnp.where(
            seq_at == 0,
            jnp.concatenate([mine, other], axis=0),
            jnp.concatenate([other, mine], axis=0),
        )

    keep_mine, keep_other = halves(key_keep)
    tok_mine, tok_other = halves(tokens)
    cot_mine, cot_other = halves(cotangent)
    keep_all = jnp.concatenate([keep_mine, exchange(keep_other, 1, n)], axis=1)
    tok_all = jnp.concatenate([tok_mine, exchange(tok_other, 1, n)], axis=1)
    cot_all = jnp.concatenate([cot_mine, exchange(cot_other, 1, n)], axis=1)

    def columns(l):
        return [norm_gain[l, 0], norm_gain[l, 1], norm_bias[l, 0], norm_bias[l, 1]] + [
            qv_bias[l, 0],
            qv_bias[l, 1],
            out_bias[l],
            down_bias[l],
        ] + [up_bias[l, q * width : (q + 1) * width] for q in range(ratio)]

    stacked = jnp.stack(sum([columns(l) for l in range(LAYERS)], []))
    per_layer = stacked.shape[0] // LAYERS
    side = 128
    stacked = jnp.pad(stacked, ((0, side - stacked.shape[0]), (0, 0))).T

    w_qkv, w_up_out, w_down = [], [], []
    for l in range(LAYERS):
        own = qkv_weight[l]
        if l == 0:
            own = jnp.concatenate([own, stacked], axis=1)
        w_qkv.append(gather(own, orders["qkv"], me, n))
        own = jnp.concatenate([up_weight[l], out_weight[l]], axis=1)
        w_up_out.append(gather(own, orders["up"], me, n))
        w_down.append(gather(down_weight[l], orders["down"], me, n))
    table = w_qkv[0][:, 3 * model_dim :].T.astype(f32)
    w_qkv[0] = w_qkv[0][:, : 3 * model_dim]

    vectors = []
    for l in range(LAYERS):
        rows = table[l * per_layer : (l + 1) * per_layer]
        up_shift = rows[8:].reshape(ratio, n, width).transpose(1, 0, 2).reshape(-1)
        vectors.append((rows[0:2], rows[2:4], rows[4:6], rows[6], up_shift, rows[7]))
    vectors = [(g, s, qv, o, u, d) for g, s, qv, o, u, d in vectors]

    outputs, input_grads = [], []
    sums = None
    for image in range(half_images):
        x = tok_all[image].astype(f32)
        flags = keep_all[image]
        saves = []
        for l in range(LAYERS):
            x, saved = layer_forward(x, flags, vectors[l], w_qkv[l], w_up_out[l], w_down[l], scale)
            saves.append(saved)
        mask_rows = flags.astype(f32)[:, None]
        outputs.append((x * mask_rows).astype(bf16))
        grad = cot_all[image].astype(f32) * mask_rows
        parts = [None] * LAYERS
        for l in reversed(range(LAYERS)):
            grad, vg, g_qkv, g_up_out, g_down = layer_backward(
                grad, saves[l], vectors[l], w_qkv[l], w_up_out[l], w_down[l], scale
            )
            parts[l] = (vg, g_qkv, g_up_out, g_down)
        input_grads.append(grad.astype(bf16))
        sums = parts if sums is None else jax.tree.map(jnp.add, sums, parts)

    out_qkv, out_up, out_out, out_down = [None] * 2, [None] * 2, [None] * 2, [None] * 2
    hidden_dim = up_bias.shape[1] * n
    vector_out = None
    for l in reversed(range(LAYERS)):
        vg, g_qkv, g_up_out, g_down = sums[l]
        out_down[l] = scatter_sum(g_down, orders["down"], me, n)
        both = scatter_sum(g_up_out, orders["up"], me, n)
        out_up[l], out_out[l] = both[:, :hidden_dim], both[:, hidden_dim:]
        if l == 0:
            rows = []
            for k in range(LAYERS):
                vk = sums[k][0]
                rows += vk[:8]
                up_rows = vk[8].reshape(n, ratio, width).transpose(1, 0, 2).reshape(ratio, -1)
                rows += [up_rows[q] for q in range(ratio)]
            rows = jnp.stack(rows)
            rows = jnp.pad(rows, ((0, side - rows.shape[0]), (0, 0))).T.astype(bf16)
            g_qkv = jnp.concatenate([g_qkv, rows], axis=1)
        got = scatter_sum(g_qkv, orders["qkv"], me, n)
        out_qkv[l] = got[:, : 3 * model_dim]
        if l == 0:
            vector_out = got[:, 3 * model_dim :].T

    def pick(at):
        return jnp.stack([vector_out[l * per_layer + at] for l in range(LAYERS)])

    grad_gain = jnp.stack([pick(0), pick(1)], axis=1)
    grad_shift = jnp.stack([pick(2), pick(3)], axis=1)
    grad_qv = jnp.stack([pick(4), pick(5)], axis=1)
    grad_up_shift = jnp.concatenate([pick(8 + q) for q in range(ratio)], axis=1)

    def handed_back(values):
        whole = jnp.stack(values)
        back = exchange(whole[:, local_len:], 1, n)
        return joined(whole[:, :local_len], back)

    return (
        handed_back(outputs),
        handed_back(input_grads).astype(f32),
        grad_gain,
        grad_shift,
        jnp.stack(out_qkv),
        grad_qv,
        jnp.stack(out_out),
        pick(6),
        jnp.stack(out_up),
        grad_up_shift,
        jnp.stack(out_down),
        pick(7),
    )


def solution(mesh):
    n_devices = mesh.shape["dp"] * mesh.shape["seq"]
    rows = P(None, AXES, None)
    last = P(None, None, AXES)
    flat = P(None, AXES)
    batch = P("dp", "seq", None)

    def body(*args):
        return per_device(n_devices, *args)

    return jax.shard_map(
        body,
        mesh=mesh,
        in_specs=(
            batch,
            P("dp", "seq"),
            last,
            last,
            rows,
            last,
            rows,
            flat,
            rows,
            flat,
            rows,
            flat,
            batch,
        ),
        out_specs=(batch, batch, last, last, rows, last, rows, flat, rows, flat, rows, flat),
        check_vma=False,
    )
```

time: 3690 us -> 1250 us (0.34)
  waiting for transfers between devices: 2470 us -> 410 us
  blocking collectives: 635 us -> 0 us
  Pallas kernels: 0 us -> 240 us
  starting transfers between devices: 1.82 us -> 125 us
  matrix products: 303 us -> 190 us
    reduce_scatter x4 -> x0, waiting for transfers between devices: 1850 us -> none  [the longest x1 712 us: reduce_all(): lax.psum_scatter(turned[8], ('dp', 'seq'), scatter_dimension=1, tiled=True)]
    unnamed x40 -> x0, waiting for transfers between devices: 621 us -> none
    all_gather x16 -> x0, blocking collectives: 588 us -> none  [the longest x2 131 us: gather_forward(): lax.all_gather(pieces[7], ('dp', 'seq'), axis=0, tiled=True)]
    ppermute x0 -> x65, waiting for transfers between devices: none -> 410 us  [exchange(): return lax.ppermute(value, AXES, [(i, i ^ mask) for i in range(n)])]
    pallas_call x0 -> x12, Pallas kernels: none -> 240 us  [reorder(): pl.pallas_call(reorder_body, grid_spec=pltpu.PrefetchScalarGridSpec(num_s...]
    ppermute x0 -> x65, starting transfers between devices: none -> 125 us  [exchange(): return lax.ppermute(value, AXES, [(i, i ^ mask) for i in range(n)])]
    dot_general x72 -> x36, matrix products: 303 us -> 190 us  [the longest x2 35.4 us: layer_forward(): up_pre = jnp.dot(normed_two, w_up, preferred_element_type=f32) + up_shift]
    unnamed x526 -> x332, local copies, waits for them, and re-layouts: 110 us -> 35 us
  transfers between devices with their start and end apart: 26 -> 65, of which waited for: 10 -> 26; matrix products, arithmetic and copies ran while one was open for 12% -> 25% of each run, Pallas kernels for 0% -> 18%
where the time goes in v1:
time: 1250 us; the launch traced here: 1220 us
  waiting for transfers between devices  410 us (33%)
  Pallas kernels  240 us (19%)
  matrix products  190 us (15%)
  local copies, waits for them, and re-layouts  147 us (12%)
  starting transfers between devices  125 us (10%)
  other arithmetic  110 us (9%)
    ppermute x65, waiting for transfers between devices, exchange(): return lax.ppermute(value, AXES, [(i, i ^ mask) for i in range(n)])  410 us
    pallas_call x12, Pallas kernels, reorder(): pl.pallas_call(reorder_body, grid_spec=pltpu.PrefetchScalarGridSpec(num_s...  240 us
    ppermute x65, starting transfers between devices, exchange(): return lax.ppermute(value, AXES, [(i, i ^ mask) for i in range(n)])  125 us
    convert_element_type x24, other arithmetic, scatter_sum(): held = total if half == 1 else total.astype(bf16)  55.2 us
    slice x30, local copies, waits for them, and re-layouts, scatter_sum(): got = exchange(held[half:], m, n)  43.5 us
    concatenate x12, local copies, waits for them, and re-layouts, gather(): held = jnp.concatenate([held, exchange(held, m, n)], axis=0)  40.7 us
    dot_general x2, matrix products, layer_forward(): up_pre = jnp.dot(normed_two, w_up, preferred_element_type=f32) + up_shift  35.4 us
    unnamed x332, local copies, waits for them, and re-layouts  35 us
  transfers between devices with their start and end apart: 65, of which 26 were waited for; matrix products, arithmetic and copies ran while one was open for 25% of the time, Pallas kernels for 18%

profile of v1, /device:TPU:0, one launch (start us, length us, event | category | flops | bytes accessed | tf_op | source)
XLA Modules:
  0.0 1225.0 jit_solution(7325072694572178502)
XLA Ops:
  111.7 15.9 %collective-permute-done.19 = bf16[4,32,3072]{2,1,0:T(8,128)(2,1)S(1)} collective-permute-done((bf16[4,32,3072]{2,1,0:T(8,128)(2,1)S(1)}, bf16[4,32,3072]{2,1,0:T(8,128)(2,1)S(1)}, u32[]{:S(2)}, u32[]{:S(2)}) %collective-permute-start.19) | collective-permute-done | bytes 786464 | tf_op jit(solution)/shard_map/ppermute | solution.py:30
  151.5 16.0 %collective-permute-done.9 = bf16[4,32,5120]{2,1,0:T(8,128)(2,1)S(1)} collective-permute-done((bf16[4,32,5120]{2,1,0:T(8,128)(2,1)S(1)}, bf16[4,32,5120]{2,1,0:T(8,128)(2,1)S(1)}, u32[]{:S(2)}, u32[]{:S(2)}) %collective-permute-start.9) | collective-permute-done | bytes 1310752 | tf_op jit(solution)/shard_map/ppermute | solution.py:30
  182.2 28.3 %collective-permute-done.4 = bf16[8,32,3200]{2,1,0:T(8,128)(2,1)S(1)} collective-permute-done((bf16[8,32,3200]{2,1,0:T(8,128)(2,1)S(1)}, bf16[8,32,3200]{2,1,0:T(8,128)(2,1)S(1)}, u32[]{:S(2)}, u32[]{:S(2)}) %collective-permute-start.4) | collective-permute-done | bytes 1638432 | tf_op jit(solution)/shard_map/ppermute | solution.py:30
  219.2 35.2 %collective-permute-done.15 = bf16[8,128,1024]{2,1,0:T(8,128)(2,1)S(1)} collective-permute-done((bf16[8,128,1024]{2,1,0:T(8,128)(2,1)S(1)}, bf16[8,128,1024]{2,1,0:T(8,128)(2,1)S(1)}, u32[]{:S(2)}, u32[]{:S(2)}) %collective-permute-start.15) | collective-permute-done | bytes 2097184 | tf_op jit(solution)/shard_map/ppermute | solution.py:30
  275.8 19.2 %reorder.15 = bf16[32,32,3072]{2,1,0:T(8,128)(2,1)} custom-call(s32[32]{0:T(128)} %gather_fusion, bf16[32,32,3072]{2,1,0:T(8,128)(2,1)} %constant_dynamic-update-slice_fusion.38.src), custom_call_target="tpu_custom_call" | custom-call | bytes 12582912 | tf_op jit(solution)/shard_map/reorder/pallas_call | solution.py:75
  298.8 19.5 %reorder.12 = bf16[32,32,3200]{2,1,0:T(8,128)(2,1)} custom-call(s32[32]{0:T(128)} %gather_fusion, bf16[32,32,3200]{2,1,0:T(8,128)(2,1)} %constant_dynamic-update-slice_fusion.5.src), custom_call_target="tpu_custom_call" | custom-call | bytes 13107200 | tf_op jit(solution)/shard_map/reorder/pallas_call | solution.py:75
  343.9 19.8 %reorder.17 = bf16[32,128,1024]{2,1,0:T(8,128)(2,1)} custom-call(s32[32]{0:T(128)} %gather_fusion.2, bf16[32,128,1024]{2,1,0:T(8,128)(2,1)} %constant_dynamic-update-slice_fusion.60.src), custom_call_target="tpu_custom_call" | custom-call | bytes 16777216 | tf_op jit(solution)/shard_map/reorder/pallas_call | solution.py:75
  368.6 19.8 %reorder.14 = bf16[32,128,1024]{2,1,0:T(8,128)(2,1)} custom-call(s32[32]{0:T(128)} %gather_fusion.2, bf16[32,128,1024]{2,1,0:T(8,128)(2,1)} %constant_dynamic-update-slice_fusion.27.src), custom_call_target="tpu_custom_call" | custom-call | bytes 16777216 | tf_op jit(solution)/shard_map/reorder/pallas_call | solution.py:75
  393.8 20.5 %reorder.16 = bf16[32,32,5120]{2,1,0:T(8,128)(2,1)} custom-call(s32[32]{0:T(128)} %gather_fusion.1, bf16[32,32,5120]{2,1,0:T(8,128)(2,1)} %constant_dynamic-update-slice_fusion.49.src), custom_call_target="tpu_custom_call" | custom-call | bytes 20971520 | tf_op jit(solution)/shard_map/reorder/pallas_call | solution.py:75
  419.6 20.8 %reorder.13 = bf16[32,32,5120]{2,1,0:T(8,128)(2,1)} custom-call(s32[32]{0:T(128)} %gather_fusion.1, bf16[32,32,5120]{2,1,0:T(8,128)(2,1)} %constant_dynamic-update-slice_fusion.16.src), custom_call_target="tpu_custom_call" | custom-call | bytes 20971520 | tf_op jit(solution)/shard_map/reorder/pallas_call | solution.py:75
  443.6 18.4 %multiply_convert_fusion.3 = (bf16[320,4096]{1,0:T(8,128)(2,1)S(1)}, f32[320,4096]{1,0:T(8,128)}, f32[320,4096]{1,0:T(8,128)}) fusion(f32[4096]{0:T(1024)S(1)} %add.369, bf16[1024,5120]{1,0:T(8,128)(2,1)} %bitcast.278, f32[320,1024]{1,0:T(8,128)S(1)} %get-tuple-element.237, f32[1024]{0:T(1024)S(1)} %bitcast.370, f32[1024]{0:T(1024)S(1)} %bitcast.355, ...), kind=kOutput, calls=%fused_computation.65 | convolution fusion | flops 2772500480 | bytes 22833664 | tf_op jit(solution)/shard_map/dot_general | solution.py:137
  485.7 17.0 %multiply_convert_fusion.2 = (bf16[320,4096]{1,0:T(8,128)(2,1)}, f32[320,4096]{1,0:T(8,128)}, f32[320,4096]{1,0:T(8,128)}) fusion(f32[4096]{0:T(1024)S(1)} %add.395, bf16[1024,5120]{1,0:T(8,128)(2,1)S(1)} %bitcast.285, f32[320,1024]{1,0:T(8,128)S(1)} %get-tuple-element.244, f32[1024]{0:T(1024)S(1)} %bitcast.363, f32[1024]{0:T(1024)S(1)} %bitcast.347, ...), kind=kOutput, calls=%fused_computation.52 | convolution fusion | flops 2772500480 | bytes 22835200 | tf_op jit(solution)/shard_map/dot_general | solution.py:137
  632.4 19.3 %reorder.18 = bf16[32,32,3200]{2,1,0:T(8,128)(2,1)} custom-call(s32[32]{0:T(128)} %broadcast_xor_fusion.2.order, bf16[32,32,3200]{2,1,0:T(8,128)(2,1)} %bitcast.272), custom_call_target="tpu_custom_call" | custom-call | bytes 13107200 | tf_op jit(solution)/shard_map/reorder/pallas_call | solution.py:75
  656.0 19.8 %reorder.22 = bf16[32,128,1024]{2,1,0:T(8,128)(2,1)} custom-call(s32[32]{0:T(128)} %get-tuple-element.267.order, bf16[32,128,1024]{2,1,0:T(8,128)(2,1)} %bitcast.293), custom_call_target="tpu_custom_call" | custom-call | bytes 16777216 | tf_op jit(solution)/shard_map/reorder/pallas_call | solution.py:75
  688.8 20.2 %reorder.23 = bf16[32,128,1024]{2,1,0:T(8,128)(2,1)} custom-call(s32[32]{0:T(128)} %get-tuple-element.267.order, bf16[32,128,1024]{2,1,0:T(8,128)(2,1)} %bitcast.294), custom_call_target="tpu_custom_call" | custom-call | bytes 16777216 | tf_op jit(solution)/shard_map/reorder/pallas_call | solution.py:75
  714.3 19.2 %reorder.19 = bf16[32,32,3072]{2,1,0:T(8,128)(2,1)} custom-call(s32[32]{0:T(128)} %broadcast_xor_fusion.2.order, bf16[32,32,3072]{2,1,0:T(8,128)(2,1)} %bitcast.316), custom_call_target="tpu_custom_call" | custom-call | bytes 12582912 | tf_op jit(solution)/shard_map/reorder/pallas_call | solution.py:75
  769.9 20.6 %reorder.20 = bf16[32,32,5120]{2,1,0:T(8,128)(2,1)} custom-call(s32[32]{0:T(128)} %get-tuple-element.266.order, bf16[32,32,5120]{2,1,0:T(8,128)(2,1)} %bitcast.264), custom_call_target="tpu_custom_call" | custom-call | bytes 20971520 | tf_op jit(solution)/shard_map/reorder/pallas_call | solution.py:75
  795.7 20.8 %reorder.21 = bf16[32,32,5120]{2,1,0:T(8,128)(2,1)} custom-call(s32[32]{0:T(128)} %get-tuple-element.266.order, bf16[32,32,5120]{2,1,0:T(8,128)(2,1)} %bitcast.265), custom_call_target="tpu_custom_call" | custom-call | bytes 20971520 | tf_op jit(solution)/shard_map/reorder/pallas_call | solution.py:75
  851.2 15.6 %collective-permute-done.41 = bf16[8,32,3072]{2,1,0:T(8,128)(2,1)} collective-permute-done((bf16[8,32,3072]{2,1,0:T(8,128)(2,1)S(1)}, bf16[8,32,3072]{2,1,0:T(8,128)(2,1)}, u32[]{:S(2)}, u32[]{:S(2)}) %collective-permute-start.41) | collective-permute-done | bytes 1572896 | tf_op jit(solution)/shard_map/ppermute | solution.py:30
  869.4 31.3 %collective-permute-done.36 = bf16[8,32,3200]{2,1,0:T(8,128)(2,1)} collective-permute-done((bf16[8,32,3200]{2,1,0:T(8,128)(2,1)}, bf16[8,32,3200]{2,1,0:T(8,128)(2,1)}, u32[]{:S(2)}, u32[]{:S(2)}) %collective-permute-start.36) | collective-permute-done | bytes 1638432 | tf_op jit(solution)/shard_map/ppermute | solution.py:30
  937.0 51.6 %collective-permute-done.43 = bf16[2,32,3072]{2,1,0:T(8,128)(2,1)S(1)} collective-permute-done((bf16[2,32,3072]{2,1,0:T(8,128)(2,1)S(1)}, bf16[2,32,3072]{2,1,0:T(8,128)(2,1)S(1)}, u32[]{:S(2)}, u32[]{:S(2)}) %collective-permute-start.43) | collective-permute-done | bytes 393248 | tf_op jit(solution)/shard_map/ppermute | solution.py:30
  996.5 55.1 %collective-permute-done.38 = bf16[2,32,3200]{2,1,0:T(8,128)(2,1)S(1)} collective-permute-done((bf16[2,32,3200]{2,1,0:T(8,128)(2,1)S(1)}, bf16[2,32,3200]{2,1,0:T(8,128)(2,1)S(1)}, u32[]{:S(2)}, u32[]{:S(2)}) %collective-permute-start.38) | collective-permute-done | bytes 409632 | tf_op jit(solution)/shard_map/ppermute | solution.py:30
  1084.5 33.0 %collective-permute-start.58 = (bf16[2,128,1024]{2,1,0:T(8,128)(2,1)S(1)}, bf16[2,128,1024]{2,1,0:T(8,128)(2,1)S(1)}, u32[]{:S(2)}, u32[]{:S(2)}) collective-permute-start(bf16[2,128,1024]{2,1,0:T(8,128)(2,1)S(1)} %slice.887), channel_id=1, source_target_pairs={{0,8},{1,9},{2,10},{3,11},{4,12},{5,13},{6,14},{7,15},{8,0},{9,1},... | collective-permute-start | bytes 1572872 | tf_op jit(solution)/shard_map/ppermute | solution.py:30
  1156.3 25.3 %collective-permute-done.47 = bf16[4,32,5120]{2,1,0:T(8,128)(2,1)S(1)} collective-permute-done((bf16[4,32,5120]{2,1,0:T(8,128)(2,1)S(1)}, bf16[4,32,5120]{2,1,0:T(8,128)(2,1)S(1)}, u32[]{:S(2)}, u32[]{:S(2)}) %collective-permute-start.47) | collective-permute-done | bytes 1310752 | tf_op jit(solution)/shard_map/ppermute | solution.py:30
  (786 shorter events, 638.8 us)
Async XLA Ops:
  68.8 73.4 %collective-permute-start.3 = (bf16[4,32,3200]{2,1,0:T(8,128)(2,1)S(1)}, bf16[4,32,3200]{2,1,0:T(8,128)(2,1)S(1)}, u32[]{:S(2)}, u32[]{:S(2)}) collective-permute-start(bf16[4,32,3200]{2,1,0:T(8,128)(2,1)S(1)} %pad_maximum_fusion.21), channel_id=1, source_target_pairs={{0,24},{1,25},{2,26},{3,27},{4,28},{5,29},{6,30},{7,31},{8,16},{9,... | collective-permute-start | bytes 2457608 | tf_op jit(solution)/shard_map/ppermute | solution.py:30
  80.1 63.7 %collective-permute-start.29 = (bf16[4,128,1024]{2,1,0:T(8,128)(2,1)S(1)}, bf16[4,128,1024]{2,1,0:T(8,128)(2,1)S(1)}, u32[]{:S(2)}, u32[]{:S(2)}) collective-permute-start(bf16[4,128,1024]{2,1,0:T(8,128)(2,1)S(1)} %pad_maximum_fusion.14), channel_id=1, source_target_pairs={{0,4},{1,5},{2,6},{3,7},{4,0},{5,1},{6,2},{7,3},{8,12},{9,13},{10,... | collective-permute-start | bytes 3145736 | tf_op jit(solution)/shard_map/ppermute | solution.py:30
  143.8 66.8 %collective-permute-start.4 = (bf16[8,32,3200]{2,1,0:T(8,128)(2,1)S(1)}, bf16[8,32,3200]{2,1,0:T(8,128)(2,1)S(1)}, u32[]{:S(2)}, u32[]{:S(2)}) collective-permute-start(bf16[8,32,3200]{2,1,0:T(8,128)(2,1)S(1)} %pad_maximum_fusion.9), channel_id=1, source_target_pairs={{0,8},{1,9},{2,10},{3,11},{4,12},{5,13},{6,14},{7,15},{8,0},{9,1},... | collective-permute-start | bytes 4915208 | tf_op jit(solution)/shard_map/ppermute | solution.py:30
  147.6 64.9 %collective-permute-start.30 = (bf16[8,128,1024]{2,1,0:T(8,128)(2,1)S(1)}, bf16[8,128,1024]{2,1,0:T(8,128)(2,1)S(1)}, u32[]{:S(2)}, u32[]{:S(2)}) collective-permute-start(bf16[8,128,1024]{2,1,0:T(8,128)(2,1)S(1)} %pad_maximum_fusion.8), channel_id=1, source_target_pairs={{0,1},{1,0},{2,3},{3,2},{4,5},{5,4},{6,7},{7,6},{8,9},{9,8},{10,11... | collective-permute-start | bytes 6291464 | tf_op jit(solution)/shard_map/ppermute | solution.py:30
  150.6 103.8 %collective-permute-start.15 = (bf16[8,128,1024]{2,1,0:T(8,128)(2,1)S(1)}, bf16[8,128,1024]{2,1,0:T(8,128)(2,1)S(1)}, u32[]{:S(2)}, u32[]{:S(2)}) collective-permute-start(bf16[8,128,1024]{2,1,0:T(8,128)(2,1)S(1)} %pad_maximum_fusion.7), channel_id=1, source_target_pairs={{0,1},{1,0},{2,3},{3,2},{4,5},{5,4},{6,7},{7,6},{8,9},{9,8},{10,11... | collective-permute-start | bytes 6291464 | tf_op jit(solution)/shard_map/ppermute | solution.py:30
  167.5 90.0 %collective-permute-start.25 = (bf16[8,32,5120]{2,1,0:T(8,128)(2,1)S(1)}, bf16[8,32,5120]{2,1,0:T(8,128)(2,1)S(1)}, u32[]{:S(2)}, u32[]{:S(2)}) collective-permute-start(bf16[8,32,5120]{2,1,0:T(8,128)(2,1)S(1)} %pad_maximum_fusion.4), channel_id=1, source_target_pairs={{0,4},{1,5},{2,6},{3,7},{4,0},{5,1},{6,2},{7,3},{8,12},{9,13},{10,... | collective-permute-start | bytes 7864328 | tf_op jit(solution)/shard_map/ppermute | solution.py:30
  179.6 90.6 %collective-permute-start.10 = (bf16[8,32,5120]{2,1,0:T(8,128)(2,1)S(1)}, bf16[8,32,5120]{2,1,0:T(8,128)(2,1)S(1)}, u32[]{:S(2)}, u32[]{:S(2)}) collective-permute-start(bf16[8,32,5120]{2,1,0:T(8,128)(2,1)S(1)} %pad_maximum_fusion.3), channel_id=1, source_target_pairs={{0,4},{1,5},{2,6},{3,7},{4,0},{5,1},{6,2},{7,3},{8,12},{9,13},{10,... | collective-permute-start | bytes 7864328 | tf_op jit(solution)/shard_map/ppermute | solution.py:30
  212.5 82.5 %collective-permute-start.5 = (bf16[16,32,3200]{2,1,0:T(8,128)(2,1)}, bf16[16,32,3200]{2,1,0:T(8,128)(2,1)}, u32[]{:S(2)}, u32[]{:S(2)}) collective-permute-start(bf16[16,32,3200]{2,1,0:T(8,128)(2,1)} %get-tuple-element.97), channel_id=1, source_target_pairs={{0,2},{1,3},{2,0},{3,1},{4,6},{5,7},{6,4},{7,5},{8,10},{9,11},{10,... | collective-permute-start | bytes 9830408 | tf_op jit(solution)/shard_map/ppermute | solution.py:30
  254.4 248.2 %collective-permute-start.33 = (bf16[1,160,1024]{2,1,0:T(8,128)(2,1)}, bf16[1,160,1024]{2,1,0:T(8,128)(2,1)}, u32[]{:S(2)}, u32[]{:S(2)}) collective-permute-start(bf16[1,160,1024]{2,1,0:T(8,128)(2,1)} %get-tuple-element.117), channel_id=1, source_target_pairs={{0,1},{1,0},{2,3},{3,2},{4,5},{5,4},{6,7},{7,6},{8,9},{9,8},{10,11... | collective-permute-start | bytes 983048 | tf_op jit(solution)/shard_map/ppermute | solution.py:30
  257.6 81.6 %collective-permute-start.31 = (bf16[16,128,1024]{2,1,0:T(8,128)(2,1)}, bf16[16,128,1024]{2,1,0:T(8,128)(2,1)}, u32[]{:S(2)}, u32[]{:S(2)}) collective-permute-start(bf16[16,128,1024]{2,1,0:T(8,128)(2,1)} %get-tuple-element.93), channel_id=1, source_target_pairs={{0,2},{1,3},{2,0},{3,1},{4,6},{5,7},{6,4},{7,5},{8,10},{9,11},{10,... | collective-permute-start | bytes 12582920 | tf_op jit(solution)/shard_map/ppermute | solution.py:30
  270.3 118.2 %collective-permute-start.26 = (bf16[16,32,5120]{2,1,0:T(8,128)(2,1)}, bf16[16,32,5120]{2,1,0:T(8,128)(2,1)}, u32[]{:S(2)}, u32[]{:S(2)}) collective-permute-start(bf16[16,32,5120]{2,1,0:T(8,128)(2,1)} %get-tuple-element.89), channel_id=1, source_target_pairs={{0,2},{1,3},{2,0},{3,1},{4,6},{5,7},{6,4},{7,5},{8,10},{9,11},{10,... | collective-permute-start | bytes 15728648 | tf_op jit(solution)/shard_map/ppermute | solution.py:30
  273.3 141.1 %collective-permute-start.11 = (bf16[16,32,5120]{2,1,0:T(8,128)(2,1)}, bf16[16,32,5120]{2,1,0:T(8,128)(2,1)}, u32[]{:S(2)}, u32[]{:S(2)}) collective-permute-start(bf16[16,32,5120]{2,1,0:T(8,128)(2,1)} %get-tuple-element.91), channel_id=1, source_target_pairs={{0,2},{1,3},{2,0},{3,1},{4,6},{5,7},{6,4},{7,5},{8,10},{9,11},{10,... | collective-permute-start | bytes 15728648 | tf_op jit(solution)/shard_map/ppermute | solution.py:30
  295.0 68.8 %collective-permute-start.16 = (bf16[16,128,1024]{2,1,0:T(8,128)(2,1)}, bf16[16,128,1024]{2,1,0:T(8,128)(2,1)}, u32[]{:S(2)}, u32[]{:S(2)}) collective-permute-start(bf16[16,128,1024]{2,1,0:T(8,128)(2,1)} %copy-done.83), channel_id=1, source_target_pairs={{0,2},{1,3},{2,0},{3,1},{4,6},{5,7},{6,4},{7,5},{8,10},{9,11},{10,... | collective-permute-start | bytes 12582920 | tf_op jit(solution)/shard_map/ppermute | solution.py:30
  655.5 173.8 %collective-permute-start.35 = (bf16[16,32,3200]{2,1,0:T(8,128)(2,1)}, bf16[16,32,3200]{2,1,0:T(8,128)(2,1)}, u32[]{:S(2)}, u32[]{:S(2)}) collective-permute-start(bf16[16,32,3200]{2,1,0:T(8,128)(2,1)} %slice.813), channel_id=1, source_target_pairs={{0,2},{1,3},{2,0},{3,1},{4,6},{5,7},{6,4},{7,5},{8,10},{9,11},{10,... | collective-permute-start | bytes 9830408 | tf_op jit(solution)/shard_map/ppermute | solution.py:30
  680.9 156.4 %collective-permute-start.55 = (bf16[16,128,1024]{2,1,0:T(8,128)(2,1)}, bf16[16,128,1024]{2,1,0:T(8,128)(2,1)}, u32[]{:S(2)}, u32[]{:S(2)}) collective-permute-start(bf16[16,128,1024]{2,1,0:T(8,128)(2,1)} %slice.881), channel_id=1, source_target_pairs={{0,2},{1,3},{2,0},{3,1},{4,6},{5,7},{6,4},{7,5},{8,10},{9,11},{10,... | collective-permute-start | bytes 12582920 | tf_op jit(solution)/shard_map/ppermute | solution.py:30
  713.8 130.9 %collective-permute-start.60 = (bf16[16,128,1024]{2,1,0:T(8,128)(2,1)}, bf16[16,128,1024]{2,1,0:T(8,128)(2,1)}, u32[]{:S(2)}, u32[]{:S(2)}) collective-permute-start(bf16[16,128,1024]{2,1,0:T(8,128)(2,1)} %slice.891), channel_id=1, source_target_pairs={{0,2},{1,3},{2,0},{3,1},{4,6},{5,7},{6,4},{7,5},{8,10},{9,11},{10,... | collective-permute-start | bytes 12582920 | tf_op jit(solution)/shard_map/ppermute | solution.py:30
  737.4 86.4 %collective-permute-start.40 = (bf16[16,32,3072]{2,1,0:T(8,128)(2,1)}, bf16[16,32,3072]{2,1,0:T(8,128)(2,1)}, u32[]{:S(2)}, u32[]{:S(2)}) collective-permute-start(bf16[16,32,3072]{2,1,0:T(8,128)(2,1)} %slice.833), channel_id=1, source_target_pairs={{0,2},{1,3},{2,0},{3,1},{4,6},{5,7},{6,4},{7,5},{8,10},{9,11},{10,... | collective-permute-start | bytes 9437192 | tf_op jit(solution)/shard_map/ppermute | solution.py:30
  821.8 82.9 %collective-permute-start.45 = (bf16[16,32,5120]{2,1,0:T(8,128)(2,1)}, bf16[16,32,5120]{2,1,0:T(8,128)(2,1)}, u32[]{:S(2)}, u32[]{:S(2)}) collective-permute-start(bf16[16,32,5120]{2,1,0:T(8,128)(2,1)} %slice.847), channel_id=1, source_target_pairs={{0,2},{1,3},{2,0},{3,1},{4,6},{5,7},{6,4},{7,5},{8,10},{9,11},{10,... | collective-permute-start | bytes 15728648 | tf_op jit(solution)/shard_map/ppermute | solution.py:30
  823.9 101.2 %collective-permute-start.50 = (bf16[16,32,5120]{2,1,0:T(8,128)(2,1)}, bf16[16,32,5120]{2,1,0:T(8,128)(2,1)}, u32[]{:S(2)}, u32[]{:S(2)}) collective-permute-start(bf16[16,32,5120]{2,1,0:T(8,128)(2,1)} %slice.858), channel_id=1, source_target_pairs={{0,2},{1,3},{2,0},{3,1},{4,6},{5,7},{6,4},{7,5},{8,10},{9,11},{10,... | collective-permute-start | bytes 15728648 | tf_op jit(solution)/shard_map/ppermute | solution.py:30
  844.7 207.6 %collective-permute-start.56 = (bf16[8,128,1024]{2,1,0:T(8,128)(2,1)}, bf16[8,128,1024]{2,1,0:T(8,128)(2,1)}, u32[]{:S(2)}, u32[]{:S(2)}) collective-permute-start(bf16[8,128,1024]{2,1,0:T(8,128)(2,1)} %slice.883), channel_id=1, source_target_pairs={{0,1},{1,0},{2,3},{3,2},{4,5},{5,4},{6,7},{7,6},{8,9},{9,8},{10,11... | collective-permute-start | bytes 6291464 | tf_op jit(solution)/shard_map/ppermute | solution.py:30
  866.8 189.9 %collective-permute-start.61 = (bf16[8,128,1024]{2,1,0:T(8,128)(2,1)}, bf16[8,128,1024]{2,1,0:T(8,128)(2,1)}, u32[]{:S(2)}, u32[]{:S(2)}) collective-permute-start(bf16[8,128,1024]{2,1,0:T(8,128)(2,1)} %slice.893), channel_id=1, source_target_pairs={{0,1},{1,0},{2,3},{3,2},{4,5},{5,4},{6,7},{7,6},{8,9},{9,8},{10,11... | collective-permute-start | bytes 6291464 | tf_op jit(solution)/shard_map/ppermute | solution.py:30
  904.7 84.5 %collective-permute-start.37 = (bf16[4,32,3200]{2,1,0:T(8,128)(2,1)}, bf16[4,32,3200]{2,1,0:T(8,128)(2,1)}, u32[]{:S(2)}, u32[]{:S(2)}) collective-permute-start(bf16[4,32,3200]{2,1,0:T(8,128)(2,1)} %slice.817), channel_id=1, source_target_pairs={{0,24},{1,25},{2,26},{3,27},{4,28},{5,29},{6,30},{7,31},{8,16},{9,... | collective-permute-start | bytes 2457608 | tf_op jit(solution)/shard_map/ppermute | solution.py:30
  923.2 224.1 %collective-permute-start.46 = (bf16[8,32,5120]{2,1,0:T(8,128)(2,1)}, bf16[8,32,5120]{2,1,0:T(8,128)(2,1)}, u32[]{:S(2)}, u32[]{:S(2)}) collective-permute-start(bf16[8,32,5120]{2,1,0:T(8,128)(2,1)} %slice.849), channel_id=1, source_target_pairs={{0,4},{1,5},{2,6},{3,7},{4,0},{5,1},{6,2},{7,3},{8,12},{9,13},{10,... | collective-permute-start | bytes 7864328 | tf_op jit(solution)/shard_map/ppermute | solution.py:30
  988.5 162.9 %collective-permute-start.51 = (bf16[8,32,5120]{2,1,0:T(8,128)(2,1)}, bf16[8,32,5120]{2,1,0:T(8,128)(2,1)}, u32[]{:S(2)}, u32[]{:S(2)}) collective-permute-start(bf16[8,32,5120]{2,1,0:T(8,128)(2,1)} %slice.860), channel_id=1, source_target_pairs={{0,4},{1,5},{2,6},{3,7},{4,0},{5,1},{6,2},{7,3},{8,12},{9,13},{10,... | collective-permute-start | bytes 7864328 | tf_op jit(solution)/shard_map/ppermute | solution.py:30
  (195 other events, 4515.1 us)

commit v2 on v1

v2 whole, which is shorter than its diff:
```python
import functools

import jax
import jax.numpy as jnp
from jax import lax
from jax.experimental import pallas as pl
from jax.experimental.pallas import tpu as pltpu
from jax.sharding import PartitionSpec as P

HEAD = 64
BUFFER = 64
LAYERS = 2
AXES = ("dp", "seq")
BLOCKS = 32
SIDE = 128

masked_score = -1e30
f32 = jnp.float32
bf16 = jnp.bfloat16
INV_SQRT2 = 0.7071067811865476
INV_SQRT2PI = 0.3989422804014327

VMEM = pl.BlockSpec(memory_space=pltpu.VMEM)
SMEM = pl.BlockSpec(memory_space=pltpu.SMEM)
ANY = pl.BlockSpec(memory_space=pl.ANY)
weight_now = [10]
VMEM_LIMIT = 58 * 1024 * 1024


def mm(a, b):
    return lax.dot_general(a, b, (((1,), (0,)), ((), ())), preferred_element_type=f32)


def mm_nt(a, b):
    return lax.dot_general(a, b, (((1,), (1,)), ((), ())), preferred_element_type=f32)


def mm_tn(a, b):
    return lax.dot_general(a, b, (((0,), (0,)), ((), ())), preferred_element_type=f32)


def centred(x):
    mean = jnp.mean(x, axis=-1, keepdims=True)
    c = x - mean
    r = lax.rsqrt(jnp.mean(c * c, axis=-1, keepdims=True) + 1e-06)
    return c * r, r


def norm_back(d, n, r, gain):
    e = d * gain
    mean_e = jnp.mean(e, axis=-1, keepdims=True)
    mean_en = jnp.mean(e * n, axis=-1, keepdims=True)
    return r * (e - mean_e - n * mean_en)


def columns_sum(v):
    return jnp.sum(v, axis=0, keepdims=True)


def fetch(colors, parts, me, dst, sem, start=0):
    stop = start + dst.shape[1]
    for first, width, table, at, per, base, fixed in colors:
        low, high = max(start, first), min(stop, first + width)
        if low >= high:
            continue
        rows = dst.shape[0] // len(table)
        for p, offset in enumerate(table):
            owner = p if fixed else me ^ offset
            to_rows = pl.ds(pl.multiple_of(owner * rows, rows), rows)
            cols = pl.ds(low - first, high - low)
            src = parts[at + p // per].at[p % per, pl.ds(base, rows), cols]
            to = dst.at[to_rows, pl.ds(low - start, high - low)]
            pltpu.make_async_copy(src, to, sem).start()


def arrived(dst, sem):
    pltpu.make_async_copy(dst, dst, sem).wait()


def spread(src, out, me, arrays, sem, start):
    first, _, table, at, per, base, fixed = out
    width = src.shape[1]
    rows = src.shape[0] // len(table)
    for p, offset in enumerate(table):
        owner = p if fixed else me ^ offset
        from_rows = pl.ds(pl.multiple_of(owner * rows, rows), rows)
        to = arrays[at + p // per].at[p % per, pl.ds(base, rows), pl.ds(start, width)]
        pltpu.make_async_copy(src.at[from_rows, :], to, sem).start()


def holds(outs, column):
    return [o for o in outs if o[0] <= column < o[0] + o[1]][0]


def attn_fwd_body(colors, many, me_ref, x_ref, flag_ref, gain_ref, shift_ref, bias_ref, *refs):
    parts, refs = refs[:many], refs[many:]
    normed_ref, qkv_ref, att_ref, lse_ref, w, sem = refs
    dim = x_ref.shape[1]
    fetch(colors, parts, me_ref[0], w, sem)
    n, _ = centred(x_ref[...].astype(f32))
    normed_ref[...] = (n * gain_ref[...] + shift_ref[...]).astype(bf16)
    arrived(w, sem)

    def project(c, carry):
        cols = pl.ds(pl.multiple_of(c * 512, 512), 512)
        qkv_ref[:, cols] = (mm(normed_ref[...], w[:, cols]) + bias_ref[:, cols]).astype(bf16)
        return carry

    lax.fori_loop(0, 3 * dim // 512, project, 0)
    allowed = flag_ref[...] > 0
    scale = HEAD ** (-0.5)

    def two_heads(hp, carry):
        base = pl.multiple_of(hp * 128, 128)
        q2 = qkv_ref[:, pl.ds(base, 128)]
        k2 = qkv_ref[:, pl.ds(pl.multiple_of(dim + hp * 128, 128), 128)]
        v2 = qkv_ref[:, pl.ds(pl.multiple_of(2 * dim + hp * 128, 128), 128)]
        outs = []
        for s in range(2):
            cut = slice(s * HEAD, (s + 1) * HEAD)
            score = jnp.where(allowed, mm_nt(k2[:, cut], q2[:, cut]) * scale, masked_score)
            top = jnp.max(score, axis=0, keepdims=True)
            e = jnp.exp(score - top)
            total = jnp.sum(e, axis=0, keepdims=True)
            probs = (e * (1.0 / total)).astype(bf16)
            lse_ref[pl.ds(2 * hp + s, 1), :] = top + jnp.log(total)
            outs.append(mm_tn(probs, v2[:, cut]))
        att_ref[:, pl.ds(base, 128)] = jnp.concatenate(outs, axis=1).astype(bf16)
        return carry

    lax.fori_loop(0, dim // 128, two_heads, 0)


def mlp_up_body(colors, many, me_ref, x_ref, att_ref, ob_ref, gain_ref, shift_ref, ub_ref, *refs):
    parts, refs = refs[:many], refs[many:]
    mid_ref, normed_ref, hidden_ref, slope_ref, w_out, w_up, sem = refs
    ff = ub_ref.shape[1]
    fetch(colors, parts, me_ref[0], w_out, sem.at[0], ff)
    fetch(colors, parts, me_ref[0], w_up, sem.at[1])
    arrived(w_out, sem.at[0])
    mid = x_ref[...].astype(f32) + mm(att_ref[...], w_out[...]) + ob_ref[...]
    mid_ref[...] = mid
    n, _ = centred(mid)
    normed_ref[...] = (n * gain_ref[...] + shift_ref[...]).astype(bf16)
    arrived(w_up, sem.at[1])

    def step(c, carry):
        cols = pl.ds(pl.multiple_of(c * 512, 512), 512)
        u = mm(normed_ref[...], w_up[:, cols]) + ub_ref[:, cols]
        phi = 0.5 + 0.5 * lax.erf(u * INV_SQRT2)
        hidden_ref[:, cols] = (u * phi).astype(bf16)
        slope_ref[:, cols] = phi + u * (INV_SQRT2PI * jnp.exp(-0.5 * u * u))
        return carry

    lax.fori_loop(0, ff // 512, step, 0)


def mlp_down_body(colors, many, last, me_ref, mid_ref, hidden_ref, db_ref, flag_ref, *refs):
    parts, refs = refs[:many], refs[many:]
    out_ref, w, sem = refs
    fetch(colors, parts, me_ref[0], w, sem)
    arrived(w, sem)
    for c in range(0, w.shape[1], 512):
        cols = slice(c, c + 512)
        y = mid_ref[:, cols] + mm(hidden_ref[...], w[:, cols]) + db_ref[:, cols]
        if last:
            y = (y * flag_ref[...]).astype(bf16)
        out_ref[:, cols] = y


def down_grad_body(outs, many, me_ref, grad_ref, hidden_ref, *refs):
    arrays, refs = refs[:many], refs[many:]
    low_ref, sum_ref, perm, tile, sem = refs
    me = me_ref[0]
    grad = grad_ref[...]
    low_ref[...] = grad.astype(bf16)
    sum_ref[...] = columns_sum(grad)
    group = 4
    ((first, width, table, at, per, base, fixed),) = outs
    rows = hidden_ref.shape[1] // len(table)
    for p, offset in enumerate(table):
        owner = pl.ds(pl.multiple_of((p if fixed else me ^ offset) * rows, rows), rows)
        perm[:, p * rows : (p + 1) * rows] = hidden_ref[:, owner]
    pending = [None, None]
    for g in reversed(range(len(table) // group)):
        slot = g % 2
        if pending[slot] is not None:
            pending[slot].wait()
        cut = slice(g * group * rows, (g + 1) * group * rows)
        block = mm_tn(perm[:, cut], low_ref[...])
        tile[slot] = block.astype(bf16).reshape(tile.shape[1:])
        b0 = g * group
        to = arrays[at + b0 // per].at[pl.ds(b0 % per, group), pl.ds(base, rows)]
        pending[slot] = pltpu.make_async_copy(tile.at[slot], to, sem.at[slot])
        pending[slot].start()
    for copy in pending:
        copy.wait()


def mlp_back_body(ups, downs, outs, many, me_ref, grad_ref, low_ref, slope_ref, mid_ref, *refs):
    normed_ref, att_ref, gain_ref, refs = refs[0], refs[1], refs[2], refs[3:]
    many_up, many_down, many_in, many_out = many
    up_parts, refs = refs[:many_up], refs[many_up:]
    down_parts, refs = refs[:many_down], refs[many_down:]
    refs = refs[many_in:]
    halves, refs = refs[:many_out], refs[many_out:]
    d_mid_ref, d_att_ref, g_up_ref, g_gain, g_shift, g_out, refs = (*refs[:6], refs[6:])
    w_down, w_up, w_out, turned, turned_att, d_low_ref, acc, tile, low_mid, sem, out_sem = refs
    me = me_ref[0]
    ff, dim = w_down.shape
    fetch(downs, down_parts, me, w_down, sem.at[0])
    fetch(ups, up_parts, me, w_up, sem.at[1])
    fetch(ups, up_parts, me, w_out, sem.at[2], ff)
    turned[...] = normed_ref[...].T
    turned_att[...] = att_ref[...].T
    acc[...] = jnp.zeros_like(acc)
    arrived(w_down, sem.at[0])

    def first_step(c, carry):
        cols = pl.ds(pl.multiple_of(c * 512, 512), 512)
        d_up = mm_nt(low_ref[...], w_down[cols, :]) * slope_ref[:, cols]
        g_up_ref[:, cols] = columns_sum(d_up)
        d_low_ref[:, cols] = d_up.astype(bf16)
        return carry

    lax.fori_loop(0, ff // 512, first_step, 0)
    arrived(w_up, sem.at[1])

    def flush(slot):
        pltpu.make_async_copy(tile.at[slot], tile.at[slot], out_sem.at[slot]).wait()

    for out in outs:
        first, width = out[:2]
        stop = min(first + width, ff)

        def step(c, carry, out=out, first=first):
            start = pl.multiple_of(c * 512, 512)
            cols = pl.ds(start, 512)
            slot = lax.rem(c, 2)

            @pl.when(c >= 2)
            def _():
                flush(slot)

            tile[slot] = mm(turned[...], d_low_ref[:, cols]).astype(bf16)
            local = pl.multiple_of(start - first, 512)
            spread(tile.at[slot], out, me, halves, out_sem.at[slot], local)
            acc[...] += mm_nt(d_low_ref[:, cols], w_up[:, cols])
            return carry

        lax.fori_loop(first // 512, stop // 512, step, 0)
    n, r = centred(mid_ref[...])
    d = acc[...]
    g_gain[...] = columns_sum(d * n)
    g_shift[...] = columns_sum(d)
    d_mid = grad_ref[...] + norm_back(d, n, r, gain_ref[...])
    d_mid_ref[...] = d_mid
    g_out[...] = columns_sum(d_mid)
    low_mid[...] = d_mid.astype(bf16)
    arrived(w_out, sem.at[2])
    for c in range(dim // 512):
        flush(c % 2)
        tile[c % 2] = mm(turned_att[...], low_mid[:, c * 512 : (c + 1) * 512]).astype(bf16)
        start = ff + c * 512
        out = holds(outs, start)
        spread(tile.at[c % 2], out, me, halves, out_sem.at[c % 2], start - out[0])
    d_att_ref[...] = mm_nt(low_mid[...], w_out[...]).astype(bf16)
    flush(0)
    flush(1)


def attn_back_body(colors, outs, counts, extra, me_ref, d_att_ref, qkv_ref, lse_ref, flag_ref, *refs):
    many, many_in, many_out = counts
    normed_ref, x_ref, d_mid_ref, gain_ref, refs = *refs[:4], refs[4:]
    if extra:
        others_ref, refs = refs[0], refs[1:]
    parts, refs = refs[:many], refs[many:]
    refs = refs[many_in:]
    halves, refs = refs[:many_out], refs[many_out:]
    d_x_ref, g_gain, g_shift, g_query, g_value, refs = (*refs[:5], refs[5:])
    if extra:
        w, d_qkv, turned, tile, sem, out_sem, column, wide = refs
    else:
        w, d_qkv, turned, tile, sem, out_sem = refs
    me = me_ref[0]
    dim = x_ref.shape[1]
    fetch(colors, parts, me, w, sem)
    turned[...] = normed_ref[...].T
    allowed = flag_ref[...] > 0
    scale = HEAD ** (-0.5)

    def two_heads(hp, carry):
        at_q = pl.ds(pl.multiple_of(hp * 128, 128), 128)
        at_k = pl.ds(pl.multiple_of(dim + hp * 128, 128), 128)
        at_v = pl.ds(pl.multiple_of(2 * dim + hp * 128, 128), 128)
        q2, k2, v2, d2 = qkv_ref[:, at_q], qkv_ref[:, at_k], qkv_ref[:, at_v], d_att_ref[:, at_q]
        dq, dk, dv = [], [], []
        for s in range(2):
            cut = slice(s * HEAD, (s + 1) * HEAD)
            q, k, v, d = q2[:, cut], k2[:, cut], v2[:, cut], d2[:, cut]
            score = jnp.where(allowed, mm_nt(k, q) * scale, masked_score)
            probs = jnp.exp(score - lse_ref[pl.ds(2 * hp + s, 1), :])
            dv.append(mm(probs.astype(bf16), d))
            d_probs = mm_nt(v, d)
            inner = jnp.sum(probs * d_probs, axis=0, keepdims=True)
            d_score = (probs * (d_probs - inner)).astype(bf16)
            dq.append(mm_tn(d_score, k) * scale)
            dk.append(mm(d_score, q) * scale)
        d_qkv[:, at_q] = jnp.concatenate(dq, axis=1).astype(bf16)
        d_qkv[:, at_k] = jnp.concatenate(dk, axis=1).astype(bf16)
        d_qkv[:, at_v] = jnp.concatenate(dv, axis=1).astype(bf16)
        return carry

    lax.fori_loop(0, dim // 128, two_heads, 0)

    def flush(slot):
        pltpu.make_async_copy(tile.at[slot], tile.at[slot], out_sem.at[slot]).wait()

    for c in range(3 * dim // 512):
        if c >= 2:
            flush(c % 2)
        tile[c % 2] = mm(turned[...], d_qkv[:, c * 512 : (c + 1) * 512]).astype(bf16)
        out = holds(outs, c * 512)
        spread(tile.at[c % 2], out, me, halves, out_sem.at[c % 2], c * 512 - out[0])
    g_query[...] = columns_sum(d_qkv[:, :dim].astype(f32))
    g_value[...] = columns_sum(d_qkv[:, 2 * dim :].astype(f32))
    arrived(w, sem)
    d = mm_nt(d_qkv[...], w[...])
    n, r = centred(x_ref[...].astype(f32))
    g_gain[...] = columns_sum(d * n)
    g_shift[...] = columns_sum(d)
    d_x_ref[...] = (d_mid_ref[...] + norm_back(d, n, r, gain_ref[...])).astype(d_x_ref.dtype)
    if extra:
        wide[...] = others_ref[...]
        for at, row in zip(extra, (g_gain, g_shift, g_query, g_value)):
            wide[at : at + 1, :] = row[...]
        column[...] = wide[...].T.astype(bf16)
        spread(column, outs[-1], me, halves, sem, 3 * dim - outs[-1][0])
        arrived(column, sem)
    flush(0)
    flush(1)


def shaped(shape, dtype=f32):
    return jax.ShapeDtypeStruct(shape, dtype)


def call(body, name, in_specs, out_shapes, out_specs, scratch, args, aliases=None):
    return pl.pallas_call(
        body,
        in_specs=in_specs,
        out_specs=out_specs,
        out_shape=out_shapes,
        scratch_shapes=scratch,
        input_output_aliases=aliases or {},
        compiler_params=pltpu.CompilerParams(vmem_limit_bytes=VMEM_LIMIT),
        cost_estimate=pl.CostEstimate(
            flops=10 ** weight_now[0], bytes_accessed=0, transcendentals=0
        ),
        name=name,
    )(*args)


def attn_fwd(me, x, flag, gain, shift, bias, weight):
    length, dim = x.shape
    colors, parts = weight
    return call(
        functools.partial(attn_fwd_body, colors, len(parts)),
        "attn_fwd",
        [SMEM] + [VMEM] * 5 + [ANY] * len(parts),
        (
            shaped((length, dim), bf16),
            shaped((length, 3 * dim), bf16),
            shaped((length, dim), bf16),
            shaped((dim // HEAD, length)),
        ),
        (VMEM,) * 4,
        [pltpu.VMEM((dim, 3 * dim), bf16), pltpu.SemaphoreType.DMA],
        (me, x, flag, gain, shift, bias, *parts),
    )


def mlp_up(me, x, att, out_bias, gain, shift, up_bias, weight):
    length, dim = x.shape
    ff = up_bias.shape[1]
    colors, parts = weight
    return call(
        functools.partial(mlp_up_body, colors, len(parts)),
        "mlp_up",
        [SMEM] + [VMEM] * 6 + [ANY] * len(parts),
        (
            shaped((length, dim)),
            shaped((length, dim), bf16),
            shaped((length, ff), bf16),
            shaped((length, ff)),
        ),
        (VMEM,) * 4,
        [
            pltpu.VMEM((dim, dim), bf16),
            pltpu.VMEM((dim, ff), bf16),
            pltpu.SemaphoreType.DMA((2,)),
        ],
        (me, x, att, out_bias, gain, shift, up_bias, *parts),
    )


def mlp_down(me, mid, hidden, down_bias, flag, weight, last):
    length, dim = mid.shape
    ff = hidden.shape[1]
    colors, parts = weight
    return call(
        functools.partial(mlp_down_body, colors, len(parts), last),
        "mlp_down",
        [SMEM] + [VMEM] * 4 + [ANY] * len(parts),
        shaped((length, dim), bf16 if last else f32),
        VMEM,
        [pltpu.VMEM((ff, dim), bf16), pltpu.SemaphoreType.DMA],
        (me, mid, hidden, down_bias, flag, *parts),
    )


def down_grad(me, grad, hidden, outs, shapes):
    length, dim = grad.shape
    ff = hidden.shape[1]
    return call(
        functools.partial(down_grad_body, outs, len(shapes)),
        "down_grad",
        [SMEM, VMEM, VMEM],
        (*shapes, shaped((length, dim), bf16), shaped((1, dim))),
        (ANY,) * len(shapes) + (VMEM, VMEM),
        [
            pltpu.VMEM((length, ff), bf16),
            pltpu.VMEM((2, 4, ff // BLOCKS, dim), bf16),
            pltpu.SemaphoreType.DMA((2,)),
        ],
        (me, grad, hidden),
    )


def mlp_back(me, grad, low, slope, mid, normed, att, gain, up_weight, down_weight, outs, shapes, old):
    length, dim = grad.shape
    ff = slope.shape[1]
    ups, up_parts = up_weight
    downs, down_parts = down_weight
    many = (len(up_parts), len(down_parts), len(old), len(shapes))
    row = shaped((1, dim))
    return call(
        functools.partial(mlp_back_body, ups, downs, outs, many),
        "mlp_back",
        [SMEM] + [VMEM] * 7 + [ANY] * (len(up_parts) + len(down_parts) + len(old)),
        (
            *shapes,
            shaped((length, dim)),
            shaped((length, dim), bf16),
            shaped((1, ff)),
            row,
            row,
            row,
        ),
        (ANY,) * len(shapes) + (VMEM,) * 6,
        [
            pltpu.VMEM((ff, dim), bf16),
            pltpu.VMEM((dim, ff), bf16),
            pltpu.VMEM((dim, dim), bf16),
            pltpu.VMEM((dim, length), bf16),
            pltpu.VMEM((dim, length), bf16),
            pltpu.VMEM((length, ff), bf16),
            pltpu.VMEM((length, dim), f32),
            pltpu.VMEM((2, dim, 512), bf16),
            pltpu.VMEM((length, dim), bf16),
            pltpu.SemaphoreType.DMA((3,)),
            pltpu.SemaphoreType.DMA((2,)),
        ],
        (me, grad, low, slope, mid, normed, att, gain, *up_parts, *down_parts, *old),
        {8 + len(up_parts) + len(down_parts): 0} if old else None,
    )


def attn_back(me, d_att, qkv, lse, flag, normed, x, d_mid, gain, weight, others, at, last, outs, shapes, old):
    length, dim = x.shape
    colors, parts = weight
    extra = () if others is None else tuple(at)
    counts = (len(parts), len(old), len(shapes))
    before = 10 if extra else 9
    row = shaped((1, dim))
    scratch = [
        pltpu.VMEM((dim, 3 * dim), bf16),
        pltpu.VMEM((length, 3 * dim), bf16),
        pltpu.VMEM((dim, length), bf16),
        pltpu.VMEM((2, dim, 512), bf16),
        pltpu.SemaphoreType.DMA,
        pltpu.SemaphoreType.DMA((2,)),
    ]
    if extra:
        scratch += [pltpu.VMEM((dim, SIDE), bf16), pltpu.VMEM((SIDE, dim), f32)]
    return call(
        functools.partial(attn_back_body, colors, outs, counts, extra),
        "attn_back",
        [SMEM] + [VMEM] * (before - 1) + [ANY] * (len(parts) + len(old)),
        (*shapes, shaped((length, dim), bf16 if last else f32), row, row, row, row),
        (ANY,) * len(shapes) + (VMEM,) * 5,
        scratch,
        (me, d_att, qkv, lse, flag, normed, x, d_mid, gain)
        + ((others,) if extra else ())
        + tuple(parts)
        + tuple(old),
        {before + len(parts): 0} if old else None,
    )


def pack_body(a_ref, b_ref, out_ref):
    half = a_ref.shape[0]

    def step(i, carry):
        out_ref[i] = a_ref[i]
        out_ref[half + i] = b_ref[i]
        return carry

    lax.fori_loop(0, half, step, 0)


def pack(a, b):
    shape = (a.shape[0] * 2, *a.shape[1:])
    return call(pack_body, "pack", [VMEM] * 2, shaped(shape, bf16), VMEM, [], (a, b))


def merge_body(keep_ref, got_ref, low_ref, high_ref):
    half = low_ref.shape[0]

    def step(i, carry):
        low_ref[i] = keep_ref[i] + got_ref[i]
        high_ref[i] = keep_ref[half + i] + got_ref[half + i]
        return carry

    lax.fori_loop(0, half, step, 0)


def merge(keep, got):
    half = shaped((keep.shape[0] // 2, *keep.shape[1:]), bf16)
    return call(
        merge_body, "merge", [VMEM] * 2, (half, half), (VMEM, VMEM), [], (keep, got)
    )


def exchange(value, mask, n):
    return lax.ppermute(value, AXES, [(i, i ^ mask) for i in range(n)])


PARTNER = 2
NAMED = dict(x=1, y=4, b=8, a=24)


def other_masks(n):
    bits = n.bit_length() - 1
    return [1 << k for k in range(bits - 1, 1, -1)] + [1]


def span_table(masks):
    table = [0]
    for m in masks:
        table = table + [t ^ m for t in table]
    return tuple(table)


def owners_of(masks, me):
    return me ^ jnp.asarray(span_table(masks), jnp.int32)


def positions_of(masks, me):
    table = span_table(masks)
    inverse = [0] * len(table)
    for p, t in enumerate(table):
        inverse[t] = p
    return jnp.asarray(inverse, jnp.int32)[me ^ jnp.arange(len(table), dtype=jnp.int32)]


class Plan:
    def __init__(self, tied):
        self.actions = {}
        self.tied = tied
        self.last = None

    def ended(self, holder, key):
        self.last = (holder, key)

    def tie(self, value):
        if not self.tied or self.last is None:
            return value
        holder, key = self.last
        value, holder[key] = lax.optimization_barrier((value, holder[key]))
        return value

    def add(self, name, action):
        self.actions[name] = action

    def run(self, order):
        left = dict(self.actions)
        for name in order:
            weight_now[0] = PLACES.get(name, PLACE)
            left.pop(name)()
        assert not left, sorted(left)


def plan_gather(plan, name, own, masks, me, n, ready):
    state = dict(held=own[None])
    last = len(masks) - 1

    def start(k):
        state["got"] = exchange(plan.tie(state["held"]), masks[k], n)

    def finish(k):
        got = plan.tie(state["got"])
        if k < last:
            state["held"] = pack(state["held"], got)
            plan.ended(state, "held")
        else:
            state["end"] = got
            plan.ended(state, "end")

    def cross(k):
        state[k] = exchange(plan.tie(state["held" if k == 1 else "end"]), PARTNER, n)

    def crossed(k):
        state[k] = plan.tie(state[k])
        plan.ended(state, k)
        if k == 2:
            whole = masks + [PARTNER]
            parts = [state["held"], state["end"], state[1], state[2]]
            if n == BLOCKS:
                ready(span_table(whole), parts)
                plan.ended(parts, 3)
            else:
                joined = jnp.concatenate(parts, axis=0)[positions_of(whole, me)]
                joined = joined.reshape(4, BLOCKS // 4, -1, own.shape[1])
                ready(tuple(range(BLOCKS)), list(joined))

    for k in range(len(masks)):
        plan.add(name + k, functools.partial(start, k))
        plan.add(name + k + ENDS, functools.partial(finish, k))
    for k in (1, 2):
        plan.add(name + 19 + k, functools.partial(cross, k))
        plan.add(name + 19 + k + ENDS, functools.partial(crossed, k))


def plan_scatter(plan, name, given, masks, me, n, ready):
    state = {}

    def start(k):
        if k < 0:
            keep, send = given()
            if n != BLOCKS:
                whole = jnp.concatenate([keep, send], axis=0).reshape(n, -1, keep.shape[2])
                whole = whole[owners_of(masks[::-1] + [PARTNER], me)]
                keep, send = whole[: n // 2], whole[n // 2 :]
            state["keep"], state["send"] = keep, send
        mask = PARTNER if k < 0 else masks[k]
        state["got"] = exchange(plan.tie(state["send"]), mask, n)

    def finish(k):
        keep, got = state["keep"], plan.tie(state["got"])
        if k == len(masks) - 1:
            ready((keep.astype(f32) + got.astype(f32))[0])
            return
        state["keep"], state["send"] = merge(keep, got)
        plan.ended(state, "keep")

    for k in range(-1, len(masks)):
        plan.add(name + k + 1, functools.partial(start, k))
        plan.add(name + k + 1 + ENDS, functools.partial(finish, k))


WEIGHTS = ("qkv", "up", "down")
ENDS = 50
OUTWARD = 1000
TOKENS, COTANGENT, OUTPUT, INPUT_GRAD = 2000, 2001, 2002, 2003
GATHERED, SCATTERED = 2010, 2020
KERNELS = 3000


def number(w, l):
    return 100 * (2 * WEIGHTS.index(w) + l)


def plain_order(plan):
    def stage(a):
        if a >= KERNELS:
            return (1, LAYERS * (a - KERNELS >= 30), -(a % 10) if a >= KERNELS + 30 else a % 10, a)
        late = OUTWARD <= a < TOKENS or a % ENDS >= 2 and a >= TOKENS
        return (2 if late else 0, 0, 0, 0)

    return sorted(plan.actions, key=stage)


def per_device(
    n_devices,
    tokens,
    keep,
    norm_gain,
    norm_bias,
    qkv_weight,
    qv_bias,
    out_weight,
    out_bias,
    up_weight,
    up_bias,
    down_weight,
    down_bias,
    cotangent,
):
    n = n_devices
    seq_at = lax.axis_index("seq")
    me = lax.axis_index("dp") * 2 + seq_at
    n_images, local_len, model_dim = tokens.shape
    half_images = n_images // 2
    width = norm_gain.shape[2]
    ratio = up_bias.shape[1] // width
    hidden_dim = up_bias.shape[1] * n
    exact = n == BLOCKS
    who = (me if exact else jnp.zeros_like(me)).reshape(1)
    images = range(half_images)
    plan = Plan(exact and half_images == 1)

    positions = seq_at * local_len + lax.iota(jnp.int32, local_len)
    key_keep = ((keep == 1) | (positions < BUFFER)[None, :]).astype(bf16)

    def halves(value):
        low, high = value[:half_images], value[half_images:]
        mine = jnp.where(seq_at == 0, low, high)
        other = jnp.where(seq_at == 0, high, low)
        return mine, other

    def joined(mine, other):
        return jnp.where(
            seq_at == 0,
            jnp.concatenate([mine, other], axis=0),
            jnp.concatenate([other, mine], axis=0),
        )

    tok_mine, tok_other = halves(tokens)
    cot_mine, cot_other = halves(cotangent)
    keep_mine, keep_other = halves(key_keep)
    box = {}

    def start_tokens():
        below = ((0, 0), (0, 7), (0, model_dim - local_len))
        flags = jnp.pad(keep_other[:, None, :], below)
        sent = jnp.concatenate([tok_other, flags], axis=1)
        box["sent"] = exchange(plan.tie(sent), 1, n)

    def finish_tokens():
        got = plan.tie(box["sent"])
        box["tok"] = jnp.concatenate([tok_mine, got[:, :local_len]], axis=1)
        flags = jnp.concatenate([keep_mine, got[:, local_len, :local_len]], axis=1)
        box["keep"] = flags.astype(f32)[:, :, None]
        plan.ended(box, "tok")

    def start_cotangent():
        box["cot"] = exchange(plan.tie(cot_other), 1, n)

    def finish_cotangent():
        box["cot"] = jnp.concatenate([cot_mine, plan.tie(box["cot"])], axis=1)
        plan.ended(box, "cot")

    plan.add(TOKENS, start_tokens)
    plan.add(TOKENS + ENDS, finish_tokens)
    plan.add(COTANGENT, start_cotangent)
    plan.add(COTANGENT + ENDS, finish_cotangent)

    def columns(l):
        return [norm_gain[l, 0], norm_gain[l, 1], norm_bias[l, 0], norm_bias[l, 1]] + [
            qv_bias[l, 0],
            qv_bias[l, 1],
            out_bias[l],
            down_bias[l],
        ] + [up_bias[l, q * width : (q + 1) * width] for q in range(ratio)]

    stacked = jnp.stack(sum([columns(l) for l in range(LAYERS)], []))
    per_layer = stacked.shape[0] // LAYERS
    stacked = jnp.pad(stacked, ((0, SIDE - stacked.shape[0]), (0, 0))).T

    def ways(table, key):
        return [[NAMED[c] for c in way] for way in table[key]] if exact else [other_masks(n)]

    weights = {}
    packed = [exact and l == LAYERS - 1 for l in range(LAYERS)]
    chunks = dict(qkv=(0, 3), out=(3, 1), up=(4, ratio))
    tall = width * (4 + ratio)

    def receive(key, size, table, parts):
        weights[key] = (((0, size, table, 0, parts[0].shape[0], 0, not exact),), parts)

    def packed_colors(name, start=0):
        at, count = chunks[name]
        same = tuple(range(BLOCKS))
        return tuple(
            (start + c * model_dim, model_dim, same, 0, BLOCKS, width * (at + c), True)
            for c in range(count)
        )

    packed_kinds = dict(
        qkv=packed_colors("qkv"),
        up=packed_colors("up") + packed_colors("out", hidden_dim),
        down=((0, model_dim, tuple(range(BLOCKS)), 0, BLOCKS, tall, True),),
    )

    def start_packed(l):
        def rows(value):
            return value.reshape(width, -1, model_dim).swapaxes(0, 1).reshape(-1, model_dim)

        own = [rows(qkv_weight[l]), out_weight[l], rows(up_weight[l]), down_weight[l]]
        own = plan.tie(jnp.concatenate(own, axis=0))
        whole = lax.all_gather(own, AXES, axis=0, tiled=False)
        for w in WEIGHTS:
            weights[w + str(l)] = (packed_kinds[w], [whole])

    for l in range(LAYERS):
        if packed[l]:
            plan.add(GATHERED + l, functools.partial(start_packed, l))
            continue
        for w in WEIGHTS:
            key = w + str(l)
            if w == "qkv":
                own = qkv_weight[l]
                if l == 0:
                    own = jnp.concatenate([own, stacked], axis=1)
            elif w == "up":
                own = jnp.concatenate([up_weight[l], out_weight[l]], axis=1)
            else:
                own = down_weight[l]
            masks = ways(GATHER, key)[0]
            got = functools.partial(receive, key, own.shape[1])
            plan_gather(plan, number(w, l), own, masks, me, n, got)

    vectors = []

    def read_vectors():
        parts = weights["qkv0"][1]
        side = jnp.concatenate([part[:, :, 3 * model_dim :] for part in parts], axis=0)
        if exact:
            side = side[positions_of(ways(GATHER, "qkv0")[0] + [PARTNER], me)]
        side = side.reshape(model_dim, SIDE).T.astype(f32)
        for l in range(LAYERS):
            rows = side[l * per_layer : (l + 1) * per_layer]
            up_shift = rows[8:].reshape(ratio, n, width).transpose(1, 0, 2).reshape(1, -1)
            no_bias = jnp.zeros((1, model_dim), f32)
            vectors.append(
                dict(
                    gain=(rows[0:1], rows[1:2]),
                    shift=(rows[2:3], rows[3:4]),
                    qkv=jnp.concatenate([rows[4:5], no_bias, rows[5:6]], axis=1),
                    out=rows[6:7],
                    down=rows[7:8],
                    up=up_shift,
                )
            )

    saved = [[None] * LAYERS for _ in images]
    grads = {}
    vector_rows = [[None] * LAYERS for _ in images]
    outs, shapes = {}, {}
    for l in range(LAYERS):
        for w in WEIGHTS:
            key = w + str(l)
            if packed[l] and w != "down":
                outs[key] = packed_kinds[w]
                shapes[key] = [shaped((BLOCKS, tall + width, model_dim), bf16)]
                continue
            total = {"qkv": 3 * model_dim, "up": hidden_dim + model_dim, "down": model_dim}[w]
            total += SIDE if (w, l) == ("qkv", 0) else 0
            masks = ways(SCATTER, key)[0]
            table = span_table(masks[::-1] + [PARTNER]) if exact else tuple(range(BLOCKS))
            rows = (hidden_dim if w == "down" else model_dim) // BLOCKS
            outs[key] = ((0, total, table, 0, BLOCKS // 2, 0, not exact),)
            shapes[key] = [shaped((BLOCKS // 2, rows, total), bf16)] * 2

    def old_of(l, i):
        return [saved[i][l]["packed"]] if packed[l] and "packed" in saved[i][l] else []

    def gave(key, values, l, i):
        if packed[l] and len(values) == 1:
            saved[i][l]["packed"] = values[0]
            return
        grads[key] = values if key not in grads else [a + b for a, b in zip(grads[key], values)]

    def forward_one(l):
        if not vectors:
            read_vectors()
        v = vectors[l]
        for i in images:
            s = saved[i][l] = {}
            s["x"] = box["tok"][i] if l == 0 else saved[i][l - 1]["next"]
            s["normed"], s["qkv"], s["att"], s["lse"] = attn_fwd(
                plan.tie(who),
                s["x"],
                box["keep"][i],
                v["gain"][0],
                v["shift"][0],
                v["qkv"],
                weights["qkv" + str(l)],
            )
            plan.ended(s, "lse")

    def forward_two(l):
        v = vectors[l]
        for i in images:
            s = saved[i][l]
            s["mid"], s["normed_two"], s["hidden"], s["slope"] = mlp_up(
                plan.tie(who),
                s["x"],
                s["att"],
                v["out"],
                v["gain"][1],
                v["shift"][1],
                v["up"],
                weights["up" + str(l)],
            )
            plan.ended(s, "normed_two")

    def forward_three(l):
        for i in images:
            s = saved[i][l]
            s["next"] = mlp_down(
                plan.tie(who),
                s["mid"],
                s["hidden"],
                vectors[l]["down"],
                box["keep"][i],
                weights["down" + str(l)],
                l == LAYERS - 1,
            )
            plan.ended(s, "next")

    def back_one(l):
        for i in images:
            s = saved[i][l]
            if l == LAYERS - 1:
                s["grad"] = box["cot"][i].astype(f32) * box["keep"][i]
            else:
                s["grad"] = saved[i][l + 1]["d_x"]
            key = "down" + str(l)
            *values, s["low"], s["g_down"] = down_grad(
                plan.tie(who), s["grad"], s["hidden"], outs[key], shapes[key]
            )
            plan.ended(s, "low")
            gave(key, values, l, i)

    def back_two(l):
        for i in images:
            s = saved[i][l]
            key = "up" + str(l)
            *values, s["d_mid"], s["d_att"], g_up, g_gain, g_shift, g_out = mlp_back(
                plan.tie(who),
                s["grad"],
                s["low"],
                s["slope"],
                s["mid"],
                s["normed_two"],
                s["att"],
                vectors[l]["gain"][1],
                weights[key],
                weights["down" + str(l)],
                outs[key],
                shapes[key],
                old_of(l, i),
            )
            plan.ended(s, "d_mid")
            gave(key, values, l, i)
            up_rows = g_up.reshape(n, ratio, width).transpose(1, 0, 2).reshape(ratio, -1)
            blank = jnp.zeros_like(g_gain)
            vector_rows[i][l] = [blank, g_gain, blank, g_shift, blank, blank, g_out, s["g_down"]]
            vector_rows[i][l].append(up_rows)

    def back_three(l):
        for i in images:
            s = saved[i][l]
            others = None
            if l == 0:
                others = jnp.concatenate(sum(vector_rows[i], []), axis=0)
                others = jnp.pad(others, ((0, SIDE - others.shape[0]), (0, 0)))
            key = "qkv" + str(l)
            *values, s["d_x"], g_gain, g_shift, g_q, g_v = attn_back(
                plan.tie(who),
                s["d_att"],
                s["qkv"],
                s["lse"],
                box["keep"][i],
                s["normed"],
                s["x"],
                s["d_mid"],
                vectors[l]["gain"][0],
                weights[key],
                others,
                (0, 2, 4, 5),
                l == 0,
                outs[key],
                shapes[key],
                old_of(l, i),
            )
            plan.ended(s, "d_x")
            gave(key, values, l, i)
            rows = vector_rows[i][l]
            rows[0], rows[2], rows[4], rows[5] = g_gain, g_shift, g_q, g_v

    for l in range(LAYERS):
        steps = (forward_one, forward_two, forward_three, back_one, back_two, back_three)
        for at, step in enumerate(steps):
            plan.add(KERNELS + 10 * at + l, functools.partial(step, l))

    def start_back(name, key, l):
        whole = jnp.stack([saved[i][l][key] for i in images])
        box["mine" + name] = whole[:, :local_len]
        box[name] = exchange(plan.tie(whole[:, local_len:]), 1, n)

    def finish_back(name):
        box[name] = joined(box["mine" + name], plan.tie(box[name]))
        plan.ended(box, name)

    plan.add(OUTPUT, functools.partial(start_back, "out", "next", LAYERS - 1))
    plan.add(OUTPUT + ENDS, functools.partial(finish_back, "out"))
    plan.add(INPUT_GRAD, functools.partial(start_back, "dx", "d_x", 0))
    plan.add(INPUT_GRAD + ENDS, functools.partial(finish_back, "dx"))

    results = {}

    def take(key):
        return grads[key]

    def final(key, value):
        results[key] = value
        plan.ended(results, key)

    def start_scatter(l):
        whole = sum(saved[i][l]["packed"] for i in images[1:]) if len(images) > 1 else None
        whole = saved[0][l]["packed"] if whole is None else whole + saved[0][l]["packed"]
        whole = whole.reshape(-1, model_dim)
        got = lax.psum_scatter(whole, AXES, scatter_dimension=0, tiled=True).astype(f32)

        def wide(name):
            at, count = chunks[name]
            part = got[width * at : width * (at + count)]
            return part.reshape(count, width, model_dim).swapaxes(0, 1).reshape(width, -1)

        results["qkv" + str(l)] = wide("qkv")
        results["up" + str(l)] = jnp.concatenate([wide("up"), wide("out")], axis=1)

    for l in reversed(range(LAYERS)):
        if packed[l]:
            plan.add(SCATTERED + l, functools.partial(start_scatter, l))
        for w in ("down",) if packed[l] else ("down", "up", "qkv"):
            key = w + str(l)
            given = functools.partial(take, key)
            name = OUTWARD + number(w, l)
            masks = ways(SCATTER, key)[0]
            plan_scatter(plan, name, given, masks, me, n, functools.partial(final, key))

    plan.run(ORDER if plan.tied else plain_order(plan))

    g_qkv, g_up, g_down = ([results[w + str(l)] for l in range(LAYERS)] for w in WEIGHTS)
    vector_out = g_qkv[0][:, 3 * model_dim :].T

    def pick(at):
        return jnp.stack([vector_out[l * per_layer + at] for l in range(LAYERS)])

    return (
        box["out"],
        box["dx"].astype(f32),
        jnp.stack([pick(0), pick(1)], axis=1),
        jnp.stack([pick(2), pick(3)], axis=1),
        jnp.stack([g[:, : 3 * model_dim] for g in g_qkv]),
        jnp.stack([pick(4), pick(5)], axis=1),
        jnp.stack([g[:, hidden_dim:] for g in g_up]),
        pick(6),
        jnp.stack([g[:, :hidden_dim] for g in g_up]),
        jnp.concatenate([pick(8 + q) for q in range(ratio)], axis=1),
        jnp.stack(g_down),
        pick(7),
    )


GATHER = dict(
    up0=("abyx",),
    down0=("xaby",),
    qkv0=("byxa",),
)
SCATTER = dict(
    up0=("bxya",),
    down0=("yxba",),
    qkv0=("yxba",),
    down1=("xyab",),
)
PLACE = 10
PLACES = {3030: 9, 3040: 9, 3050: 9, 1550: 9, 1551: 9, 1552: 9, 1553: 9, 1554: 9, 1250: 9, 1251: 9, 1252: 9, 1253: 9, 1254: 9}
ORDER = (
    2011, 0, 200, 400, 2000, 2001, 50, 1, 250, 201, 450, 401, 2050, 2051, 51, 2, 251, 202, 451,
    402, 52, 3, 252, 203, 452, 403, 53, 21, 20, 220, 253, 221, 453, 421, 71, 420, 70, 3000, 270,
    271, 3010, 471, 470, 3020, 3001, 3011, 3031, 1500, 3041, 3051, 2021, 3030, 1400, 3040, 1200,
    1550, 1501, 1450, 1401, 1250, 1201, 3050, 2003, 1000, 3021, 1551, 1502, 1451, 1402, 1251,
    1202, 2053, 1050, 1001, 1552, 1503, 2002, 1452, 1403, 1252, 1203, 1051, 1002, 1553, 1504,
    2052, 1453, 1404, 1253, 1204, 1052, 1003, 1554, 1454, 1254, 1053, 1004, 1054,
)


def solution(mesh):
    n_devices = mesh.shape["dp"] * mesh.shape["seq"]
    rows = P(None, AXES, None)
    last = P(None, None, AXES)
    flat = P(None, AXES)
    batch = P("dp", "seq", None)

    def body(*args):
        return per_device(n_devices, *args)

    return jax.shard_map(
        body,
        mesh=mesh,
        in_specs=(
            batch,
            P("dp", "seq"),
            last,
            last,
            rows,
            last,
            rows,
            flat,
            rows,
            flat,
            rows,
            flat,
            batch,
        ),
        out_specs=(batch, batch, last, last, rows, last, rows, flat, rows, flat, rows, flat),
        check_vma=False,
    )
```

time: 1250 us -> 735 us (0.59); the launches traced: 1220 us -> 730 us
  matrix products: 190 us -> 0 us
  waiting for transfers between devices: 410 us -> 296 us
  local copies, waits for them, and re-layouts: 147 us -> 40.6 us
  other arithmetic: 110 us -> 15.6 us
  starting transfers between devices: 125 us -> 75 us
  Pallas kernels: 240 us -> 287 us
    dot_general x36 -> x0, matrix products: 190 us -> none  [the longest x2 35.4 us: layer_forward(): up_pre = jnp.dot(normed_two, w_up, preferred_element_type=f32) + up_shift]
    ppermute x65 -> x42, waiting for transfers between devices: 410 us -> 296 us  [exchange(): return lax.ppermute(value, AXES, [(i, i ^ mask) for i in range(n)])]
    convert_element_type x31 -> x5, other arithmetic: 63.7 us -> 2.14 us  [the longest x1 1.2 us: per_device(): box['dx'].astype(f32)]
    ppermute x65 -> x42, starting transfers between devices: 125 us -> 74.9 us  [exchange(): return lax.ppermute(value, AXES, [(i, i ^ mask) for i in range(n)])]
    pallas_call x12 -> x37, Pallas kernels: 240 us -> 287 us  [call(): pl.pallas_call(body, in_specs=in_specs, out_specs=out_specs, out_shape=ou...]
    concatenate x12 -> x3, local copies, waits for them, and re-layouts: 40.7 us -> 0.99 us  [the longest x2 0.83 us: back_three(): others = jnp.concatenate(sum(vector_rows[i], []), axis=0)]
    slice x49 -> x14, local copies, waits for them, and re-layouts: 47.9 us -> 10.1 us  [the longest x4 3.39 us: read_vectors(): part[:, :, 3 * model_dim:]]
    unnamed x332 -> x111, local copies, waits for them, and re-layouts: 35 us -> 16.1 us
  transfers between devices with their start and end apart: 65 -> 44, of which waited for: 26 -> 19; matrix products, arithmetic and copies ran while one was open for 25% -> 4% of each run, Pallas kernels for 18% -> 27%
where the time goes in v2:
time: 735 us; the launch traced here: 730 us
  waiting for transfers between devices  296 us (40%)
  Pallas kernels  287 us (39%)
  starting transfers between devices  75 us (10%)
  local copies, waits for them, and re-layouts  40.6 us (6%)
  other arithmetic  15.6 us (2%)
  between operations  15.3 us (2%)
    ppermute x42, waiting for transfers between devices, exchange(): return lax.ppermute(value, AXES, [(i, i ^ mask) for i in range(n)])  296 us
    pallas_call x37, Pallas kernels, call(): pl.pallas_call(body, in_specs=in_specs, out_specs=out_specs, out_shape=ou...  287 us
    ppermute x42, starting transfers between devices, exchange(): return lax.ppermute(value, AXES, [(i, i ^ mask) for i in range(n)])  74.9 us
    unnamed x111, local copies, waits for them, and re-layouts  16.1 us
  transfers between devices with their start and end apart: 44, of which 19 were waited for; matrix products, arithmetic and copies ran while one was open for 4% of the time, Pallas kernels for 27%

profile of v2, /device:TPU:0, one launch (start us, length us, event | category | flops | bytes accessed | tf_op | source)
XLA Modules:
  0.0 730.0 jit_solution(9822357325255900520)
XLA Ops:
  28.5 8.5 %collective-permute-done.1.b_ref = bf16[1,32,5120]{2,1,0:T(8,128)(2,1)S(1)} collective-permute-done((bf16[1,32,5120]{2,1,0:T(8,128)(2,1)S(1)}, bf16[1,32,5120]{2,1,0:T(8,128)(2,1)S(1)}, u32[]{:S(2)}, u32[]{:S(2)}) %collective-permute-start.1) | collective-permute-done | bytes 327712 | tf_op jit(solution)/shard_map/ppermute | solution.py:546
  42.3 9.5 %collective-permute-start.4 = (bf16[2,32,5120]{2,1,0:T(8,128)(2,1)S(1)}, bf16[2,32,5120]{2,1,0:T(8,128)(2,1)S(1)}, u32[]{:S(2)}, u32[]{:S(2)}) collective-permute-start(bf16[2,32,5120]{2,1,0:T(8,128)(2,1)S(1)} %copy-done.43), channel_id=1, source_target_pairs={{0,8},{1,9},{2,10},{3,11},{4,12},{5,13},{6,14},{7,15},{8,0},{9,1},... | collective-permute-start | bytes 1966088 | tf_op jit(solution)/shard_map/ppermute | solution.py:546
  61.5 28.5 %collective-permute-done.4.b_ref = bf16[2,32,5120]{2,1,0:T(8,128)(2,1)S(1)} collective-permute-done((bf16[2,32,5120]{2,1,0:T(8,128)(2,1)S(1)}, bf16[2,32,5120]{2,1,0:T(8,128)(2,1)S(1)}, u32[]{:S(2)}, u32[]{:S(2)}) %collective-permute-start.4) | collective-permute-done | bytes 655392 | tf_op jit(solution)/shard_map/ppermute | solution.py:546
  121.6 19.8 %collective-permute-done.11.b_ref = bf16[4,128,1024]{2,1,0:T(8,128)(2,1)S(1)} collective-permute-done((bf16[4,128,1024]{2,1,0:T(8,128)(2,1)}, bf16[4,128,1024]{2,1,0:T(8,128)(2,1)S(1)}, u32[]{:S(2)}, u32[]{:S(2)}) %collective-permute-start.11) | collective-permute-done | bytes 1048608 | tf_op jit(solution)/shard_map/ppermute | solution.py:546
  146.5 60.6 %collective-permute-done.12.refs_1_.refs_6_ = bf16[8,32,3200]{2,1,0:T(8,128)(2,1)} collective-permute-done((bf16[8,32,3200]{2,1,0:T(8,128)(2,1)}, bf16[8,32,3200]{2,1,0:T(8,128)(2,1)}, u32[]{:S(2)}, u32[]{:S(2)}) %collective-permute-start.12) | collective-permute-done | bytes 1638432 | tf_op jit(solution)/shard_map/ppermute | solution.py:546
  230.5 16.9 %attn_fwd.2 = (bf16[320,1024]{1,0:T(8,128)(2,1)}, bf16[320,3072]{1,0:T(8,128)(2,1)}, bf16[320,1024]{1,0:T(8,128)(2,1)}, f32[16,320]{1,0:T(8,128)}) custom-call(s32[1]{0:T(128)} %bitcast.me_ref, bf16[320,1024]{1,0:T(8,128)(2,1)} %bitcast.124, f32[320,1]{1,0:T(8,128)} %convert_element_type.70.flag_ref, f32[1,1024]{1,0:T(1,128)} %get-tuple-element.577.gain_ref.refs_3_, ...), custom_call_target="tpu_custom_call" | custom-call | flops 10000000000 | tf_op jit(solution)/shard_map/attn_fwd/pallas_call | solution.py:349
  247.5 14.3 %mlp_up.2 = (f32[320,1024]{1,0:T(8,128)}, bf16[320,1024]{1,0:T(8,128)(2,1)}, bf16[320,4096]{1,0:T(8,128)(2,1)}, f32[320,4096]{1,0:T(8,128)}) custom-call(s32[1]{0:T(128)} %bitcast.me_ref, bf16[320,1024]{1,0:T(8,128)(2,1)} %bitcast.125, bf16[320,1024]{1,0:T(8,128)(2,1)} %get-tuple-element.316.att_ref.refs_1_, f32[1,1024]{1,0:T(1,128)} %get-tuple-element.573.ob_ref, ...), custom_call_target="tpu_custom_call" | custom-call | flops 10000000000 | tf_op jit(solution)/shard_map/mlp_up/pallas_call | solution.py:349
  261.8 9.4 %mlp_down.2.x_ref.refs_1_ = f32[320,1024]{1,0:T(8,128)} custom-call(s32[1]{0:T(128)} %bitcast.me_ref, f32[320,1024]{1,0:T(8,128)} %get-tuple-element.320.mid_ref, bf16[320,4096]{1,0:T(8,128)(2,1)} %get-tuple-element.321.hidden_ref, f32[1,1024]{1,0:T(1,128)} %get-tuple-element.570.db_ref, f32[320,1]{1,0:T(8,128)} %convert_element_type.70.flag_ref, ...), custom_call_target="tpu_custom_call" | custom-call | flops 10000000000 | tf_op jit(solution)/shard_map/mlp_down/pallas_call | solution.py:349
  271.2 17.1 %attn_fwd.3 = (bf16[320,1024]{1,0:T(8,128)(2,1)}, bf16[320,3072]{1,0:T(8,128)(2,1)}, bf16[320,1024]{1,0:T(8,128)(2,1)}, f32[16,320]{1,0:T(8,128)}) custom-call(s32[1]{0:T(128)} %bitcast.me_ref, f32[320,1024]{1,0:T(8,128)} %mlp_down.2.x_ref.refs_1_, f32[320,1]{1,0:T(8,128)} %convert_element_type.70.flag_ref, f32[1,1024]{1,0:T(1,128)} %get-tuple-element.569.gain_ref.refs_3_, ...), custom_call_target="tpu_custom_call" | custom-call | flops 10000000000 | tf_op jit(solution)/shard_map/attn_fwd/pallas_call | solution.py:349
  288.4 14.6 %mlp_up.3 = (f32[320,1024]{1,0:T(8,128)}, bf16[320,1024]{1,0:T(8,128)(2,1)}, bf16[320,4096]{1,0:T(8,128)(2,1)}, f32[320,4096]{1,0:T(8,128)}) custom-call(s32[1]{0:T(128)} %bitcast.me_ref, f32[320,1024]{1,0:T(8,128)} %mlp_down.2.x_ref.refs_1_, bf16[320,1024]{1,0:T(8,128)(2,1)} %get-tuple-element.331.att_ref.refs_1_, f32[1,1024]{1,0:T(1,128)} %get-tuple-element.565.ob_ref, ...), custom_call_target="tpu_custom_call" | custom-call | flops 10000000000 | tf_op jit(solution)/shard_map/mlp_up/pallas_call | solution.py:349
  302.9 11.4 %down_grad.2 = (bf16[16,128,1024]{2,1,0:T(8,128)(2,1)}, bf16[16,128,1024]{2,1,0:T(8,128)(2,1)}, bf16[320,1024]{1,0:T(8,128)(2,1)}, f32[1,1024]{1,0:T(1,128)}) custom-call(s32[1]{0:T(128)} %bitcast.me_ref, f32[320,1024]{1,0:T(8,128)} %convert_multiply_fusion.grad_ref, bf16[320,4096]{1,0:T(8,128)(2,1)} %get-tuple-element.335.hidden_ref), custom_call_target="tpu_custom_call" | custom-call | flops 10000000000 | tf_op jit(solution)/shard_map/down_grad/pallas_call | solution.py:349
  314.4 24.7 %mlp_back.2 = (bf16[32,288,1024]{2,1,0:T(8,128)(2,1)}, f32[320,1024]{1,0:T(8,128)}, bf16[320,1024]{1,0:T(8,128)(2,1)}, f32[1,4096]{1,0:T(1,128)}, f32[1,1024]{1,...) custom-call(s32[1]{0:T(128)} %bitcast.me_ref, f32[320,1024]{1,0:T(8,128)} %convert_multiply_fusion.grad_ref, ...), custom_call_target="tpu_custom_call" | custom-call | flops 10000000000 | tf_op jit(solution)/shard_map/mlp_back/pallas_call | solution.py:349
  339.1 25.2 %attn_back.2 = (bf16[32,288,1024]{2,1,0:T(8,128)(2,1)}, f32[320,1024]{1,0:T(8,128)}, f32[1,1024]{1,0:T(1,128)}, f32[1,1024]{1,0:T(1,128)}, f32[1,1024]{1,0:T(1,128)}, /*index=5*/f32[1,1024]{1,0:T(1,128)}) custom-call(s32[1]{0:T(128)} %bitcast.me_ref, bf16[320,1024]{1,0:T(8,128)(2,1)} %get-tuple-element.346.d_att_ref, ...), custom_call_target="tpu_custom_call", output_to_operand_aliasing={{0}: (10, {})} | custom-call | flops 10000000000 | tf_op jit(solution)/shard_map/attn_back/pallas_call | solution.py:349
  364.3 11.4 %down_grad.3 = (bf16[16,128,1024]{2,1,0:T(8,128)(2,1)}, bf16[16,128,1024]{2,1,0:T(8,128)(2,1)}, bf16[320,1024]{1,0:T(8,128)(2,1)}, f32[1,1024]{1,0:T(1,128)}) custom-call(s32[1]{0:T(128)} %bitcast.me_ref, f32[320,1024]{1,0:T(8,128)} %get-tuple-element.352.grad_ref, bf16[320,4096]{1,0:T(8,128)(2,1)} %get-tuple-element.321.hidden_ref), custom_call_target="tpu_custom_call" | custom-call | flops 1000000000 | tf_op jit(solution)/shard_map/down_grad/pallas_call | solution.py:349
  375.8 25.0 %mlp_back.3 = (bf16[16,32,5120]{2,1,0:T(8,128)(2,1)}, bf16[16,32,5120]{2,1,0:T(8,128)(2,1)}, f32[320,1024]{1,0:T(8,128)}, bf16[320,1024]{1,0:T(8,128)(2,1)}, f32...) custom-call(s32[1]{0:T(128)} %bitcast.me_ref, ...), custom_call_target="tpu_custom_call" | custom-call | flops 1000000000 | tf_op jit(solution)/shard_map/mlp_back/pallas_call | solution.py:349
  406.3 11.3 %collective-permute-done.22.got_ref = bf16[16,128,1024]{2,1,0:T(8,128)(2,1)} collective-permute-done((bf16[16,128,1024]{2,1,0:T(8,128)(2,1)}, bf16[16,128,1024]{2,1,0:T(8,128)(2,1)}, u32[]{:S(2)}, u32[]{:S(2)}) %collective-permute-start.22) | collective-permute-done | bytes 4194336 | tf_op jit(solution)/shard_map/ppermute | solution.py:546
  439.8 25.5 %attn_back.3 = (bf16[16,32,3200]{2,1,0:T(8,128)(2,1)}, bf16[16,32,3200]{2,1,0:T(8,128)(2,1)}, bf16[320,1024]{1,0:T(8,128)(2,1)}, f32[1,1024]{1,0:T(1,128)}, f32[...) custom-call(s32[1]{0:T(128)} %bitcast.me_ref, bf16[320,1024]{1,0:T(8,128)(2,1)} %get-tuple-element.401.d_att_ref, ...), custom_call_target="tpu_custom_call" | custom-call | flops 1000000000 | tf_op jit(solution)/shard_map/attn_back/pallas_call | solution.py:349
  467.0 14.8 %collective-permute-start.23 = (bf16[8,32,5120]{2,1,0:T(8,128)(2,1)}, bf16[8,32,5120]{2,1,0:T(8,128)(2,1)S(1)}, u32[]{:S(2)}, u32[]{:S(2)}) collective-permute-start(bf16[8,32,5120]{2,1,0:T(8,128)(2,1)} %get-tuple-element.381), channel_id=1, source_target_pairs={{0,8},{1,9},{2,10},{3,11},{4,12},{5,13},{6,14},{7,15},{8,0},{9,1},... | collective-permute-start | bytes 7864328 | tf_op jit(solution)/shard_map/ppermute | solution.py:546
  481.7 9.7 %mlp_down.3 = bf16[320,1024]{1,0:T(8,128)(2,1)} custom-call(s32[1]{0:T(128)} %bitcast.me_ref, f32[320,1024]{1,0:T(8,128)} %get-tuple-element.342.mid_ref, bf16[320,4096]{1,0:T(8,128)(2,1)} %get-tuple-element.335.hidden_ref, f32[1,1024]{1,0:T(1,128)} %get-tuple-element.562.db_ref, f32[320,1]{1,0:T(8,128)} %convert_element_type.70.flag_ref, ...), custom_call_target="tpu_custom_call" | custom-call | flops 10000000000 | tf_op jit(solution)/shard_map/mlp_down/pallas_call | solution.py:349
  497.6 24.6 %collective-permute-done.24.got_ref = bf16[8,128,1024]{2,1,0:T(8,128)(2,1)} collective-permute-done((bf16[8,128,1024]{2,1,0:T(8,128)(2,1)}, bf16[8,128,1024]{2,1,0:T(8,128)(2,1)}, u32[]{:S(2)}, u32[]{:S(2)}) %collective-permute-start.24) | collective-permute-done | bytes 2097184 | tf_op jit(solution)/shard_map/ppermute | solution.py:546
  527.7 39.3 %collective-permute-done.23.got_ref = bf16[8,32,5120]{2,1,0:T(8,128)(2,1)S(1)} collective-permute-done((bf16[8,32,5120]{2,1,0:T(8,128)(2,1)}, bf16[8,32,5120]{2,1,0:T(8,128)(2,1)S(1)}, u32[]{:S(2)}, u32[]{:S(2)}) %collective-permute-start.23) | collective-permute-done | bytes 2621472 | tf_op jit(solution)/shard_map/ppermute | solution.py:546
  591.1 26.9 %collective-permute-done.34.got_ref = bf16[4,32,5120]{2,1,0:T(8,128)(2,1)S(1)} collective-permute-done((bf16[4,32,5120]{2,1,0:T(8,128)(2,1)S(1)}, bf16[4,32,5120]{2,1,0:T(8,128)(2,1)S(1)}, u32[]{:S(2)}, u32[]{:S(2)}) %collective-permute-start.34) | collective-permute-done | bytes 1310752 | tf_op jit(solution)/shard_map/ppermute | solution.py:546
  636.9 10.1 %collective-permute-done.37.got_ref = bf16[2,32,5120]{2,1,0:T(8,128)(2,1)S(1)} collective-permute-done((bf16[2,32,5120]{2,1,0:T(8,128)(2,1)}, bf16[2,32,5120]{2,1,0:T(8,128)(2,1)S(1)}, u32[]{:S(2)}, u32[]{:S(2)}) %collective-permute-start.37) | collective-permute-done | bytes 655392 | tf_op jit(solution)/shard_map/ppermute | solution.py:546
  660.8 8.6 %collective-permute-done.35 = bf16[1,128,1024]{2,1,0:T(8,128)(2,1)S(1)} collective-permute-done((bf16[1,128,1024]{2,1,0:T(8,128)(2,1)S(1)}, bf16[1,128,1024]{2,1,0:T(8,128)(2,1)S(1)}, u32[]{:S(2)}, u32[]{:S(2)}) %collective-permute-start.35) | collective-permute-done | bytes 262176 | tf_op jit(solution)/shard_map/ppermute | solution.py:546
  (366 shorter events, 246.8 us)
Async XLA Ops:
  7.2 264.0 %all-gather.3.cloned.1.call-start = ((), (), s32[]{:S(2)}) async-start(), calls=%async_computation.2 | async-start | bytes 25952256 | tf_op jit(solution)/shard_map/all_gather | solution.py:812
  12.1 705.6 %reduce-scatter.2.cloned.1.call-start = ((), (), s32[]{:S(2)}) async-start(), calls=%async_computation.1 | async-start | bytes 19464192 | tf_op jit(solution)/shard_map/reduce_scatter | solution.py:1036
  42.3 47.7 %collective-permute-start.4 = (bf16[2,32,5120]{2,1,0:T(8,128)(2,1)S(1)}, bf16[2,32,5120]{2,1,0:T(8,128)(2,1)S(1)}, u32[]{:S(2)}, u32[]{:S(2)}) collective-permute-start(bf16[2,32,5120]{2,1,0:T(8,128)(2,1)S(1)} %copy-done.43), channel_id=1, source_target_pairs={{0,8},{1,9},{2,10},{3,11},{4,12},{5,13},{6,14},{7,15},{8,0},{9,1},... | collective-permute-start | bytes 1966088 | tf_op jit(solution)/shard_map/ppermute | solution.py:546
  51.8 45.9 %collective-permute-start.3 = (bf16[2,128,1024]{2,1,0:T(8,128)(2,1)}, bf16[2,128,1024]{2,1,0:T(8,128)(2,1)S(1)}, u32[]{:S(2)}, u32[]{:S(2)}) collective-permute-start(bf16[2,128,1024]{2,1,0:T(8,128)(2,1)} %pack.11.a_ref), channel_id=1, source_target_pairs={{0,24},{1,25},{2,26},{3,27},{4,28},{5,29},{6,30},{7,31},{8,16},{9,... | collective-permute-start | bytes 1572872 | tf_op jit(solution)/shard_map/ppermute | solution.py:546
  60.0 41.7 %collective-permute-start.9 = (bf16[4,32,3200]{2,1,0:T(8,128)(2,1)}, bf16[4,32,3200]{2,1,0:T(8,128)(2,1)S(1)}, u32[]{:S(2)}, u32[]{:S(2)}) collective-permute-start(bf16[4,32,3200]{2,1,0:T(8,128)(2,1)} %pack.12.a_ref), channel_id=1, source_target_pairs={{0,1},{1,0},{2,3},{3,2},{4,5},{5,4},{6,7},{7,6},{8,9},{9,8},{10,11... | collective-permute-start | bytes 2457608 | tf_op jit(solution)/shard_map/ppermute | solution.py:546
  101.7 39.8 %collective-permute-start.11 = (bf16[4,128,1024]{2,1,0:T(8,128)(2,1)}, bf16[4,128,1024]{2,1,0:T(8,128)(2,1)S(1)}, u32[]{:S(2)}, u32[]{:S(2)}) collective-permute-start(bf16[4,128,1024]{2,1,0:T(8,128)(2,1)} %pack.14.a_ref), channel_id=1, source_target_pairs={{0,8},{1,9},{2,10},{3,11},{4,12},{5,13},{6,14},{7,15},{8,0},{9,1},... | collective-permute-start | bytes 3145736 | tf_op jit(solution)/shard_map/ppermute | solution.py:546
  105.2 101.9 %collective-permute-start.12 = (bf16[8,32,3200]{2,1,0:T(8,128)(2,1)}, bf16[8,32,3200]{2,1,0:T(8,128)(2,1)}, u32[]{:S(2)}, u32[]{:S(2)}) collective-permute-start(bf16[8,32,3200]{2,1,0:T(8,128)(2,1)} %pack.15.refs_0_.refs_5_), channel_id=1, source_target_pairs={{0,24},{1,25},{2,26},{3,27},{4,28},{5,29},{6,30},{7,31},{8,16},{9,... | collective-permute-start | bytes 4915208 | tf_op jit(solution)/shard_map/ppermute | solution.py:546
  120.1 88.4 %collective-permute-start.10 = (bf16[8,32,5120]{2,1,0:T(8,128)(2,1)}, bf16[8,32,5120]{2,1,0:T(8,128)(2,1)}, u32[]{:S(2)}, u32[]{:S(2)}) collective-permute-start(bf16[8,32,5120]{2,1,0:T(8,128)(2,1)} %pack.16.refs_0_.refs_3_), channel_id=1, source_target_pairs={{0,1},{1,0},{2,3},{3,2},{4,5},{5,4},{6,7},{7,6},{8,9},{9,8},{10,11... | collective-permute-start | bytes 7864328 | tf_op jit(solution)/shard_map/ppermute | solution.py:546
  145.4 76.1 %collective-permute-start.17 = (bf16[8,128,1024]{2,1,0:T(8,128)(2,1)}, bf16[8,128,1024]{2,1,0:T(8,128)(2,1)}, u32[]{:S(2)}, u32[]{:S(2)}) collective-permute-start(bf16[8,128,1024]{2,1,0:T(8,128)(2,1)} %pack.17.refs_0_.refs_7_), channel_id=1, source_target_pairs={{0,4},{1,5},{2,6},{3,7},{4,0},{5,1},{6,2},{7,3},{8,12},{9,13},{10,... | collective-permute-start | bytes 6291464 | tf_op jit(solution)/shard_map/ppermute | solution.py:546
  208.4 39.0 %collective-permute-start.14 = (bf16[8,32,5120]{2,1,0:T(8,128)(2,1)S(1)}, bf16[8,32,5120]{2,1,0:T(8,128)(2,1)}, u32[]{:S(2)}, u32[]{:S(2)}) collective-permute-start(bf16[8,32,5120]{2,1,0:T(8,128)(2,1)S(1)} %copy-done.3), channel_id=1, source_target_pairs={{0,2},{1,3},{2,0},{3,1},{4,6},{5,7},{6,4},{7,5},{8,10},{9,11},{10,... | collective-permute-start | bytes 7864328 | tf_op jit(solution)/shard_map/ppermute | solution.py:546
  208.5 38.9 %collective-permute-start.13 = (bf16[8,32,5120]{2,1,0:T(8,128)(2,1)}, bf16[8,32,5120]{2,1,0:T(8,128)(2,1)}, u32[]{:S(2)}, u32[]{:S(2)}) collective-permute-start(bf16[8,32,5120]{2,1,0:T(8,128)(2,1)} %collective-permute-done.10.refs_1_.refs_4_), channel_id=1, source_target_pairs={{0,2},{1,3},{2,0},{3,1},{4,6},{5,7},{6,4},{7,5},{8,10},{9,11},{10,... | collective-permute-start | bytes 7864328 | tf_op jit(solution)/shard_map/ppermute | solution.py:546
  226.6 35.2 %collective-permute-start.18 = (bf16[8,128,1024]{2,1,0:T(8,128)(2,1)}, bf16[8,128,1024]{2,1,0:T(8,128)(2,1)}, u32[]{:S(2)}, u32[]{:S(2)}) collective-permute-start(bf16[8,128,1024]{2,1,0:T(8,128)(2,1)} %pack.17.refs_0_.refs_7_), channel_id=1, source_target_pairs={{0,2},{1,3},{2,0},{3,1},{4,6},{5,7},{6,4},{7,5},{8,10},{9,11},{10,... | collective-permute-start | bytes 6291464 | tf_op jit(solution)/shard_map/ppermute | solution.py:546
  424.0 68.6 %collective-permute-start.25 = (bf16[8,128,1024]{2,1,0:T(8,128)(2,1)}, bf16[8,128,1024]{2,1,0:T(8,128)(2,1)S(1)}, u32[]{:S(2)}, u32[]{:S(2)}) collective-permute-start(bf16[8,128,1024]{2,1,0:T(8,128)(2,1)} %get-tuple-element.385), channel_id=1, source_target_pairs={{0,1},{1,0},{2,3},{3,2},{4,5},{5,4},{6,7},{7,6},{8,9},{9,8},{10,11... | collective-permute-start | bytes 6291464 | tf_op jit(solution)/shard_map/ppermute | solution.py:546
  465.4 107.6 %collective-permute-start.28 = (bf16[16,32,3200]{2,1,0:T(8,128)(2,1)}, bf16[16,32,3200]{2,1,0:T(8,128)(2,1)}, u32[]{:S(2)}, u32[]{:S(2)}) collective-permute-start(bf16[16,32,3200]{2,1,0:T(8,128)(2,1)} %get-tuple-element.421), channel_id=1, source_target_pairs={{0,2},{1,3},{2,0},{3,1},{4,6},{5,7},{6,4},{7,5},{8,10},{9,11},{10,... | collective-permute-start | bytes 9830408 | tf_op jit(solution)/shard_map/ppermute | solution.py:546
  465.4 56.8 %collective-permute-start.24 = (bf16[8,128,1024]{2,1,0:T(8,128)(2,1)}, bf16[8,128,1024]{2,1,0:T(8,128)(2,1)}, u32[]{:S(2)}, u32[]{:S(2)}) collective-permute-start(bf16[8,128,1024]{2,1,0:T(8,128)(2,1)} %get-tuple-element.383), channel_id=1, source_target_pairs={{0,4},{1,5},{2,6},{3,7},{4,0},{5,1},{6,2},{7,3},{8,12},{9,13},{10,... | collective-permute-start | bytes 6291464 | tf_op jit(solution)/shard_map/ppermute | solution.py:546
  467.0 100.0 %collective-permute-start.23 = (bf16[8,32,5120]{2,1,0:T(8,128)(2,1)}, bf16[8,32,5120]{2,1,0:T(8,128)(2,1)S(1)}, u32[]{:S(2)}, u32[]{:S(2)}) collective-permute-start(bf16[8,32,5120]{2,1,0:T(8,128)(2,1)} %get-tuple-element.381), channel_id=1, source_target_pairs={{0,8},{1,9},{2,10},{3,11},{4,12},{5,13},{6,14},{7,15},{8,0},{9,1},... | collective-permute-start | bytes 7864328 | tf_op jit(solution)/shard_map/ppermute | solution.py:546
  491.5 81.3 %collective-permute-start.29 = (bf16[1,160,1024]{2,1,0:T(8,128)(2,1)S(1)}, bf16[1,160,1024]{2,1,0:T(8,128)(2,1)S(1)}, u32[]{:S(2)}, u32[]{:S(2)}) collective-permute-start(bf16[1,160,1024]{2,1,0:T(8,128)(2,1)S(1)} %get-tuple-element.423), channel_id=1, source_target_pairs={{0,1},{1,0},{2,3},{3,2},{4,5},{5,4},{6,7},{7,6},{8,9},{9,8},{10,11... | collective-permute-start | bytes 983048 | tf_op jit(solution)/shard_map/ppermute | solution.py:546
  526.0 54.2 %collective-permute-start.27 = (bf16[4,128,1024]{2,1,0:T(8,128)(2,1)}, bf16[4,128,1024]{2,1,0:T(8,128)(2,1)}, u32[]{:S(2)}, u32[]{:S(2)}) collective-permute-start(bf16[4,128,1024]{2,1,0:T(8,128)(2,1)} %get-tuple-element.398), channel_id=1, source_target_pairs={{0,4},{1,5},{2,6},{3,7},{4,0},{5,1},{6,2},{7,3},{8,12},{9,13},{10,... | collective-permute-start | bytes 3145736 | tf_op jit(solution)/shard_map/ppermute | solution.py:546
  527.1 55.7 %collective-permute-start.26 = (bf16[4,128,1024]{2,1,0:T(8,128)(2,1)}, bf16[4,128,1024]{2,1,0:T(8,128)(2,1)}, u32[]{:S(2)}, u32[]{:S(2)}) collective-permute-start(bf16[4,128,1024]{2,1,0:T(8,128)(2,1)} %get-tuple-element.395), channel_id=1, source_target_pairs={{0,1},{1,0},{2,3},{3,2},{4,5},{5,4},{6,7},{7,6},{8,9},{9,8},{10,11... | collective-permute-start | bytes 3145736 | tf_op jit(solution)/shard_map/ppermute | solution.py:546
  578.1 48.5 %collective-permute-start.33 = (bf16[8,32,3200]{2,1,0:T(8,128)(2,1)}, bf16[8,32,3200]{2,1,0:T(8,128)(2,1)S(1)}, u32[]{:S(2)}, u32[]{:S(2)}) collective-permute-start(bf16[8,32,3200]{2,1,0:T(8,128)(2,1)} %get-tuple-element.447), channel_id=1, source_target_pairs={{0,4},{1,5},{2,6},{3,7},{4,0},{5,1},{6,2},{7,3},{8,12},{9,13},{10,... | collective-permute-start | bytes 4915208 | tf_op jit(solution)/shard_map/ppermute | solution.py:546
  579.6 38.5 %collective-permute-start.34 = (bf16[4,32,5120]{2,1,0:T(8,128)(2,1)S(1)}, bf16[4,32,5120]{2,1,0:T(8,128)(2,1)S(1)}, u32[]{:S(2)}, u32[]{:S(2)}) collective-permute-start(bf16[4,32,5120]{2,1,0:T(8,128)(2,1)S(1)} %copy-done.35), channel_id=1, source_target_pairs={{0,1},{1,0},{2,3},{3,2},{4,5},{5,4},{6,7},{7,6},{8,9},{9,8},{10,11... | collective-permute-start | bytes 3932168 | tf_op jit(solution)/shard_map/ppermute | solution.py:546
  585.5 45.7 %collective-permute-start.32 = (bf16[2,128,1024]{2,1,0:T(8,128)(2,1)}, bf16[2,128,1024]{2,1,0:T(8,128)(2,1)}, u32[]{:S(2)}, u32[]{:S(2)}) collective-permute-start(bf16[2,128,1024]{2,1,0:T(8,128)(2,1)} %get-tuple-element.445), channel_id=1, source_target_pairs={{0,24},{1,25},{2,26},{3,27},{4,28},{5,29},{6,30},{7,31},{8,16},{9,... | collective-permute-start | bytes 1572872 | tf_op jit(solution)/shard_map/ppermute | solution.py:546
  587.9 45.3 %collective-permute-start.31 = (bf16[1,160,1024]{2,1,0:T(8,128)(2,1)S(1)}, bf16[1,160,1024]{2,1,0:T(8,128)(2,1)S(1)}, u32[]{:S(2)}, u32[]{:S(2)}) collective-permute-start(bf16[1,160,1024]{2,1,0:T(8,128)(2,1)S(1)} %get-tuple-element.443), channel_id=1, source_target_pairs={{0,1},{1,0},{2,3},{3,2},{4,5},{5,4},{6,7},{7,6},{8,9},{9,8},{10,11... | collective-permute-start | bytes 983048 | tf_op jit(solution)/shard_map/ppermute | solution.py:546
  589.4 44.8 %collective-permute-start.30 = (bf16[2,128,1024]{2,1,0:T(8,128)(2,1)}, bf16[2,128,1024]{2,1,0:T(8,128)(2,1)}, u32[]{:S(2)}, u32[]{:S(2)}) collective-permute-start(bf16[2,128,1024]{2,1,0:T(8,128)(2,1)} %get-tuple-element.442), channel_id=1, source_target_pairs={{0,8},{1,9},{2,10},{3,11},{4,12},{5,13},{6,14},{7,15},{8,0},{9,1},... | collective-permute-start | bytes 1572872 | tf_op jit(solution)/shard_map/ppermute | solution.py:546
  (74 other events, 1161.4 us)
Sparse Core Ops, SparseCore 0:
  12.2 237.4 all-gather.2
  364.4 322.1 reduce-scatter.1

commit v3 on v2

--- a/solution.py
+++ b/solution.py
@@ -1083,13 +1083,13 @@
     qkv0=("byxa",),
 )
 SCATTER = dict(
-    up0=("bxya",),
+    up0=("xbay",),
     down0=("yxba",),
     qkv0=("yxba",),
-    down1=("xyab",),
+    down1=("byxa",),
 )
 PLACE = 10
-PLACES = {3030: 9, 3040: 9, 3050: 9, 1550: 9, 1551: 9, 1552: 9, 1553: 9, 1554: 9, 1250: 9, 1251: 9, 1252: 9, 1253: 9, 1254: 9}
+PLACES = {}
 ORDER = (
     2011, 0, 200, 400, 2000, 2001, 50, 1, 250, 201, 450, 401, 2050, 2051, 51, 2, 251, 202, 451,
     402, 52, 3, 252, 203, 452, 403, 53, 21, 20, 220, 253, 221, 453, 421, 71, 420, 70, 3000, 270,

time: 735 us -> 711 us (0.967)
  waiting for transfers between devices: 296 us -> 263 us
  starting transfers between devices: 75 us -> 91.1 us
    ppermute x42, waiting for transfers between devices: 296 us -> 263 us  [exchange(): return lax.ppermute(value, AXES, [(i, i ^ mask) for i in range(n)])]
    ppermute x42, starting transfers between devices: 74.9 us -> 91 us  [exchange(): return lax.ppermute(value, AXES, [(i, i ^ mask) for i in range(n)])]
    unnamed x111 -> x109, local copies, waits for them, and re-layouts: 16.1 us -> 13.3 us
  transfers between devices with their start and end apart: 44 -> 44, of which waited for: 19 -> 16; matrix products, arithmetic and copies ran while one was open for 4% -> 4% of each run, Pallas kernels for 27% -> 26%
where the time goes in v3:
time: 711 us; the launch traced here: 707 us
  Pallas kernels  288 us (41%)
  waiting for transfers between devices  263 us (37%)
  starting transfers between devices  91.1 us (13%)
  local copies, waits for them, and re-layouts  34.8 us (5%)
  between operations  15.4 us (2%)
  other arithmetic  14.9 us (2%)
    pallas_call x37, Pallas kernels, call(): pl.pallas_call(body, in_specs=in_specs, out_specs=out_specs, out_shape=ou...  288 us
    ppermute x42, waiting for transfers between devices, exchange(): return lax.ppermute(value, AXES, [(i, i ^ mask) for i in range(n)])  263 us
    ppermute x42, starting transfers between devices, exchange(): return lax.ppermute(value, AXES, [(i, i ^ mask) for i in range(n)])  91 us
  transfers between devices with their start and end apart: 44, of which 16 were waited for; matrix products, arithmetic and copies ran while one was open for 4% of the time, Pallas kernels for 26%

profile of v3, /device:TPU:0, one launch (start us, length us, event | category | flops | bytes accessed | tf_op | source)
XLA Modules:
  0.0 707.3 jit_solution(16493541456400908323)
XLA Ops:
  28.5 8.5 %collective-permute-done.1.b_ref = bf16[1,32,5120]{2,1,0:T(8,128)(2,1)S(1)} collective-permute-done((bf16[1,32,5120]{2,1,0:T(8,128)(2,1)S(1)}, bf16[1,32,5120]{2,1,0:T(8,128)(2,1)S(1)}, u32[]{:S(2)}, u32[]{:S(2)}) %collective-permute-start.1) | collective-permute-done | bytes 327712 | tf_op jit(solution)/shard_map/ppermute | solution.py:546
  42.3 9.5 %collective-permute-start.4 = (bf16[2,32,5120]{2,1,0:T(8,128)(2,1)S(1)}, bf16[2,32,5120]{2,1,0:T(8,128)(2,1)S(1)}, u32[]{:S(2)}, u32[]{:S(2)}) collective-permute-start(bf16[2,32,5120]{2,1,0:T(8,128)(2,1)S(1)} %copy-done.43), channel_id=1, source_target_pairs={{0,8},{1,9},{2,10},{3,11},{4,12},{5,13},{6,14},{7,15},{8,0},{9,1},... | collective-permute-start | bytes 1966088 | tf_op jit(solution)/shard_map/ppermute | solution.py:546
  60.7 29.3 %collective-permute-done.4.b_ref = bf16[2,32,5120]{2,1,0:T(8,128)(2,1)S(1)} collective-permute-done((bf16[2,32,5120]{2,1,0:T(8,128)(2,1)S(1)}, bf16[2,32,5120]{2,1,0:T(8,128)(2,1)S(1)}, u32[]{:S(2)}, u32[]{:S(2)}) %collective-permute-start.4) | collective-permute-done | bytes 655392 | tf_op jit(solution)/shard_map/ppermute | solution.py:546
  121.8 19.9 %collective-permute-done.11.b_ref = bf16[4,128,1024]{2,1,0:T(8,128)(2,1)S(1)} collective-permute-done((bf16[4,128,1024]{2,1,0:T(8,128)(2,1)}, bf16[4,128,1024]{2,1,0:T(8,128)(2,1)S(1)}, u32[]{:S(2)}, u32[]{:S(2)}) %collective-permute-start.11) | collective-permute-done | bytes 1048608 | tf_op jit(solution)/shard_map/ppermute | solution.py:546
  146.8 60.6 %collective-permute-done.12.refs_1_.refs_6_ = bf16[8,32,3200]{2,1,0:T(8,128)(2,1)} collective-permute-done((bf16[8,32,3200]{2,1,0:T(8,128)(2,1)}, bf16[8,32,3200]{2,1,0:T(8,128)(2,1)}, u32[]{:S(2)}, u32[]{:S(2)}) %collective-permute-start.12) | collective-permute-done | bytes 1638432 | tf_op jit(solution)/shard_map/ppermute | solution.py:546
  227.6 17.1 %attn_fwd.2 = (bf16[320,1024]{1,0:T(8,128)(2,1)}, bf16[320,3072]{1,0:T(8,128)(2,1)}, bf16[320,1024]{1,0:T(8,128)(2,1)}, f32[16,320]{1,0:T(8,128)}) custom-call(s32[1]{0:T(128)} %bitcast.me_ref, bf16[320,1024]{1,0:T(8,128)(2,1)} %bitcast.135, f32[320,1]{1,0:T(8,128)} %convert_element_type.70.flag_ref, f32[1,1024]{1,0:T(1,128)} %get-tuple-element.577.gain_ref.refs_3_, ...), custom_call_target="tpu_custom_call" | custom-call | flops 10000000000 | tf_op jit(solution)/shard_map/attn_fwd/pallas_call | solution.py:349
  244.7 14.7 %mlp_up.2 = (f32[320,1024]{1,0:T(8,128)}, bf16[320,1024]{1,0:T(8,128)(2,1)}, bf16[320,4096]{1,0:T(8,128)(2,1)}, f32[320,4096]{1,0:T(8,128)}) custom-call(s32[1]{0:T(128)} %bitcast.me_ref, bf16[320,1024]{1,0:T(8,128)(2,1)} %bitcast.136, bf16[320,1024]{1,0:T(8,128)(2,1)} %get-tuple-element.316.att_ref.refs_1_, f32[1,1024]{1,0:T(1,128)} %get-tuple-element.573.ob_ref, ...), custom_call_target="tpu_custom_call" | custom-call | flops 10000000000 | tf_op jit(solution)/shard_map/mlp_up/pallas_call | solution.py:349
  259.4 9.4 %mlp_down.2.x_ref.refs_1_ = f32[320,1024]{1,0:T(8,128)} custom-call(s32[1]{0:T(128)} %bitcast.me_ref, f32[320,1024]{1,0:T(8,128)} %get-tuple-element.320.mid_ref, bf16[320,4096]{1,0:T(8,128)(2,1)} %get-tuple-element.321.hidden_ref, f32[1,1024]{1,0:T(1,128)} %get-tuple-element.570.db_ref, f32[320,1]{1,0:T(8,128)} %convert_element_type.70.flag_ref, ...), custom_call_target="tpu_custom_call" | custom-call | flops 10000000000 | tf_op jit(solution)/shard_map/mlp_down/pallas_call | solution.py:349
  268.9 17.1 %attn_fwd.3 = (bf16[320,1024]{1,0:T(8,128)(2,1)}, bf16[320,3072]{1,0:T(8,128)(2,1)}, bf16[320,1024]{1,0:T(8,128)(2,1)}, f32[16,320]{1,0:T(8,128)}) custom-call(s32[1]{0:T(128)} %bitcast.me_ref, f32[320,1024]{1,0:T(8,128)} %mlp_down.2.x_ref.refs_1_, f32[320,1]{1,0:T(8,128)} %convert_element_type.70.flag_ref, f32[1,1024]{1,0:T(1,128)} %get-tuple-element.569.gain_ref.refs_3_, ...), custom_call_target="tpu_custom_call" | custom-call | flops 10000000000 | tf_op jit(solution)/shard_map/attn_fwd/pallas_call | solution.py:349
  286.0 14.6 %mlp_up.3 = (f32[320,1024]{1,0:T(8,128)}, bf16[320,1024]{1,0:T(8,128)(2,1)}, bf16[320,4096]{1,0:T(8,128)(2,1)}, f32[320,4096]{1,0:T(8,128)}) custom-call(s32[1]{0:T(128)} %bitcast.me_ref, f32[320,1024]{1,0:T(8,128)} %mlp_down.2.x_ref.refs_1_, bf16[320,1024]{1,0:T(8,128)(2,1)} %get-tuple-element.331.att_ref.refs_1_, f32[1,1024]{1,0:T(1,128)} %get-tuple-element.565.ob_ref, ...), custom_call_target="tpu_custom_call" | custom-call | flops 10000000000 | tf_op jit(solution)/shard_map/mlp_up/pallas_call | solution.py:349
  300.6 11.3 %down_grad.2 = (bf16[16,128,1024]{2,1,0:T(8,128)(2,1)}, bf16[16,128,1024]{2,1,0:T(8,128)(2,1)}, bf16[320,1024]{1,0:T(8,128)(2,1)}, f32[1,1024]{1,0:T(1,128)}) custom-call(s32[1]{0:T(128)} %bitcast.me_ref, f32[320,1024]{1,0:T(8,128)} %convert_multiply_fusion.grad_ref, bf16[320,4096]{1,0:T(8,128)(2,1)} %get-tuple-element.335.hidden_ref), custom_call_target="tpu_custom_call" | custom-call | flops 10000000000 | tf_op jit(solution)/shard_map/down_grad/pallas_call | solution.py:349
  312.0 24.9 %mlp_back.2 = (bf16[32,288,1024]{2,1,0:T(8,128)(2,1)}, f32[320,1024]{1,0:T(8,128)}, bf16[320,1024]{1,0:T(8,128)(2,1)}, f32[1,4096]{1,0:T(1,128)}, f32[1,1024]{1,...) custom-call(s32[1]{0:T(128)} %bitcast.me_ref, f32[320,1024]{1,0:T(8,128)} %convert_multiply_fusion.grad_ref, ...), custom_call_target="tpu_custom_call" | custom-call | flops 10000000000 | tf_op jit(solution)/shard_map/mlp_back/pallas_call | solution.py:349
  336.9 24.9 %attn_back.2 = (bf16[32,288,1024]{2,1,0:T(8,128)(2,1)}, f32[320,1024]{1,0:T(8,128)}, f32[1,1024]{1,0:T(1,128)}, f32[1,1024]{1,0:T(1,128)}, f32[1,1024]{1,0:T(1,128)}, /*index=5*/f32[1,1024]{1,0:T(1,128)}) custom-call(s32[1]{0:T(128)} %bitcast.me_ref, bf16[320,1024]{1,0:T(8,128)(2,1)} %get-tuple-element.346.d_att_ref, ...), custom_call_target="tpu_custom_call", output_to_operand_aliasing={{0}: (10, {})} | custom-call | flops 10000000000 | tf_op jit(solution)/shard_map/attn_back/pallas_call | solution.py:349
  361.9 11.4 %down_grad.3 = (bf16[16,128,1024]{2,1,0:T(8,128)(2,1)}, bf16[16,128,1024]{2,1,0:T(8,128)(2,1)}, bf16[320,1024]{1,0:T(8,128)(2,1)}, f32[1,1024]{1,0:T(1,128)}) custom-call(s32[1]{0:T(128)} %bitcast.me_ref, f32[320,1024]{1,0:T(8,128)} %get-tuple-element.352.grad_ref, bf16[320,4096]{1,0:T(8,128)(2,1)} %get-tuple-element.321.hidden_ref), custom_call_target="tpu_custom_call" | custom-call | flops 10000000000 | tf_op jit(solution)/shard_map/down_grad/pallas_call | solution.py:349
  373.3 25.2 %mlp_back.3 = (bf16[16,32,5120]{2,1,0:T(8,128)(2,1)}, bf16[16,32,5120]{2,1,0:T(8,128)(2,1)}, f32[320,1024]{1,0:T(8,128)}, bf16[320,1024]{1,0:T(8,128)(2,1)}, f32...) custom-call(s32[1]{0:T(128)} %bitcast.me_ref, ...), custom_call_target="tpu_custom_call" | custom-call | flops 10000000000 | tf_op jit(solution)/shard_map/mlp_back/pallas_call | solution.py:349
  402.9 9.2 %mlp_down.3 = bf16[320,1024]{1,0:T(8,128)(2,1)} custom-call(s32[1]{0:T(128)} %bitcast.me_ref, f32[320,1024]{1,0:T(8,128)} %get-tuple-element.342.mid_ref, bf16[320,4096]{1,0:T(8,128)(2,1)} %get-tuple-element.335.hidden_ref, f32[1,1024]{1,0:T(1,128)} %get-tuple-element.562.db_ref, f32[320,1]{1,0:T(8,128)} %convert_element_type.70.flag_ref, ...), custom_call_target="tpu_custom_call" | custom-call | flops 10000000000 | tf_op jit(solution)/shard_map/mlp_down/pallas_call | solution.py:349
  418.0 10.8 %collective-permute-start.25 = (bf16[8,128,1024]{2,1,0:T(8,128)(2,1)}, bf16[8,128,1024]{2,1,0:T(8,128)(2,1)}, u32[]{:S(2)}, u32[]{:S(2)}) collective-permute-start(bf16[8,128,1024]{2,1,0:T(8,128)(2,1)} %get-tuple-element.385), channel_id=1, source_target_pairs={{0,8},{1,9},{2,10},{3,11},{4,12},{5,13},{6,14},{7,15},{8,0},{9,1},... | collective-permute-start | bytes 6291464 | tf_op jit(solution)/shard_map/ppermute | solution.py:546
  446.0 25.9 %attn_back.3 = (bf16[16,32,3200]{2,1,0:T(8,128)(2,1)}, bf16[16,32,3200]{2,1,0:T(8,128)(2,1)}, bf16[320,1024]{1,0:T(8,128)(2,1)}, f32[1,1024]{1,0:T(1,128)}, f32[...) custom-call(s32[1]{0:T(128)} %bitcast.me_ref, bf16[320,1024]{1,0:T(8,128)(2,1)} %get-tuple-element.401.d_att_ref, ...), custom_call_target="tpu_custom_call" | custom-call | flops 10000000000 | tf_op jit(solution)/shard_map/attn_back/pallas_call | solution.py:349
  479.5 9.2 %collective-permute-done.24.got_ref = bf16[8,128,1024]{2,1,0:T(8,128)(2,1)} collective-permute-done((bf16[8,128,1024]{2,1,0:T(8,128)(2,1)}, bf16[8,128,1024]{2,1,0:T(8,128)(2,1)}, u32[]{:S(2)}, u32[]{:S(2)}) %collective-permute-start.24) | collective-permute-done | bytes 2097184 | tf_op jit(solution)/shard_map/ppermute | solution.py:546
  496.0 23.3 %collective-permute-done.23.got_ref = bf16[8,32,5120]{2,1,0:T(8,128)(2,1)} collective-permute-done((bf16[8,32,5120]{2,1,0:T(8,128)(2,1)}, bf16[8,32,5120]{2,1,0:T(8,128)(2,1)}, u32[]{:S(2)}, u32[]{:S(2)}) %collective-permute-start.23) | collective-permute-done | bytes 2621472 | tf_op jit(solution)/shard_map/ppermute | solution.py:546
  537.9 25.4 %collective-permute-done.26.got_ref = bf16[4,128,1024]{2,1,0:T(8,128)(2,1)} collective-permute-done((bf16[4,128,1024]{2,1,0:T(8,128)(2,1)}, bf16[4,128,1024]{2,1,0:T(8,128)(2,1)}, u32[]{:S(2)}, u32[]{:S(2)}) %collective-permute-start.26) | collective-permute-done | bytes 1048608 | tf_op jit(solution)/shard_map/ppermute | solution.py:546
  577.9 28.8 %collective-permute-done.33.got_ref = bf16[8,32,3200]{2,1,0:T(8,128)(2,1)S(1)} collective-permute-done((bf16[8,32,3200]{2,1,0:T(8,128)(2,1)S(1)}, bf16[8,32,3200]{2,1,0:T(8,128)(2,1)S(1)}, u32[]{:S(2)}, u32[]{:S(2)}) %collective-permute-start.33) | collective-permute-done | bytes 1638432 | tf_op jit(solution)/shard_map/ppermute | solution.py:546
  637.2 21.2 %collective-permute-start.38 = (bf16[2,32,3200]{2,1,0:T(8,128)(2,1)S(1)}, bf16[2,32,3200]{2,1,0:T(8,128)(2,1)S(1)}, u32[]{:S(2)}, u32[]{:S(2)}) collective-permute-start(bf16[2,32,3200]{2,1,0:T(8,128)(2,1)S(1)} %copy-done.46), channel_id=1, source_target_pairs={{0,8},{1,9},{2,10},{3,11},{4,12},{5,13},{6,14},{7,15},{8,0},{9,1},... | collective-permute-start | bytes 1228808 | tf_op jit(solution)/shard_map/ppermute | solution.py:546
  659.6 18.7 %collective-permute-done.38.got_ref = bf16[2,32,3200]{2,1,0:T(8,128)(2,1)S(1)} collective-permute-done((bf16[2,32,3200]{2,1,0:T(8,128)(2,1)S(1)}, bf16[2,32,3200]{2,1,0:T(8,128)(2,1)S(1)}, u32[]{:S(2)}, u32[]{:S(2)}) %collective-permute-start.38) | collective-permute-done | bytes 409632 | tf_op jit(solution)/shard_map/ppermute | solution.py:546
  (364 shorter events, 220.8 us)
Async XLA Ops:
  7.2 261.7 %all-gather.3.cloned.1.call-start = ((), (), s32[]{:S(2)}) async-start(), calls=%async_computation.2 | async-start | bytes 25952256 | tf_op jit(solution)/shard_map/all_gather | solution.py:812
  12.1 682.9 %reduce-scatter.2.cloned.1.call-start = ((), (), s32[]{:S(2)}) async-start(), calls=%async_computation.1 | async-start | bytes 19464192 | tf_op jit(solution)/shard_map/reduce_scatter | solution.py:1036
  42.3 47.6 %collective-permute-start.4 = (bf16[2,32,5120]{2,1,0:T(8,128)(2,1)S(1)}, bf16[2,32,5120]{2,1,0:T(8,128)(2,1)S(1)}, u32[]{:S(2)}, u32[]{:S(2)}) collective-permute-start(bf16[2,32,5120]{2,1,0:T(8,128)(2,1)S(1)} %copy-done.43), channel_id=1, source_target_pairs={{0,8},{1,9},{2,10},{3,11},{4,12},{5,13},{6,14},{7,15},{8,0},{9,1},... | collective-permute-start | bytes 1966088 | tf_op jit(solution)/shard_map/ppermute | solution.py:546
  51.8 46.1 %collective-permute-start.3 = (bf16[2,128,1024]{2,1,0:T(8,128)(2,1)}, bf16[2,128,1024]{2,1,0:T(8,128)(2,1)S(1)}, u32[]{:S(2)}, u32[]{:S(2)}) collective-permute-start(bf16[2,128,1024]{2,1,0:T(8,128)(2,1)} %pack.11.a_ref), channel_id=1, source_target_pairs={{0,24},{1,25},{2,26},{3,27},{4,28},{5,29},{6,30},{7,31},{8,16},{9,... | collective-permute-start | bytes 1572872 | tf_op jit(solution)/shard_map/ppermute | solution.py:546
  59.2 42.7 %collective-permute-start.9 = (bf16[4,32,3200]{2,1,0:T(8,128)(2,1)}, bf16[4,32,3200]{2,1,0:T(8,128)(2,1)S(1)}, u32[]{:S(2)}, u32[]{:S(2)}) collective-permute-start(bf16[4,32,3200]{2,1,0:T(8,128)(2,1)} %pack.12.a_ref), channel_id=1, source_target_pairs={{0,1},{1,0},{2,3},{3,2},{4,5},{5,4},{6,7},{7,6},{8,9},{9,8},{10,11... | collective-permute-start | bytes 2457608 | tf_op jit(solution)/shard_map/ppermute | solution.py:546
  101.9 39.8 %collective-permute-start.11 = (bf16[4,128,1024]{2,1,0:T(8,128)(2,1)}, bf16[4,128,1024]{2,1,0:T(8,128)(2,1)S(1)}, u32[]{:S(2)}, u32[]{:S(2)}) collective-permute-start(bf16[4,128,1024]{2,1,0:T(8,128)(2,1)} %pack.14.a_ref), channel_id=1, source_target_pairs={{0,8},{1,9},{2,10},{3,11},{4,12},{5,13},{6,14},{7,15},{8,0},{9,1},... | collective-permute-start | bytes 3145736 | tf_op jit(solution)/shard_map/ppermute | solution.py:546
  105.5 102.0 %collective-permute-start.12 = (bf16[8,32,3200]{2,1,0:T(8,128)(2,1)}, bf16[8,32,3200]{2,1,0:T(8,128)(2,1)}, u32[]{:S(2)}, u32[]{:S(2)}) collective-permute-start(bf16[8,32,3200]{2,1,0:T(8,128)(2,1)} %pack.15.refs_0_.refs_5_), channel_id=1, source_target_pairs={{0,24},{1,25},{2,26},{3,27},{4,28},{5,29},{6,30},{7,31},{8,16},{9,... | collective-permute-start | bytes 4915208 | tf_op jit(solution)/shard_map/ppermute | solution.py:546
  120.3 88.5 %collective-permute-start.10 = (bf16[8,32,5120]{2,1,0:T(8,128)(2,1)}, bf16[8,32,5120]{2,1,0:T(8,128)(2,1)}, u32[]{:S(2)}, u32[]{:S(2)}) collective-permute-start(bf16[8,32,5120]{2,1,0:T(8,128)(2,1)} %pack.16.refs_0_.refs_3_), channel_id=1, source_target_pairs={{0,1},{1,0},{2,3},{3,2},{4,5},{5,4},{6,7},{7,6},{8,9},{9,8},{10,11... | collective-permute-start | bytes 7864328 | tf_op jit(solution)/shard_map/ppermute | solution.py:546
  145.7 75.7 %collective-permute-start.17 = (bf16[8,128,1024]{2,1,0:T(8,128)(2,1)}, bf16[8,128,1024]{2,1,0:T(8,128)(2,1)}, u32[]{:S(2)}, u32[]{:S(2)}) collective-permute-start(bf16[8,128,1024]{2,1,0:T(8,128)(2,1)} %pack.17.refs_0_.refs_7_), channel_id=1, source_target_pairs={{0,4},{1,5},{2,6},{3,7},{4,0},{5,1},{6,2},{7,3},{8,12},{9,13},{10,... | collective-permute-start | bytes 6291464 | tf_op jit(solution)/shard_map/ppermute | solution.py:546
  373.3 38.8 %collective-permute-start.22 = (bf16[16,128,1024]{2,1,0:T(8,128)(2,1)}, bf16[16,128,1024]{2,1,0:T(8,128)(2,1)}, u32[]{:S(2)}, u32[]{:S(2)}) collective-permute-start(bf16[16,128,1024]{2,1,0:T(8,128)(2,1)} %get-tuple-element.368), channel_id=1, source_target_pairs={{0,2},{1,3},{2,0},{3,1},{4,6},{5,7},{6,4},{7,5},{8,10},{9,11},{10,... | collective-permute-start | bytes 12582920 | tf_op jit(solution)/shard_map/ppermute | solution.py:546
  418.0 57.0 %collective-permute-start.25 = (bf16[8,128,1024]{2,1,0:T(8,128)(2,1)}, bf16[8,128,1024]{2,1,0:T(8,128)(2,1)}, u32[]{:S(2)}, u32[]{:S(2)}) collective-permute-start(bf16[8,128,1024]{2,1,0:T(8,128)(2,1)} %get-tuple-element.385), channel_id=1, source_target_pairs={{0,8},{1,9},{2,10},{3,11},{4,12},{5,13},{6,14},{7,15},{8,0},{9,1},... | collective-permute-start | bytes 6291464 | tf_op jit(solution)/shard_map/ppermute | solution.py:546
  435.5 53.2 %collective-permute-start.24 = (bf16[8,128,1024]{2,1,0:T(8,128)(2,1)}, bf16[8,128,1024]{2,1,0:T(8,128)(2,1)}, u32[]{:S(2)}, u32[]{:S(2)}) collective-permute-start(bf16[8,128,1024]{2,1,0:T(8,128)(2,1)} %get-tuple-element.383), channel_id=1, source_target_pairs={{0,4},{1,5},{2,6},{3,7},{4,0},{5,1},{6,2},{7,3},{8,12},{9,13},{10,... | collective-permute-start | bytes 6291464 | tf_op jit(solution)/shard_map/ppermute | solution.py:546
  444.3 75.0 %collective-permute-start.23 = (bf16[8,32,5120]{2,1,0:T(8,128)(2,1)}, bf16[8,32,5120]{2,1,0:T(8,128)(2,1)}, u32[]{:S(2)}, u32[]{:S(2)}) collective-permute-start(bf16[8,32,5120]{2,1,0:T(8,128)(2,1)} %get-tuple-element.381), channel_id=1, source_target_pairs={{0,1},{1,0},{2,3},{3,2},{4,5},{5,4},{6,7},{7,6},{8,9},{9,8},{10,11... | collective-permute-start | bytes 7864328 | tf_op jit(solution)/shard_map/ppermute | solution.py:546
  471.9 56.3 %collective-permute-start.28 = (bf16[16,32,3200]{2,1,0:T(8,128)(2,1)}, bf16[16,32,3200]{2,1,0:T(8,128)(2,1)S(1)}, u32[]{:S(2)}, u32[]{:S(2)}) collective-permute-start(bf16[16,32,3200]{2,1,0:T(8,128)(2,1)} %get-tuple-element.421), channel_id=1, source_target_pairs={{0,2},{1,3},{2,0},{3,1},{4,6},{5,7},{6,4},{7,5},{8,10},{9,11},{10,... | collective-permute-start | bytes 9830408 | tf_op jit(solution)/shard_map/ppermute | solution.py:546
  473.1 55.0 %collective-permute-start.29 = (bf16[1,160,1024]{2,1,0:T(8,128)(2,1)S(1)}, bf16[1,160,1024]{2,1,0:T(8,128)(2,1)S(1)}, u32[]{:S(2)}, u32[]{:S(2)}) collective-permute-start(bf16[1,160,1024]{2,1,0:T(8,128)(2,1)S(1)} %get-tuple-element.423), channel_id=1, source_target_pairs={{0,1},{1,0},{2,3},{3,2},{4,5},{5,4},{6,7},{7,6},{8,9},{9,8},{10,11... | collective-permute-start | bytes 983048 | tf_op jit(solution)/shard_map/ppermute | solution.py:546
  492.4 42.7 %collective-permute-start.27 = (bf16[4,128,1024]{2,1,0:T(8,128)(2,1)}, bf16[4,128,1024]{2,1,0:T(8,128)(2,1)}, u32[]{:S(2)}, u32[]{:S(2)}) collective-permute-start(bf16[4,128,1024]{2,1,0:T(8,128)(2,1)} %get-tuple-element.398), channel_id=1, source_target_pairs={{0,4},{1,5},{2,6},{3,7},{4,0},{5,1},{6,2},{7,3},{8,12},{9,13},{10,... | collective-permute-start | bytes 3145736 | tf_op jit(solution)/shard_map/ppermute | solution.py:546
  494.4 68.8 %collective-permute-start.26 = (bf16[4,128,1024]{2,1,0:T(8,128)(2,1)}, bf16[4,128,1024]{2,1,0:T(8,128)(2,1)}, u32[]{:S(2)}, u32[]{:S(2)}) collective-permute-start(bf16[4,128,1024]{2,1,0:T(8,128)(2,1)} %get-tuple-element.395), channel_id=1, source_target_pairs={{0,1},{1,0},{2,3},{3,2},{4,5},{5,4},{6,7},{7,6},{8,9},{9,8},{10,11... | collective-permute-start | bytes 3145736 | tf_op jit(solution)/shard_map/ppermute | solution.py:546
  528.1 41.9 %collective-permute-start.34 = (bf16[4,32,5120]{2,1,0:T(8,128)(2,1)}, bf16[4,32,5120]{2,1,0:T(8,128)(2,1)}, u32[]{:S(2)}, u32[]{:S(2)}) collective-permute-start(bf16[4,32,5120]{2,1,0:T(8,128)(2,1)} %get-tuple-element.449), channel_id=1, source_target_pairs={{0,8},{1,9},{2,10},{3,11},{4,12},{5,13},{6,14},{7,15},{8,0},{9,1},... | collective-permute-start | bytes 3932168 | tf_op jit(solution)/shard_map/ppermute | solution.py:546
  563.2 43.4 %collective-permute-start.33 = (bf16[8,32,3200]{2,1,0:T(8,128)(2,1)S(1)}, bf16[8,32,3200]{2,1,0:T(8,128)(2,1)S(1)}, u32[]{:S(2)}, u32[]{:S(2)}) collective-permute-start(bf16[8,32,3200]{2,1,0:T(8,128)(2,1)S(1)} %copy-done.35), channel_id=1, source_target_pairs={{0,4},{1,5},{2,6},{3,7},{4,0},{5,1},{6,2},{7,3},{8,12},{9,13},{10,... | collective-permute-start | bytes 4915208 | tf_op jit(solution)/shard_map/ppermute | solution.py:546
  566.8 44.3 %collective-permute-start.32 = (bf16[2,128,1024]{2,1,0:T(8,128)(2,1)}, bf16[2,128,1024]{2,1,0:T(8,128)(2,1)}, u32[]{:S(2)}, u32[]{:S(2)}) collective-permute-start(bf16[2,128,1024]{2,1,0:T(8,128)(2,1)} %get-tuple-element.445), channel_id=1, source_target_pairs={{0,1},{1,0},{2,3},{3,2},{4,5},{5,4},{6,7},{7,6},{8,9},{9,8},{10,11... | collective-permute-start | bytes 1572872 | tf_op jit(solution)/shard_map/ppermute | solution.py:546
  568.5 44.6 %collective-permute-start.31 = (bf16[1,160,1024]{2,1,0:T(8,128)(2,1)S(1)}, bf16[1,160,1024]{2,1,0:T(8,128)(2,1)S(1)}, u32[]{:S(2)}, u32[]{:S(2)}) collective-permute-start(bf16[1,160,1024]{2,1,0:T(8,128)(2,1)S(1)} %get-tuple-element.443), channel_id=1, source_target_pairs={{0,1},{1,0},{2,3},{3,2},{4,5},{5,4},{6,7},{7,6},{8,9},{9,8},{10,11... | collective-permute-start | bytes 983048 | tf_op jit(solution)/shard_map/ppermute | solution.py:546
  568.8 45.3 %collective-permute-start.30 = (bf16[2,128,1024]{2,1,0:T(8,128)(2,1)}, bf16[2,128,1024]{2,1,0:T(8,128)(2,1)}, u32[]{:S(2)}, u32[]{:S(2)}) collective-permute-start(bf16[2,128,1024]{2,1,0:T(8,128)(2,1)} %get-tuple-element.442), channel_id=1, source_target_pairs={{0,8},{1,9},{2,10},{3,11},{4,12},{5,13},{6,14},{7,15},{8,0},{9,1},... | collective-permute-start | bytes 1572872 | tf_op jit(solution)/shard_map/ppermute | solution.py:546
  573.0 43.2 %collective-permute-start.37 = (bf16[2,32,5120]{2,1,0:T(8,128)(2,1)}, bf16[2,32,5120]{2,1,0:T(8,128)(2,1)S(1)}, u32[]{:S(2)}, u32[]{:S(2)}) collective-permute-start(bf16[2,32,5120]{2,1,0:T(8,128)(2,1)} %get-tuple-element.470), channel_id=1, source_target_pairs={{0,24},{1,25},{2,26},{3,27},{4,28},{5,29},{6,30},{7,31},{8,16},{9,... | collective-permute-start | bytes 1966088 | tf_op jit(solution)/shard_map/ppermute | solution.py:546
  637.2 41.1 %collective-permute-start.38 = (bf16[2,32,3200]{2,1,0:T(8,128)(2,1)S(1)}, bf16[2,32,3200]{2,1,0:T(8,128)(2,1)S(1)}, u32[]{:S(2)}, u32[]{:S(2)}) collective-permute-start(bf16[2,32,3200]{2,1,0:T(8,128)(2,1)S(1)} %copy-done.46), channel_id=1, source_target_pairs={{0,8},{1,9},{2,10},{3,11},{4,12},{5,13},{6,14},{7,15},{8,0},{9,1},... | collective-permute-start | bytes 1228808 | tf_op jit(solution)/shard_map/ppermute | solution.py:546
  (73 other events, 799.6 us)
Sparse Core Ops, SparseCore 0:
  12.2 237.5 all-gather.2
  399.5 278.7 reduce-scatter.1

commit v4 on v3

--- a/solution.py
+++ b/solution.py
@@ -1078,9 +1078,9 @@
 
 
 GATHER = dict(
-    up0=("abyx",),
-    down0=("xaby",),
-    qkv0=("byxa",),
+    up0=("aybx",),
+    down0=("axyb",),
+    qkv0=("baxy",),
 )
 SCATTER = dict(
     up0=("xbay",),

time: 711 us -> 728 us (1.024)
  starting transfers between devices: 91.1 us -> 108 us
    ppermute x42, starting transfers between devices: 91 us -> 108 us  [exchange(): return lax.ppermute(value, AXES, [(i, i ^ mask) for i in range(n)])]
  transfers between devices with their start and end apart: 44 -> 44, of which waited for: 16 -> 16; matrix products, arithmetic and copies ran while one was open for 4% -> 4% of each run, Pallas kernels for 26% -> 25%
where the time goes in v4:
time: 728 us; the launch traced here: 724 us
  Pallas kernels  289 us (40%)
  waiting for transfers between devices  262 us (36%)
  starting transfers between devices  108 us (15%)
  local copies, waits for them, and re-layouts  34.8 us (5%)
  between operations  15.3 us (2%)
  other arithmetic  14.9 us (2%)
    pallas_call x37, Pallas kernels, call(): pl.pallas_call(body, in_specs=in_specs, out_specs=out_specs, out_shape=ou...  289 us
    ppermute x42, waiting for transfers between devices, exchange(): return lax.ppermute(value, AXES, [(i, i ^ mask) for i in range(n)])  262 us
    ppermute x42, starting transfers between devices, exchange(): return lax.ppermute(value, AXES, [(i, i ^ mask) for i in range(n)])  108 us
  transfers between devices with their start and end apart: 44, of which 16 were waited for; matrix products, arithmetic and copies ran while one was open for 4% of the time, Pallas kernels for 25%

profile of v4, /device:TPU:0, one launch (start us, length us, event | category | flops | bytes accessed | tf_op | source)
XLA Modules:
  0.0 724.4 jit_solution(5772307304318099268)
XLA Ops:
  67.4 37.3 %collective-permute-start.8 = (bf16[4,32,5120]{2,1,0:T(8,128)(2,1)}, bf16[4,32,5120]{2,1,0:T(8,128)(2,1)S(1)}, u32[]{:S(2)}, u32[]{:S(2)}) collective-permute-start(bf16[4,32,5120]{2,1,0:T(8,128)(2,1)} %pack.13.a_ref), channel_id=1, source_target_pairs={{0,8},{1,9},{2,10},{3,11},{4,12},{5,13},{6,14},{7,15},{8,0},{9,1},... | collective-permute-start | bytes 3932168 | tf_op jit(solution)/shard_map/ppermute | solution.py:546
  112.6 29.4 %collective-permute-done.8.b_ref = bf16[4,32,5120]{2,1,0:T(8,128)(2,1)S(1)} collective-permute-done((bf16[4,32,5120]{2,1,0:T(8,128)(2,1)}, bf16[4,32,5120]{2,1,0:T(8,128)(2,1)S(1)}, u32[]{:S(2)}, u32[]{:S(2)}) %collective-permute-start.8) | collective-permute-done | bytes 1310752 | tf_op jit(solution)/shard_map/ppermute | solution.py:546
  152.4 21.0 %collective-permute-done.12.refs_1_.refs_6_ = bf16[8,32,3200]{2,1,0:T(8,128)(2,1)} collective-permute-done((bf16[8,32,3200]{2,1,0:T(8,128)(2,1)}, bf16[8,32,3200]{2,1,0:T(8,128)(2,1)}, u32[]{:S(2)}, u32[]{:S(2)}) %collective-permute-start.12) | collective-permute-done | bytes 1638432 | tf_op jit(solution)/shard_map/ppermute | solution.py:546
  174.8 68.3 %collective-permute-done.10.refs_1_.refs_4_ = bf16[8,32,5120]{2,1,0:T(8,128)(2,1)} collective-permute-done((bf16[8,32,5120]{2,1,0:T(8,128)(2,1)}, bf16[8,32,5120]{2,1,0:T(8,128)(2,1)}, u32[]{:S(2)}, u32[]{:S(2)}) %collective-permute-start.10) | collective-permute-done | bytes 2621472 | tf_op jit(solution)/shard_map/ppermute | solution.py:546
  253.3 17.3 %attn_fwd.2 = (bf16[320,1024]{1,0:T(8,128)(2,1)}, bf16[320,3072]{1,0:T(8,128)(2,1)}, bf16[320,1024]{1,0:T(8,128)(2,1)}, f32[16,320]{1,0:T(8,128)}) custom-call(s32[1]{0:T(128)} %bitcast.me_ref, bf16[320,1024]{1,0:T(8,128)(2,1)} %bitcast.135, f32[320,1]{1,0:T(8,128)} %convert_element_type.70.flag_ref, f32[1,1024]{1,0:T(1,128)} %get-tuple-element.577.gain_ref.refs_3_, ...), custom_call_target="tpu_custom_call" | custom-call | flops 10000000000 | tf_op jit(solution)/shard_map/attn_fwd/pallas_call | solution.py:349
  270.6 14.3 %mlp_up.2 = (f32[320,1024]{1,0:T(8,128)}, bf16[320,1024]{1,0:T(8,128)(2,1)}, bf16[320,4096]{1,0:T(8,128)(2,1)}, f32[320,4096]{1,0:T(8,128)}) custom-call(s32[1]{0:T(128)} %bitcast.me_ref, bf16[320,1024]{1,0:T(8,128)(2,1)} %bitcast.136, bf16[320,1024]{1,0:T(8,128)(2,1)} %get-tuple-element.316.att_ref.refs_1_, f32[1,1024]{1,0:T(1,128)} %get-tuple-element.573.ob_ref, ...), custom_call_target="tpu_custom_call" | custom-call | flops 10000000000 | tf_op jit(solution)/shard_map/mlp_up/pallas_call | solution.py:349
  285.0 9.4 %mlp_down.2.x_ref.refs_1_ = f32[320,1024]{1,0:T(8,128)} custom-call(s32[1]{0:T(128)} %bitcast.me_ref, f32[320,1024]{1,0:T(8,128)} %get-tuple-element.320.mid_ref, bf16[320,4096]{1,0:T(8,128)(2,1)} %get-tuple-element.321.hidden_ref, f32[1,1024]{1,0:T(1,128)} %get-tuple-element.570.db_ref, f32[320,1]{1,0:T(8,128)} %convert_element_type.70.flag_ref, ...), custom_call_target="tpu_custom_call" | custom-call | flops 10000000000 | tf_op jit(solution)/shard_map/mlp_down/pallas_call | solution.py:349
  294.4 17.1 %attn_fwd.3 = (bf16[320,1024]{1,0:T(8,128)(2,1)}, bf16[320,3072]{1,0:T(8,128)(2,1)}, bf16[320,1024]{1,0:T(8,128)(2,1)}, f32[16,320]{1,0:T(8,128)}) custom-call(s32[1]{0:T(128)} %bitcast.me_ref, f32[320,1024]{1,0:T(8,128)} %mlp_down.2.x_ref.refs_1_, f32[320,1]{1,0:T(8,128)} %convert_element_type.70.flag_ref, f32[1,1024]{1,0:T(1,128)} %get-tuple-element.569.gain_ref.refs_3_, ...), custom_call_target="tpu_custom_call" | custom-call | flops 10000000000 | tf_op jit(solution)/shard_map/attn_fwd/pallas_call | solution.py:349
  311.5 14.6 %mlp_up.3 = (f32[320,1024]{1,0:T(8,128)}, bf16[320,1024]{1,0:T(8,128)(2,1)}, bf16[320,4096]{1,0:T(8,128)(2,1)}, f32[320,4096]{1,0:T(8,128)}) custom-call(s32[1]{0:T(128)} %bitcast.me_ref, f32[320,1024]{1,0:T(8,128)} %mlp_down.2.x_ref.refs_1_, bf16[320,1024]{1,0:T(8,128)(2,1)} %get-tuple-element.331.att_ref.refs_1_, f32[1,1024]{1,0:T(1,128)} %get-tuple-element.565.ob_ref, ...), custom_call_target="tpu_custom_call" | custom-call | flops 10000000000 | tf_op jit(solution)/shard_map/mlp_up/pallas_call | solution.py:349
  326.2 11.3 %down_grad.2 = (bf16[16,128,1024]{2,1,0:T(8,128)(2,1)}, bf16[16,128,1024]{2,1,0:T(8,128)(2,1)}, bf16[320,1024]{1,0:T(8,128)(2,1)}, f32[1,1024]{1,0:T(1,128)}) custom-call(s32[1]{0:T(128)} %bitcast.me_ref, f32[320,1024]{1,0:T(8,128)} %convert_multiply_fusion.grad_ref, bf16[320,4096]{1,0:T(8,128)(2,1)} %get-tuple-element.335.hidden_ref), custom_call_target="tpu_custom_call" | custom-call | flops 10000000000 | tf_op jit(solution)/shard_map/down_grad/pallas_call | solution.py:349
  337.5 24.9 %mlp_back.2 = (bf16[32,288,1024]{2,1,0:T(8,128)(2,1)}, f32[320,1024]{1,0:T(8,128)}, bf16[320,1024]{1,0:T(8,128)(2,1)}, f32[1,4096]{1,0:T(1,128)}, f32[1,1024]{1,...) custom-call(s32[1]{0:T(128)} %bitcast.me_ref, f32[320,1024]{1,0:T(8,128)} %convert_multiply_fusion.grad_ref, ...), custom_call_target="tpu_custom_call" | custom-call | flops 10000000000 | tf_op jit(solution)/shard_map/mlp_back/pallas_call | solution.py:349
  362.5 24.9 %attn_back.2 = (bf16[32,288,1024]{2,1,0:T(8,128)(2,1)}, f32[320,1024]{1,0:T(8,128)}, f32[1,1024]{1,0:T(1,128)}, f32[1,1024]{1,0:T(1,128)}, f32[1,1024]{1,0:T(1,128)}, /*index=5*/f32[1,1024]{1,0:T(1,128)}) custom-call(s32[1]{0:T(128)} %bitcast.me_ref, bf16[320,1024]{1,0:T(8,128)(2,1)} %get-tuple-element.346.d_att_ref, ...), custom_call_target="tpu_custom_call", output_to_operand_aliasing={{0}: (10, {})} | custom-call | flops 10000000000 | tf_op jit(solution)/shard_map/attn_back/pallas_call | solution.py:349
  387.4 11.4 %down_grad.3 = (bf16[16,128,1024]{2,1,0:T(8,128)(2,1)}, bf16[16,128,1024]{2,1,0:T(8,128)(2,1)}, bf16[320,1024]{1,0:T(8,128)(2,1)}, f32[1,1024]{1,0:T(1,128)}) custom-call(s32[1]{0:T(128)} %bitcast.me_ref, f32[320,1024]{1,0:T(8,128)} %get-tuple-element.352.grad_ref, bf16[320,4096]{1,0:T(8,128)(2,1)} %get-tuple-element.321.hidden_ref), custom_call_target="tpu_custom_call" | custom-call | flops 10000000000 | tf_op jit(solution)/shard_map/down_grad/pallas_call | solution.py:349
  398.9 25.2 %mlp_back.3 = (bf16[16,32,5120]{2,1,0:T(8,128)(2,1)}, bf16[16,32,5120]{2,1,0:T(8,128)(2,1)}, f32[320,1024]{1,0:T(8,128)}, bf16[320,1024]{1,0:T(8,128)(2,1)}, f32...) custom-call(s32[1]{0:T(128)} %bitcast.me_ref, ...), custom_call_target="tpu_custom_call" | custom-call | flops 10000000000 | tf_op jit(solution)/shard_map/mlp_back/pallas_call | solution.py:349
  428.4 9.2 %mlp_down.3 = bf16[320,1024]{1,0:T(8,128)(2,1)} custom-call(s32[1]{0:T(128)} %bitcast.me_ref, f32[320,1024]{1,0:T(8,128)} %get-tuple-element.342.mid_ref, bf16[320,4096]{1,0:T(8,128)(2,1)} %get-tuple-element.335.hidden_ref, f32[1,1024]{1,0:T(1,128)} %get-tuple-element.562.db_ref, f32[320,1]{1,0:T(8,128)} %convert_element_type.70.flag_ref, ...), custom_call_target="tpu_custom_call" | custom-call | flops 10000000000 | tf_op jit(solution)/shard_map/mlp_down/pallas_call | solution.py:349
  455.8 7.9 %merge.18 = (bf16[8,32,5120]{2,1,0:T(8,128)(2,1)}, bf16[8,32,5120]{2,1,0:T(8,128)(2,1)}) custom-call(bf16[16,32,5120]{2,1,0:T(8,128)(2,1)} %get-tuple-element.361.keep_ref, bf16[16,32,5120]{2,1,0:T(8,128)(2,1)} %collective-permute-done.20.got_ref), custom_call_target="tpu_custom_call" | custom-call | flops 10000000000 | tf_op jit(solution)/shard_map/merge/pallas_call | solution.py:349
  464.9 25.9 %attn_back.3 = (bf16[16,32,3200]{2,1,0:T(8,128)(2,1)}, bf16[16,32,3200]{2,1,0:T(8,128)(2,1)}, bf16[320,1024]{1,0:T(8,128)(2,1)}, f32[1,1024]{1,0:T(1,128)}, f32[...) custom-call(s32[1]{0:T(128)} %bitcast.me_ref, bf16[320,1024]{1,0:T(8,128)(2,1)} %get-tuple-element.401.d_att_ref, ...), custom_call_target="tpu_custom_call" | custom-call | flops 10000000000 | tf_op jit(solution)/shard_map/attn_back/pallas_call | solution.py:349
  497.8 10.7 %collective-permute-done.24.got_ref = bf16[8,128,1024]{2,1,0:T(8,128)(2,1)} collective-permute-done((bf16[8,128,1024]{2,1,0:T(8,128)(2,1)}, bf16[8,128,1024]{2,1,0:T(8,128)(2,1)}, u32[]{:S(2)}, u32[]{:S(2)}) %collective-permute-start.24) | collective-permute-done | bytes 2097184 | tf_op jit(solution)/shard_map/ppermute | solution.py:546
  515.6 24.5 %collective-permute-done.23.got_ref = bf16[8,32,5120]{2,1,0:T(8,128)(2,1)} collective-permute-done((bf16[8,32,5120]{2,1,0:T(8,128)(2,1)}, bf16[8,32,5120]{2,1,0:T(8,128)(2,1)}, u32[]{:S(2)}, u32[]{:S(2)}) %collective-permute-start.23) | collective-permute-done | bytes 2621472 | tf_op jit(solution)/shard_map/ppermute | solution.py:546
  557.3 25.4 %collective-permute-done.26.got_ref = bf16[4,128,1024]{2,1,0:T(8,128)(2,1)} collective-permute-done((bf16[4,128,1024]{2,1,0:T(8,128)(2,1)}, bf16[4,128,1024]{2,1,0:T(8,128)(2,1)}, u32[]{:S(2)}, u32[]{:S(2)}) %collective-permute-start.26) | collective-permute-done | bytes 1048608 | tf_op jit(solution)/shard_map/ppermute | solution.py:546
  596.0 29.3 %collective-permute-done.33.got_ref = bf16[8,32,3200]{2,1,0:T(8,128)(2,1)S(1)} collective-permute-done((bf16[8,32,3200]{2,1,0:T(8,128)(2,1)S(1)}, bf16[8,32,3200]{2,1,0:T(8,128)(2,1)S(1)}, u32[]{:S(2)}, u32[]{:S(2)}) %collective-permute-start.33) | collective-permute-done | bytes 1638432 | tf_op jit(solution)/shard_map/ppermute | solution.py:546
  643.8 7.7 %collective-permute-done.36.got_ref = bf16[4,32,3200]{2,1,0:T(8,128)(2,1)S(1)} collective-permute-done((bf16[4,32,3200]{2,1,0:T(8,128)(2,1)S(1)}, bf16[4,32,3200]{2,1,0:T(8,128)(2,1)S(1)}, u32[]{:S(2)}, u32[]{:S(2)}) %collective-permute-start.36) | collective-permute-done | bytes 819232 | tf_op jit(solution)/shard_map/ppermute | solution.py:546
  655.8 20.1 %collective-permute-start.38 = (bf16[2,32,3200]{2,1,0:T(8,128)(2,1)S(1)}, bf16[2,32,3200]{2,1,0:T(8,128)(2,1)S(1)}, u32[]{:S(2)}, u32[]{:S(2)}) collective-permute-start(bf16[2,32,3200]{2,1,0:T(8,128)(2,1)S(1)} %copy-done.46), channel_id=1, source_target_pairs={{0,8},{1,9},{2,10},{3,11},{4,12},{5,13},{6,14},{7,15},{8,0},{9,1},... | collective-permute-start | bytes 1228808 | tf_op jit(solution)/shard_map/ppermute | solution.py:546
  677.0 18.4 %collective-permute-done.38.got_ref = bf16[2,32,3200]{2,1,0:T(8,128)(2,1)S(1)} collective-permute-done((bf16[2,32,3200]{2,1,0:T(8,128)(2,1)S(1)}, bf16[2,32,3200]{2,1,0:T(8,128)(2,1)S(1)}, u32[]{:S(2)}, u32[]{:S(2)}) %collective-permute-start.38) | collective-permute-done | bytes 409632 | tf_op jit(solution)/shard_map/ppermute | solution.py:546
  (364 shorter events, 203.4 us)
Async XLA Ops:
  7.2 287.2 %all-gather.3.cloned.1.call-start = ((), (), s32[]{:S(2)}) async-start(), calls=%async_computation.2 | async-start | bytes 25952256 | tf_op jit(solution)/shard_map/all_gather | solution.py:812
  12.1 700.0 %reduce-scatter.2.cloned.1.call-start = ((), (), s32[]{:S(2)}) async-start(), calls=%async_computation.1 | async-start | bytes 19464192 | tf_op jit(solution)/shard_map/reduce_scatter | solution.py:1036
  58.7 49.6 %collective-permute-start.9 = (bf16[4,32,3200]{2,1,0:T(8,128)(2,1)}, bf16[4,32,3200]{2,1,0:T(8,128)(2,1)S(1)}, u32[]{:S(2)}, u32[]{:S(2)}) collective-permute-start(bf16[4,32,3200]{2,1,0:T(8,128)(2,1)} %pack.12.a_ref), channel_id=1, source_target_pairs={{0,1},{1,0},{2,3},{3,2},{4,5},{5,4},{6,7},{7,6},{8,9},{9,8},{10,11... | collective-permute-start | bytes 2457608 | tf_op jit(solution)/shard_map/ppermute | solution.py:546
  67.4 74.6 %collective-permute-start.8 = (bf16[4,32,5120]{2,1,0:T(8,128)(2,1)}, bf16[4,32,5120]{2,1,0:T(8,128)(2,1)S(1)}, u32[]{:S(2)}, u32[]{:S(2)}) collective-permute-start(bf16[4,32,5120]{2,1,0:T(8,128)(2,1)} %pack.13.a_ref), channel_id=1, source_target_pairs={{0,8},{1,9},{2,10},{3,11},{4,12},{5,13},{6,14},{7,15},{8,0},{9,1},... | collective-permute-start | bytes 3932168 | tf_op jit(solution)/shard_map/ppermute | solution.py:546
  107.0 40.5 %collective-permute-start.11 = (bf16[4,128,1024]{2,1,0:T(8,128)(2,1)}, bf16[4,128,1024]{2,1,0:T(8,128)(2,1)S(1)}, u32[]{:S(2)}, u32[]{:S(2)}) collective-permute-start(bf16[4,128,1024]{2,1,0:T(8,128)(2,1)} %pack.14.a_ref), channel_id=1, source_target_pairs={{0,4},{1,5},{2,6},{3,7},{4,0},{5,1},{6,2},{7,3},{8,12},{9,13},{10,... | collective-permute-start | bytes 3145736 | tf_op jit(solution)/shard_map/ppermute | solution.py:546
  111.8 61.6 %collective-permute-start.12 = (bf16[8,32,3200]{2,1,0:T(8,128)(2,1)}, bf16[8,32,3200]{2,1,0:T(8,128)(2,1)}, u32[]{:S(2)}, u32[]{:S(2)}) collective-permute-start(bf16[8,32,3200]{2,1,0:T(8,128)(2,1)} %pack.15.refs_0_.refs_5_), channel_id=1, source_target_pairs={{0,4},{1,5},{2,6},{3,7},{4,0},{5,1},{6,2},{7,3},{8,12},{9,13},{10,... | collective-permute-start | bytes 4915208 | tf_op jit(solution)/shard_map/ppermute | solution.py:546
  146.5 96.5 %collective-permute-start.10 = (bf16[8,32,5120]{2,1,0:T(8,128)(2,1)}, bf16[8,32,5120]{2,1,0:T(8,128)(2,1)}, u32[]{:S(2)}, u32[]{:S(2)}) collective-permute-start(bf16[8,32,5120]{2,1,0:T(8,128)(2,1)} %pack.16.refs_0_.refs_3_), channel_id=1, source_target_pairs={{0,1},{1,0},{2,3},{3,2},{4,5},{5,4},{6,7},{7,6},{8,9},{9,8},{10,11... | collective-permute-start | bytes 7864328 | tf_op jit(solution)/shard_map/ppermute | solution.py:546
  152.2 95.0 %collective-permute-start.17 = (bf16[8,128,1024]{2,1,0:T(8,128)(2,1)}, bf16[8,128,1024]{2,1,0:T(8,128)(2,1)}, u32[]{:S(2)}, u32[]{:S(2)}) collective-permute-start(bf16[8,128,1024]{2,1,0:T(8,128)(2,1)} %pack.17.refs_0_.refs_7_), channel_id=1, source_target_pairs={{0,8},{1,9},{2,10},{3,11},{4,12},{5,13},{6,14},{7,15},{8,0},{9,1},... | collective-permute-start | bytes 6291464 | tf_op jit(solution)/shard_map/ppermute | solution.py:546
  173.5 72.8 %collective-permute-start.15 = (bf16[8,32,3200]{2,1,0:T(8,128)(2,1)}, bf16[8,32,3200]{2,1,0:T(8,128)(2,1)}, u32[]{:S(2)}, u32[]{:S(2)}) collective-permute-start(bf16[8,32,3200]{2,1,0:T(8,128)(2,1)} %pack.15.refs_0_.refs_5_), channel_id=1, source_target_pairs={{0,2},{1,3},{2,0},{3,1},{4,6},{5,7},{6,4},{7,5},{8,10},{9,11},{10,... | collective-permute-start | bytes 4915208 | tf_op jit(solution)/shard_map/ppermute | solution.py:546
  173.5 73.7 %collective-permute-start.16 = (bf16[8,32,3200]{2,1,0:T(8,128)(2,1)}, bf16[8,32,3200]{2,1,0:T(8,128)(2,1)}, u32[]{:S(2)}, u32[]{:S(2)}) collective-permute-start(bf16[8,32,3200]{2,1,0:T(8,128)(2,1)} %collective-permute-done.12.refs_1_.refs_6_), channel_id=1, source_target_pairs={{0,2},{1,3},{2,0},{3,1},{4,6},{5,7},{6,4},{7,5},{8,10},{9,11},{10,... | collective-permute-start | bytes 4915208 | tf_op jit(solution)/shard_map/ppermute | solution.py:546
  174.7 95.9 %collective-permute-start.14 = (bf16[8,32,5120]{2,1,0:T(8,128)(2,1)}, bf16[8,32,5120]{2,1,0:T(8,128)(2,1)}, u32[]{:S(2)}, u32[]{:S(2)}) collective-permute-start(bf16[8,32,5120]{2,1,0:T(8,128)(2,1)} %pack.16.refs_0_.refs_3_), channel_id=1, source_target_pairs={{0,2},{1,3},{2,0},{3,1},{4,6},{5,7},{6,4},{7,5},{8,10},{9,11},{10,... | collective-permute-start | bytes 7864328 | tf_op jit(solution)/shard_map/ppermute | solution.py:546
  443.6 49.6 %collective-permute-start.25 = (bf16[8,128,1024]{2,1,0:T(8,128)(2,1)}, bf16[8,128,1024]{2,1,0:T(8,128)(2,1)}, u32[]{:S(2)}, u32[]{:S(2)}) collective-permute-start(bf16[8,128,1024]{2,1,0:T(8,128)(2,1)} %get-tuple-element.385), channel_id=1, source_target_pairs={{0,8},{1,9},{2,10},{3,11},{4,12},{5,13},{6,14},{7,15},{8,0},{9,1},... | collective-permute-start | bytes 6291464 | tf_op jit(solution)/shard_map/ppermute | solution.py:546
  453.7 54.8 %collective-permute-start.24 = (bf16[8,128,1024]{2,1,0:T(8,128)(2,1)}, bf16[8,128,1024]{2,1,0:T(8,128)(2,1)}, u32[]{:S(2)}, u32[]{:S(2)}) collective-permute-start(bf16[8,128,1024]{2,1,0:T(8,128)(2,1)} %get-tuple-element.383), channel_id=1, source_target_pairs={{0,4},{1,5},{2,6},{3,7},{4,0},{5,1},{6,2},{7,3},{8,12},{9,13},{10,... | collective-permute-start | bytes 6291464 | tf_op jit(solution)/shard_map/ppermute | solution.py:546
  463.7 76.4 %collective-permute-start.23 = (bf16[8,32,5120]{2,1,0:T(8,128)(2,1)}, bf16[8,32,5120]{2,1,0:T(8,128)(2,1)}, u32[]{:S(2)}, u32[]{:S(2)}) collective-permute-start(bf16[8,32,5120]{2,1,0:T(8,128)(2,1)} %get-tuple-element.381), channel_id=1, source_target_pairs={{0,1},{1,0},{2,3},{3,2},{4,5},{5,4},{6,7},{7,6},{8,9},{9,8},{10,11... | collective-permute-start | bytes 7864328 | tf_op jit(solution)/shard_map/ppermute | solution.py:546
  490.8 56.9 %collective-permute-start.28 = (bf16[16,32,3200]{2,1,0:T(8,128)(2,1)}, bf16[16,32,3200]{2,1,0:T(8,128)(2,1)S(1)}, u32[]{:S(2)}, u32[]{:S(2)}) collective-permute-start(bf16[16,32,3200]{2,1,0:T(8,128)(2,1)} %get-tuple-element.421), channel_id=1, source_target_pairs={{0,2},{1,3},{2,0},{3,1},{4,6},{5,7},{6,4},{7,5},{8,10},{9,11},{10,... | collective-permute-start | bytes 9830408 | tf_op jit(solution)/shard_map/ppermute | solution.py:546
  492.0 55.6 %collective-permute-start.29 = (bf16[1,160,1024]{2,1,0:T(8,128)(2,1)S(1)}, bf16[1,160,1024]{2,1,0:T(8,128)(2,1)S(1)}, u32[]{:S(2)}, u32[]{:S(2)}) collective-permute-start(bf16[1,160,1024]{2,1,0:T(8,128)(2,1)S(1)} %get-tuple-element.423), channel_id=1, source_target_pairs={{0,1},{1,0},{2,3},{3,2},{4,5},{5,4},{6,7},{7,6},{8,9},{9,8},{10,11... | collective-permute-start | bytes 983048 | tf_op jit(solution)/shard_map/ppermute | solution.py:546
  512.3 42.3 %collective-permute-start.27 = (bf16[4,128,1024]{2,1,0:T(8,128)(2,1)}, bf16[4,128,1024]{2,1,0:T(8,128)(2,1)}, u32[]{:S(2)}, u32[]{:S(2)}) collective-permute-start(bf16[4,128,1024]{2,1,0:T(8,128)(2,1)} %get-tuple-element.398), channel_id=1, source_target_pairs={{0,4},{1,5},{2,6},{3,7},{4,0},{5,1},{6,2},{7,3},{8,12},{9,13},{10,... | collective-permute-start | bytes 3145736 | tf_op jit(solution)/shard_map/ppermute | solution.py:546
  514.8 68.0 %collective-permute-start.26 = (bf16[4,128,1024]{2,1,0:T(8,128)(2,1)}, bf16[4,128,1024]{2,1,0:T(8,128)(2,1)}, u32[]{:S(2)}, u32[]{:S(2)}) collective-permute-start(bf16[4,128,1024]{2,1,0:T(8,128)(2,1)} %get-tuple-element.395), channel_id=1, source_target_pairs={{0,1},{1,0},{2,3},{3,2},{4,5},{5,4},{6,7},{7,6},{8,9},{9,8},{10,11... | collective-permute-start | bytes 3145736 | tf_op jit(solution)/shard_map/ppermute | solution.py:546
  547.6 41.5 %collective-permute-start.34 = (bf16[4,32,5120]{2,1,0:T(8,128)(2,1)}, bf16[4,32,5120]{2,1,0:T(8,128)(2,1)}, u32[]{:S(2)}, u32[]{:S(2)}) collective-permute-start(bf16[4,32,5120]{2,1,0:T(8,128)(2,1)} %get-tuple-element.449), channel_id=1, source_target_pairs={{0,8},{1,9},{2,10},{3,11},{4,12},{5,13},{6,14},{7,15},{8,0},{9,1},... | collective-permute-start | bytes 3932168 | tf_op jit(solution)/shard_map/ppermute | solution.py:546
  582.7 42.6 %collective-permute-start.33 = (bf16[8,32,3200]{2,1,0:T(8,128)(2,1)S(1)}, bf16[8,32,3200]{2,1,0:T(8,128)(2,1)S(1)}, u32[]{:S(2)}, u32[]{:S(2)}) collective-permute-start(bf16[8,32,3200]{2,1,0:T(8,128)(2,1)S(1)} %copy-done.35), channel_id=1, source_target_pairs={{0,4},{1,5},{2,6},{3,7},{4,0},{5,1},{6,2},{7,3},{8,12},{9,13},{10,... | collective-permute-start | bytes 4915208 | tf_op jit(solution)/shard_map/ppermute | solution.py:546
  585.6 44.2 %collective-permute-start.32 = (bf16[2,128,1024]{2,1,0:T(8,128)(2,1)}, bf16[2,128,1024]{2,1,0:T(8,128)(2,1)}, u32[]{:S(2)}, u32[]{:S(2)}) collective-permute-start(bf16[2,128,1024]{2,1,0:T(8,128)(2,1)} %get-tuple-element.445), channel_id=1, source_target_pairs={{0,1},{1,0},{2,3},{3,2},{4,5},{5,4},{6,7},{7,6},{8,9},{9,8},{10,11... | collective-permute-start | bytes 1572872 | tf_op jit(solution)/shard_map/ppermute | solution.py:546
  587.9 44.0 %collective-permute-start.31 = (bf16[1,160,1024]{2,1,0:T(8,128)(2,1)S(1)}, bf16[1,160,1024]{2,1,0:T(8,128)(2,1)S(1)}, u32[]{:S(2)}, u32[]{:S(2)}) collective-permute-start(bf16[1,160,1024]{2,1,0:T(8,128)(2,1)S(1)} %get-tuple-element.443), channel_id=1, source_target_pairs={{0,1},{1,0},{2,3},{3,2},{4,5},{5,4},{6,7},{7,6},{8,9},{9,8},{10,11... | collective-permute-start | bytes 983048 | tf_op jit(solution)/shard_map/ppermute | solution.py:546
  587.9 44.9 %collective-permute-start.30 = (bf16[2,128,1024]{2,1,0:T(8,128)(2,1)}, bf16[2,128,1024]{2,1,0:T(8,128)(2,1)}, u32[]{:S(2)}, u32[]{:S(2)}) collective-permute-start(bf16[2,128,1024]{2,1,0:T(8,128)(2,1)} %get-tuple-element.442), channel_id=1, source_target_pairs={{0,8},{1,9},{2,10},{3,11},{4,12},{5,13},{6,14},{7,15},{8,0},{9,1},... | collective-permute-start | bytes 1572872 | tf_op jit(solution)/shard_map/ppermute | solution.py:546
  592.0 42.9 %collective-permute-start.37 = (bf16[2,32,5120]{2,1,0:T(8,128)(2,1)}, bf16[2,32,5120]{2,1,0:T(8,128)(2,1)S(1)}, u32[]{:S(2)}, u32[]{:S(2)}) collective-permute-start(bf16[2,32,5120]{2,1,0:T(8,128)(2,1)} %get-tuple-element.470), channel_id=1, source_target_pairs={{0,24},{1,25},{2,26},{3,27},{4,28},{5,29},{6,30},{7,31},{8,16},{9,... | collective-permute-start | bytes 1966088 | tf_op jit(solution)/shard_map/ppermute | solution.py:546
  (73 other events, 792.0 us)
Sparse Core Ops, SparseCore 0:
  12.2 256.2 all-gather.2
  425.0 271.1 reduce-scatter.1

commit v5 on v3

--- a/solution.py
+++ b/solution.py
@@ -1094,7 +1094,7 @@
     2011, 0, 200, 400, 2000, 2001, 50, 1, 250, 201, 450, 401, 2050, 2051, 51, 2, 251, 202, 451,
     402, 52, 3, 252, 203, 452, 403, 53, 21, 20, 220, 253, 221, 453, 421, 71, 420, 70, 3000, 270,
     271, 3010, 471, 470, 3020, 3001, 3011, 3031, 1500, 3041, 3051, 2021, 3030, 1400, 3040, 1200,
-    1550, 1501, 1450, 1401, 1250, 1201, 3050, 2003, 1000, 3021, 1551, 1502, 1451, 1402, 1251,
+    1550, 1501, 1450, 1401, 1250, 1201, 3050, 2003, 1000, 1551, 1502, 1451, 1402, 3021, 1251,
     1202, 2053, 1050, 1001, 1552, 1503, 2002, 1452, 1403, 1252, 1203, 1051, 1002, 1553, 1504,
     2052, 1453, 1404, 1253, 1204, 1052, 1003, 1554, 1454, 1254, 1053, 1004, 1054,
 )

time: 711 us -> 701 us (0.986)
  waiting for transfers between devices: 263 us -> 236 us
  starting transfers between devices: 91.1 us -> 108 us
    ppermute x42, waiting for transfers between devices: 263 us -> 236 us  [exchange(): return lax.ppermute(value, AXES, [(i, i ^ mask) for i in range(n)])]
    ppermute x42, starting transfers between devices: 91 us -> 108 us  [exchange(): return lax.ppermute(value, AXES, [(i, i ^ mask) for i in range(n)])]
  transfers between devices with their start and end apart: 44 -> 44, of which waited for: 16 -> 19; matrix products, arithmetic and copies ran while one was open for 4% -> 4% of each run, Pallas kernels for 26% -> 26%
where the time goes in v5:
time: 701 us; the launch traced here: 695 us
  Pallas kernels  287 us (41%)
  waiting for transfers between devices  236 us (34%)
  starting transfers between devices  108 us (15%)
  local copies, waits for them, and re-layouts  34 us (5%)
  between operations  15.3 us (2%)
  other arithmetic  14.8 us (2%)
    pallas_call x37, Pallas kernels, call(): pl.pallas_call(body, in_specs=in_specs, out_specs=out_specs, out_shape=ou...  287 us
    ppermute x42, waiting for transfers between devices, exchange(): return lax.ppermute(value, AXES, [(i, i ^ mask) for i in range(n)])  236 us
    ppermute x42, starting transfers between devices, exchange(): return lax.ppermute(value, AXES, [(i, i ^ mask) for i in range(n)])  108 us
  transfers between devices with their start and end apart: 44, of which 19 were waited for; matrix products, arithmetic and copies ran while one was open for 4% of the time, Pallas kernels for 26%

profile of v5, /device:TPU:0, one launch (start us, length us, event | category | flops | bytes accessed | tf_op | source)
XLA Modules:
  0.0 694.9 jit_solution(2997224300255724798)
XLA Ops:
  28.5 8.5 %collective-permute-done.1.b_ref = bf16[1,32,5120]{2,1,0:T(8,128)(2,1)S(1)} collective-permute-done((bf16[1,32,5120]{2,1,0:T(8,128)(2,1)S(1)}, bf16[1,32,5120]{2,1,0:T(8,128)(2,1)S(1)}, u32[]{:S(2)}, u32[]{:S(2)}) %collective-permute-start.1) | collective-permute-done | bytes 327712 | tf_op jit(solution)/shard_map/ppermute | solution.py:546
  42.3 9.5 %collective-permute-start.4 = (bf16[2,32,5120]{2,1,0:T(8,128)(2,1)S(1)}, bf16[2,32,5120]{2,1,0:T(8,128)(2,1)S(1)}, u32[]{:S(2)}, u32[]{:S(2)}) collective-permute-start(bf16[2,32,5120]{2,1,0:T(8,128)(2,1)S(1)} %copy-done.43), channel_id=1, source_target_pairs={{0,8},{1,9},{2,10},{3,11},{4,12},{5,13},{6,14},{7,15},{8,0},{9,1},... | collective-permute-start | bytes 1966088 | tf_op jit(solution)/shard_map/ppermute | solution.py:546
  60.7 29.3 %collective-permute-done.4.b_ref = bf16[2,32,5120]{2,1,0:T(8,128)(2,1)S(1)} collective-permute-done((bf16[2,32,5120]{2,1,0:T(8,128)(2,1)S(1)}, bf16[2,32,5120]{2,1,0:T(8,128)(2,1)S(1)}, u32[]{:S(2)}, u32[]{:S(2)}) %collective-permute-start.4) | collective-permute-done | bytes 655392 | tf_op jit(solution)/shard_map/ppermute | solution.py:546
  121.8 19.9 %collective-permute-done.11.b_ref = bf16[4,128,1024]{2,1,0:T(8,128)(2,1)S(1)} collective-permute-done((bf16[4,128,1024]{2,1,0:T(8,128)(2,1)}, bf16[4,128,1024]{2,1,0:T(8,128)(2,1)S(1)}, u32[]{:S(2)}, u32[]{:S(2)}) %collective-permute-start.11) | collective-permute-done | bytes 1048608 | tf_op jit(solution)/shard_map/ppermute | solution.py:546
  146.7 60.7 %collective-permute-done.12.refs_1_.refs_6_ = bf16[8,32,3200]{2,1,0:T(8,128)(2,1)} collective-permute-done((bf16[8,32,3200]{2,1,0:T(8,128)(2,1)}, bf16[8,32,3200]{2,1,0:T(8,128)(2,1)}, u32[]{:S(2)}, u32[]{:S(2)}) %collective-permute-start.12) | collective-permute-done | bytes 1638432 | tf_op jit(solution)/shard_map/ppermute | solution.py:546
  227.6 17.1 %attn_fwd.2 = (bf16[320,1024]{1,0:T(8,128)(2,1)}, bf16[320,3072]{1,0:T(8,128)(2,1)}, bf16[320,1024]{1,0:T(8,128)(2,1)}, f32[16,320]{1,0:T(8,128)}) custom-call(s32[1]{0:T(128)} %bitcast.me_ref, bf16[320,1024]{1,0:T(8,128)(2,1)} %bitcast.135, f32[320,1]{1,0:T(8,128)} %convert_element_type.70.flag_ref, f32[1,1024]{1,0:T(1,128)} %get-tuple-element.577.gain_ref.refs_3_, ...), custom_call_target="tpu_custom_call" | custom-call | flops 10000000000 | tf_op jit(solution)/shard_map/attn_fwd/pallas_call | solution.py:349
  244.7 14.7 %mlp_up.2 = (f32[320,1024]{1,0:T(8,128)}, bf16[320,1024]{1,0:T(8,128)(2,1)}, bf16[320,4096]{1,0:T(8,128)(2,1)}, f32[320,4096]{1,0:T(8,128)}) custom-call(s32[1]{0:T(128)} %bitcast.me_ref, bf16[320,1024]{1,0:T(8,128)(2,1)} %bitcast.136, bf16[320,1024]{1,0:T(8,128)(2,1)} %get-tuple-element.316.att_ref.refs_1_, f32[1,1024]{1,0:T(1,128)} %get-tuple-element.573.ob_ref, ...), custom_call_target="tpu_custom_call" | custom-call | flops 10000000000 | tf_op jit(solution)/shard_map/mlp_up/pallas_call | solution.py:349
  259.5 9.5 %mlp_down.2.x_ref.refs_1_ = f32[320,1024]{1,0:T(8,128)} custom-call(s32[1]{0:T(128)} %bitcast.me_ref, f32[320,1024]{1,0:T(8,128)} %get-tuple-element.320.mid_ref, bf16[320,4096]{1,0:T(8,128)(2,1)} %get-tuple-element.321.hidden_ref, f32[1,1024]{1,0:T(1,128)} %get-tuple-element.570.db_ref, f32[320,1]{1,0:T(8,128)} %convert_element_type.70.flag_ref, ...), custom_call_target="tpu_custom_call" | custom-call | flops 10000000000 | tf_op jit(solution)/shard_map/mlp_down/pallas_call | solution.py:349
  269.0 17.1 %attn_fwd.3 = (bf16[320,1024]{1,0:T(8,128)(2,1)}, bf16[320,3072]{1,0:T(8,128)(2,1)}, bf16[320,1024]{1,0:T(8,128)(2,1)}, f32[16,320]{1,0:T(8,128)}) custom-call(s32[1]{0:T(128)} %bitcast.me_ref, f32[320,1024]{1,0:T(8,128)} %mlp_down.2.x_ref.refs_1_, f32[320,1]{1,0:T(8,128)} %convert_element_type.70.flag_ref, f32[1,1024]{1,0:T(1,128)} %get-tuple-element.569.gain_ref.refs_3_, ...), custom_call_target="tpu_custom_call" | custom-call | flops 10000000000 | tf_op jit(solution)/shard_map/attn_fwd/pallas_call | solution.py:349
  286.1 14.6 %mlp_up.3 = (f32[320,1024]{1,0:T(8,128)}, bf16[320,1024]{1,0:T(8,128)(2,1)}, bf16[320,4096]{1,0:T(8,128)(2,1)}, f32[320,4096]{1,0:T(8,128)}) custom-call(s32[1]{0:T(128)} %bitcast.me_ref, f32[320,1024]{1,0:T(8,128)} %mlp_down.2.x_ref.refs_1_, bf16[320,1024]{1,0:T(8,128)(2,1)} %get-tuple-element.331.att_ref.refs_1_, f32[1,1024]{1,0:T(1,128)} %get-tuple-element.565.ob_ref, ...), custom_call_target="tpu_custom_call" | custom-call | flops 10000000000 | tf_op jit(solution)/shard_map/mlp_up/pallas_call | solution.py:349
  300.7 11.4 %down_grad.2 = (bf16[16,128,1024]{2,1,0:T(8,128)(2,1)}, bf16[16,128,1024]{2,1,0:T(8,128)(2,1)}, bf16[320,1024]{1,0:T(8,128)(2,1)}, f32[1,1024]{1,0:T(1,128)}) custom-call(s32[1]{0:T(128)} %bitcast.me_ref, f32[320,1024]{1,0:T(8,128)} %convert_multiply_fusion.grad_ref, bf16[320,4096]{1,0:T(8,128)(2,1)} %get-tuple-element.335.hidden_ref), custom_call_target="tpu_custom_call" | custom-call | flops 10000000000 | tf_op jit(solution)/shard_map/down_grad/pallas_call | solution.py:349
  312.1 24.8 %mlp_back.2 = (bf16[32,288,1024]{2,1,0:T(8,128)(2,1)}, f32[320,1024]{1,0:T(8,128)}, bf16[320,1024]{1,0:T(8,128)(2,1)}, f32[1,4096]{1,0:T(1,128)}, f32[1,1024]{1,...) custom-call(s32[1]{0:T(128)} %bitcast.me_ref, f32[320,1024]{1,0:T(8,128)} %convert_multiply_fusion.grad_ref, ...), custom_call_target="tpu_custom_call" | custom-call | flops 10000000000 | tf_op jit(solution)/shard_map/mlp_back/pallas_call | solution.py:349
  336.9 25.0 %attn_back.2 = (bf16[32,288,1024]{2,1,0:T(8,128)(2,1)}, f32[320,1024]{1,0:T(8,128)}, f32[1,1024]{1,0:T(1,128)}, f32[1,1024]{1,0:T(1,128)}, f32[1,1024]{1,0:T(1,128)}, /*index=5*/f32[1,1024]{1,0:T(1,128)}) custom-call(s32[1]{0:T(128)} %bitcast.me_ref, bf16[320,1024]{1,0:T(8,128)(2,1)} %get-tuple-element.346.d_att_ref, ...), custom_call_target="tpu_custom_call", output_to_operand_aliasing={{0}: (10, {})} | custom-call | flops 10000000000 | tf_op jit(solution)/shard_map/attn_back/pallas_call | solution.py:349
  361.8 11.4 %down_grad.3 = (bf16[16,128,1024]{2,1,0:T(8,128)(2,1)}, bf16[16,128,1024]{2,1,0:T(8,128)(2,1)}, bf16[320,1024]{1,0:T(8,128)(2,1)}, f32[1,1024]{1,0:T(1,128)}) custom-call(s32[1]{0:T(128)} %bitcast.me_ref, f32[320,1024]{1,0:T(8,128)} %get-tuple-element.352.grad_ref, bf16[320,4096]{1,0:T(8,128)(2,1)} %get-tuple-element.321.hidden_ref), custom_call_target="tpu_custom_call" | custom-call | flops 10000000000 | tf_op jit(solution)/shard_map/down_grad/pallas_call | solution.py:349
  373.3 25.2 %mlp_back.3 = (bf16[16,32,5120]{2,1,0:T(8,128)(2,1)}, bf16[16,32,5120]{2,1,0:T(8,128)(2,1)}, f32[320,1024]{1,0:T(8,128)}, bf16[320,1024]{1,0:T(8,128)(2,1)}, f32...) custom-call(s32[1]{0:T(128)} %bitcast.me_ref, ...), custom_call_target="tpu_custom_call" | custom-call | flops 10000000000 | tf_op jit(solution)/shard_map/mlp_back/pallas_call | solution.py:349
  408.6 10.5 %collective-permute-start.24 = (bf16[8,128,1024]{2,1,0:T(8,128)(2,1)}, bf16[8,128,1024]{2,1,0:T(8,128)(2,1)}, u32[]{:S(2)}, u32[]{:S(2)}) collective-permute-start(bf16[8,128,1024]{2,1,0:T(8,128)(2,1)} %get-tuple-element.380), channel_id=1, source_target_pairs={{0,8},{1,9},{2,10},{3,11},{4,12},{5,13},{6,14},{7,15},{8,0},{9,1},... | collective-permute-start | bytes 6291464 | tf_op jit(solution)/shard_map/ppermute | solution.py:546
  437.4 25.8 %attn_back.3 = (bf16[16,32,3200]{2,1,0:T(8,128)(2,1)}, bf16[16,32,3200]{2,1,0:T(8,128)(2,1)}, bf16[320,1024]{1,0:T(8,128)(2,1)}, f32[1,1024]{1,0:T(1,128)}, f32[...) custom-call(s32[1]{0:T(128)} %bitcast.me_ref, bf16[320,1024]{1,0:T(8,128)(2,1)} %get-tuple-element.401.d_att_ref, ...), custom_call_target="tpu_custom_call" | custom-call | flops 10000000000 | tf_op jit(solution)/shard_map/attn_back/pallas_call | solution.py:349
  481.5 9.2 %mlp_down.3 = bf16[320,1024]{1,0:T(8,128)(2,1)} custom-call(s32[1]{0:T(128)} %bitcast.me_ref, f32[320,1024]{1,0:T(8,128)} %get-tuple-element.342.mid_ref, bf16[320,4096]{1,0:T(8,128)(2,1)} %get-tuple-element.335.hidden_ref, f32[1,1024]{1,0:T(1,128)} %get-tuple-element.562.db_ref, f32[320,1]{1,0:T(8,128)} %convert_element_type.70.flag_ref, ...), custom_call_target="tpu_custom_call" | custom-call | flops 10000000000 | tf_op jit(solution)/shard_map/mlp_down/pallas_call | solution.py:349
  490.7 13.1 %collective-permute-done.26.got_ref = bf16[8,32,5120]{2,1,0:T(8,128)(2,1)} collective-permute-done((bf16[8,32,5120]{2,1,0:T(8,128)(2,1)}, bf16[8,32,5120]{2,1,0:T(8,128)(2,1)}, u32[]{:S(2)}, u32[]{:S(2)}) %collective-permute-start.26) | collective-permute-done | bytes 2621472 | tf_op jit(solution)/shard_map/ppermute | solution.py:546
  515.7 9.1 %collective-permute-start.34 = (bf16[4,32,5120]{2,1,0:T(8,128)(2,1)}, bf16[4,32,5120]{2,1,0:T(8,128)(2,1)}, u32[]{:S(2)}, u32[]{:S(2)}) collective-permute-start(bf16[4,32,5120]{2,1,0:T(8,128)(2,1)} %get-tuple-element.449), channel_id=1, source_target_pairs={{0,8},{1,9},{2,10},{3,11},{4,12},{5,13},{6,14},{7,15},{8,0},{9,1},... | collective-permute-start | bytes 3932168 | tf_op jit(solution)/shard_map/ppermute | solution.py:546
  534.6 13.0 %collective-permute-done.25.got_ref = bf16[4,128,1024]{2,1,0:T(8,128)(2,1)} collective-permute-done((bf16[4,128,1024]{2,1,0:T(8,128)(2,1)}, bf16[4,128,1024]{2,1,0:T(8,128)(2,1)}, u32[]{:S(2)}, u32[]{:S(2)}) %collective-permute-start.25) | collective-permute-done | bytes 1048608 | tf_op jit(solution)/shard_map/ppermute | solution.py:546
  568.7 29.9 %collective-permute-done.33.got_ref = bf16[8,32,3200]{2,1,0:T(8,128)(2,1)S(1)} collective-permute-done((bf16[8,32,3200]{2,1,0:T(8,128)(2,1)S(1)}, bf16[8,32,3200]{2,1,0:T(8,128)(2,1)S(1)}, u32[]{:S(2)}, u32[]{:S(2)}) %collective-permute-start.33) | collective-permute-done | bytes 1638432 | tf_op jit(solution)/shard_map/ppermute | solution.py:546
  630.2 18.7 %collective-permute-start.38 = (bf16[2,32,3200]{2,1,0:T(8,128)(2,1)S(1)}, bf16[2,32,3200]{2,1,0:T(8,128)(2,1)S(1)}, u32[]{:S(2)}, u32[]{:S(2)}) collective-permute-start(bf16[2,32,3200]{2,1,0:T(8,128)(2,1)S(1)} %copy-done.46), channel_id=1, source_target_pairs={{0,8},{1,9},{2,10},{3,11},{4,12},{5,13},{6,14},{7,15},{8,0},{9,1},... | collective-permute-start | bytes 1228808 | tf_op jit(solution)/shard_map/ppermute | solution.py:546
  650.1 14.4 %collective-permute-done.38.got_ref = bf16[2,32,3200]{2,1,0:T(8,128)(2,1)S(1)} collective-permute-done((bf16[2,32,3200]{2,1,0:T(8,128)(2,1)S(1)}, bf16[2,32,3200]{2,1,0:T(8,128)(2,1)S(1)}, u32[]{:S(2)}, u32[]{:S(2)}) %collective-permute-start.38) | collective-permute-done | bytes 409632 | tf_op jit(solution)/shard_map/ppermute | solution.py:546
  (364 shorter events, 237.3 us)
Async XLA Ops:
  7.2 261.8 %all-gather.3.cloned.1.call-start = ((), (), s32[]{:S(2)}) async-start(), calls=%async_computation.2 | async-start | bytes 25952256 | tf_op jit(solution)/shard_map/all_gather | solution.py:812
  12.1 670.5 %reduce-scatter.2.cloned.1.call-start = ((), (), s32[]{:S(2)}) async-start(), calls=%async_computation.1 | async-start | bytes 19464192 | tf_op jit(solution)/shard_map/reduce_scatter | solution.py:1036
  42.3 47.6 %collective-permute-start.4 = (bf16[2,32,5120]{2,1,0:T(8,128)(2,1)S(1)}, bf16[2,32,5120]{2,1,0:T(8,128)(2,1)S(1)}, u32[]{:S(2)}, u32[]{:S(2)}) collective-permute-start(bf16[2,32,5120]{2,1,0:T(8,128)(2,1)S(1)} %copy-done.43), channel_id=1, source_target_pairs={{0,8},{1,9},{2,10},{3,11},{4,12},{5,13},{6,14},{7,15},{8,0},{9,1},... | collective-permute-start | bytes 1966088 | tf_op jit(solution)/shard_map/ppermute | solution.py:546
  51.8 46.1 %collective-permute-start.3 = (bf16[2,128,1024]{2,1,0:T(8,128)(2,1)}, bf16[2,128,1024]{2,1,0:T(8,128)(2,1)S(1)}, u32[]{:S(2)}, u32[]{:S(2)}) collective-permute-start(bf16[2,128,1024]{2,1,0:T(8,128)(2,1)} %pack.11.a_ref), channel_id=1, source_target_pairs={{0,24},{1,25},{2,26},{3,27},{4,28},{5,29},{6,30},{7,31},{8,16},{9,... | collective-permute-start | bytes 1572872 | tf_op jit(solution)/shard_map/ppermute | solution.py:546
  59.2 42.7 %collective-permute-start.9 = (bf16[4,32,3200]{2,1,0:T(8,128)(2,1)}, bf16[4,32,3200]{2,1,0:T(8,128)(2,1)S(1)}, u32[]{:S(2)}, u32[]{:S(2)}) collective-permute-start(bf16[4,32,3200]{2,1,0:T(8,128)(2,1)} %pack.12.a_ref), channel_id=1, source_target_pairs={{0,1},{1,0},{2,3},{3,2},{4,5},{5,4},{6,7},{7,6},{8,9},{9,8},{10,11... | collective-permute-start | bytes 2457608 | tf_op jit(solution)/shard_map/ppermute | solution.py:546
  101.9 39.8 %collective-permute-start.11 = (bf16[4,128,1024]{2,1,0:T(8,128)(2,1)}, bf16[4,128,1024]{2,1,0:T(8,128)(2,1)S(1)}, u32[]{:S(2)}, u32[]{:S(2)}) collective-permute-start(bf16[4,128,1024]{2,1,0:T(8,128)(2,1)} %pack.14.a_ref), channel_id=1, source_target_pairs={{0,8},{1,9},{2,10},{3,11},{4,12},{5,13},{6,14},{7,15},{8,0},{9,1},... | collective-permute-start | bytes 3145736 | tf_op jit(solution)/shard_map/ppermute | solution.py:546
  105.5 101.9 %collective-permute-start.12 = (bf16[8,32,3200]{2,1,0:T(8,128)(2,1)}, bf16[8,32,3200]{2,1,0:T(8,128)(2,1)}, u32[]{:S(2)}, u32[]{:S(2)}) collective-permute-start(bf16[8,32,3200]{2,1,0:T(8,128)(2,1)} %pack.15.refs_0_.refs_5_), channel_id=1, source_target_pairs={{0,24},{1,25},{2,26},{3,27},{4,28},{5,29},{6,30},{7,31},{8,16},{9,... | collective-permute-start | bytes 4915208 | tf_op jit(solution)/shard_map/ppermute | solution.py:546
  120.3 88.5 %collective-permute-start.10 = (bf16[8,32,5120]{2,1,0:T(8,128)(2,1)}, bf16[8,32,5120]{2,1,0:T(8,128)(2,1)}, u32[]{:S(2)}, u32[]{:S(2)}) collective-permute-start(bf16[8,32,5120]{2,1,0:T(8,128)(2,1)} %pack.16.refs_0_.refs_3_), channel_id=1, source_target_pairs={{0,1},{1,0},{2,3},{3,2},{4,5},{5,4},{6,7},{7,6},{8,9},{9,8},{10,11... | collective-permute-start | bytes 7864328 | tf_op jit(solution)/shard_map/ppermute | solution.py:546
  145.6 75.8 %collective-permute-start.17 = (bf16[8,128,1024]{2,1,0:T(8,128)(2,1)}, bf16[8,128,1024]{2,1,0:T(8,128)(2,1)}, u32[]{:S(2)}, u32[]{:S(2)}) collective-permute-start(bf16[8,128,1024]{2,1,0:T(8,128)(2,1)} %pack.17.refs_0_.refs_7_), channel_id=1, source_target_pairs={{0,4},{1,5},{2,6},{3,7},{4,0},{5,1},{6,2},{7,3},{8,12},{9,13},{10,... | collective-permute-start | bytes 6291464 | tf_op jit(solution)/shard_map/ppermute | solution.py:546
  208.7 36.0 %collective-permute-start.14 = (bf16[8,32,5120]{2,1,0:T(8,128)(2,1)}, bf16[8,32,5120]{2,1,0:T(8,128)(2,1)}, u32[]{:S(2)}, u32[]{:S(2)}) collective-permute-start(bf16[8,32,5120]{2,1,0:T(8,128)(2,1)} %pack.16.refs_0_.refs_3_), channel_id=1, source_target_pairs={{0,2},{1,3},{2,0},{3,1},{4,6},{5,7},{6,4},{7,5},{8,10},{9,11},{10,... | collective-permute-start | bytes 7864328 | tf_op jit(solution)/shard_map/ppermute | solution.py:546
  208.8 35.9 %collective-permute-start.13 = (bf16[8,32,5120]{2,1,0:T(8,128)(2,1)}, bf16[8,32,5120]{2,1,0:T(8,128)(2,1)}, u32[]{:S(2)}, u32[]{:S(2)}) collective-permute-start(bf16[8,32,5120]{2,1,0:T(8,128)(2,1)} %collective-permute-done.10.refs_1_.refs_4_), channel_id=1, source_target_pairs={{0,2},{1,3},{2,0},{3,1},{4,6},{5,7},{6,4},{7,5},{8,10},{9,11},{10,... | collective-permute-start | bytes 7864328 | tf_op jit(solution)/shard_map/ppermute | solution.py:546
  408.6 56.7 %collective-permute-start.24 = (bf16[8,128,1024]{2,1,0:T(8,128)(2,1)}, bf16[8,128,1024]{2,1,0:T(8,128)(2,1)}, u32[]{:S(2)}, u32[]{:S(2)}) collective-permute-start(bf16[8,128,1024]{2,1,0:T(8,128)(2,1)} %get-tuple-element.380), channel_id=1, source_target_pairs={{0,8},{1,9},{2,10},{3,11},{4,12},{5,13},{6,14},{7,15},{8,0},{9,1},... | collective-permute-start | bytes 6291464 | tf_op jit(solution)/shard_map/ppermute | solution.py:546
  425.7 47.7 %collective-permute-start.23 = (bf16[8,128,1024]{2,1,0:T(8,128)(2,1)}, bf16[8,128,1024]{2,1,0:T(8,128)(2,1)}, u32[]{:S(2)}, u32[]{:S(2)}) collective-permute-start(bf16[8,128,1024]{2,1,0:T(8,128)(2,1)} %get-tuple-element.378), channel_id=1, source_target_pairs={{0,4},{1,5},{2,6},{3,7},{4,0},{5,1},{6,2},{7,3},{8,12},{9,13},{10,... | collective-permute-start | bytes 6291464 | tf_op jit(solution)/shard_map/ppermute | solution.py:546
  434.7 69.2 %collective-permute-start.26 = (bf16[8,32,5120]{2,1,0:T(8,128)(2,1)}, bf16[8,32,5120]{2,1,0:T(8,128)(2,1)}, u32[]{:S(2)}, u32[]{:S(2)}) collective-permute-start(bf16[8,32,5120]{2,1,0:T(8,128)(2,1)} %get-tuple-element.394), channel_id=1, source_target_pairs={{0,1},{1,0},{2,3},{3,2},{4,5},{5,4},{6,7},{7,6},{8,9},{9,8},{10,11... | collective-permute-start | bytes 7864328 | tf_op jit(solution)/shard_map/ppermute | solution.py:546
  464.3 51.4 %collective-permute-start.29 = (bf16[1,160,1024]{2,1,0:T(8,128)(2,1)S(1)}, bf16[1,160,1024]{2,1,0:T(8,128)(2,1)S(1)}, u32[]{:S(2)}, u32[]{:S(2)}) collective-permute-start(bf16[1,160,1024]{2,1,0:T(8,128)(2,1)S(1)} %get-tuple-element.423), channel_id=1, source_target_pairs={{0,1},{1,0},{2,3},{3,2},{4,5},{5,4},{6,7},{7,6},{8,9},{9,8},{10,11... | collective-permute-start | bytes 983048 | tf_op jit(solution)/shard_map/ppermute | solution.py:546
  464.4 60.6 %collective-permute-start.28 = (bf16[16,32,3200]{2,1,0:T(8,128)(2,1)}, bf16[16,32,3200]{2,1,0:T(8,128)(2,1)S(1)}, u32[]{:S(2)}, u32[]{:S(2)}) collective-permute-start(bf16[16,32,3200]{2,1,0:T(8,128)(2,1)} %get-tuple-element.421), channel_id=1, source_target_pairs={{0,2},{1,3},{2,0},{3,1},{4,6},{5,7},{6,4},{7,5},{8,10},{9,11},{10,... | collective-permute-start | bytes 9830408 | tf_op jit(solution)/shard_map/ppermute | solution.py:546
  477.3 54.5 %collective-permute-start.27 = (bf16[4,128,1024]{2,1,0:T(8,128)(2,1)}, bf16[4,128,1024]{2,1,0:T(8,128)(2,1)}, u32[]{:S(2)}, u32[]{:S(2)}) collective-permute-start(bf16[4,128,1024]{2,1,0:T(8,128)(2,1)} %get-tuple-element.398), channel_id=1, source_target_pairs={{0,4},{1,5},{2,6},{3,7},{4,0},{5,1},{6,2},{7,3},{8,12},{9,13},{10,... | collective-permute-start | bytes 3145736 | tf_op jit(solution)/shard_map/ppermute | solution.py:546
  478.8 68.7 %collective-permute-start.25 = (bf16[4,128,1024]{2,1,0:T(8,128)(2,1)}, bf16[4,128,1024]{2,1,0:T(8,128)(2,1)}, u32[]{:S(2)}, u32[]{:S(2)}) collective-permute-start(bf16[4,128,1024]{2,1,0:T(8,128)(2,1)} %get-tuple-element.389), channel_id=1, source_target_pairs={{0,1},{1,0},{2,3},{3,2},{4,5},{5,4},{6,7},{7,6},{8,9},{9,8},{10,11... | collective-permute-start | bytes 3145736 | tf_op jit(solution)/shard_map/ppermute | solution.py:546
  515.7 47.9 %collective-permute-start.34 = (bf16[4,32,5120]{2,1,0:T(8,128)(2,1)}, bf16[4,32,5120]{2,1,0:T(8,128)(2,1)}, u32[]{:S(2)}, u32[]{:S(2)}) collective-permute-start(bf16[4,32,5120]{2,1,0:T(8,128)(2,1)} %get-tuple-element.449), channel_id=1, source_target_pairs={{0,8},{1,9},{2,10},{3,11},{4,12},{5,13},{6,14},{7,15},{8,0},{9,1},... | collective-permute-start | bytes 3932168 | tf_op jit(solution)/shard_map/ppermute | solution.py:546
  547.5 51.0 %collective-permute-start.33 = (bf16[8,32,3200]{2,1,0:T(8,128)(2,1)S(1)}, bf16[8,32,3200]{2,1,0:T(8,128)(2,1)S(1)}, u32[]{:S(2)}, u32[]{:S(2)}) collective-permute-start(bf16[8,32,3200]{2,1,0:T(8,128)(2,1)S(1)} %copy-done.35), channel_id=1, source_target_pairs={{0,4},{1,5},{2,6},{3,7},{4,0},{5,1},{6,2},{7,3},{8,12},{9,13},{10,... | collective-permute-start | bytes 4915208 | tf_op jit(solution)/shard_map/ppermute | solution.py:546
  550.2 52.9 %collective-permute-start.32 = (bf16[2,128,1024]{2,1,0:T(8,128)(2,1)}, bf16[2,128,1024]{2,1,0:T(8,128)(2,1)}, u32[]{:S(2)}, u32[]{:S(2)}) collective-permute-start(bf16[2,128,1024]{2,1,0:T(8,128)(2,1)} %get-tuple-element.445), channel_id=1, source_target_pairs={{0,1},{1,0},{2,3},{3,2},{4,5},{5,4},{6,7},{7,6},{8,9},{9,8},{10,11... | collective-permute-start | bytes 1572872 | tf_op jit(solution)/shard_map/ppermute | solution.py:546
  552.7 52.4 %collective-permute-start.31 = (bf16[1,160,1024]{2,1,0:T(8,128)(2,1)S(1)}, bf16[1,160,1024]{2,1,0:T(8,128)(2,1)S(1)}, u32[]{:S(2)}, u32[]{:S(2)}) collective-permute-start(bf16[1,160,1024]{2,1,0:T(8,128)(2,1)S(1)} %get-tuple-element.443), channel_id=1, source_target_pairs={{0,1},{1,0},{2,3},{3,2},{4,5},{5,4},{6,7},{7,6},{8,9},{9,8},{10,11... | collective-permute-start | bytes 983048 | tf_op jit(solution)/shard_map/ppermute | solution.py:546
  552.7 53.3 %collective-permute-start.30 = (bf16[2,128,1024]{2,1,0:T(8,128)(2,1)}, bf16[2,128,1024]{2,1,0:T(8,128)(2,1)}, u32[]{:S(2)}, u32[]{:S(2)}) collective-permute-start(bf16[2,128,1024]{2,1,0:T(8,128)(2,1)} %get-tuple-element.442), channel_id=1, source_target_pairs={{0,8},{1,9},{2,10},{3,11},{4,12},{5,13},{6,14},{7,15},{8,0},{9,1},... | collective-permute-start | bytes 1572872 | tf_op jit(solution)/shard_map/ppermute | solution.py:546
  566.5 41.7 %collective-permute-start.37 = (bf16[2,32,5120]{2,1,0:T(8,128)(2,1)}, bf16[2,32,5120]{2,1,0:T(8,128)(2,1)S(1)}, u32[]{:S(2)}, u32[]{:S(2)}) collective-permute-start(bf16[2,32,5120]{2,1,0:T(8,128)(2,1)} %get-tuple-element.470), channel_id=1, source_target_pairs={{0,24},{1,25},{2,26},{3,27},{4,28},{5,29},{6,30},{7,31},{8,16},{9,... | collective-permute-start | bytes 1966088 | tf_op jit(solution)/shard_map/ppermute | solution.py:546
  (73 other events, 781.3 us)
Sparse Core Ops, SparseCore 0:
  12.2 237.5 all-gather.2
  399.4 272.5 reduce-scatter.1
